TPU v7x, 512 devices: a whole 4x8x8 slice. The times are simulated.
512 devices in a mesh: tok: 64 (over z_hi, x, y), tp: 8 (over z_lo, core).
Axes of the slice: x: 4, y: 8, z: 8 (z_hi: 2, z_lo: 4; z = z_hi * 4 + z_lo), core: 2. Of those that a mesh axis runs over, the one named last changes fastest.
Arguments:
- tokens: bfloat16 [8192, 4096], P('tok', 'tp'), may hold values from -6 to 6
- w_query: bfloat16 [4096, 4096], P('tok', 'tp'), may hold values from -0.09375 to 0.09375
- w_key: bfloat16 [4096, 4096], P('tok', 'tp'), may hold values from -0.09375 to 0.09375
- w_value: bfloat16 [4096, 4096], P('tok', 'tp'), may hold values from -0.09375 to 0.09375
- short_taps: float32 [3, 3, 4096], P(None, None, 'tp'), may hold values from -3.5 to 3.5
- filters: float32 [4096, 8192], P(('tp', 'tok')), may hold values from -90 to 90, as said below
- skip_gain: float32 [4096], P(('tp', 'tok')), may hold values from 0.1 to 1.9
Outputs:
- layer_out: bfloat16 [8192, 4096], P('tok', 'tp')
Inputs may be any that keep to these rules, and one draw needn't show every extreme that they name: `filters`: real-valued filter taps.
All inputs are finite; a program needn't handle non-finite values.
Results may differ from a plain program's by a relative error of at most 0.009.
Values may be sent and summed in bfloat16 or wider, within the bound.
No kernel may reach another device: no remote copies, remote signals or barrier semaphores. Data moves between devices by JAX's collectives and lax.ppermute only.
A program may use at most 64 MiB of HBM per device.

v0:
```python
import math

import jax
import jax.numpy as jnp
from jax import lax
from jax.sharding import PartitionSpec as P


def in_order(parts, dim):
    parts = jnp.moveaxis(parts, 0, dim)
    shape = parts.shape
    return parts.reshape(*shape[:dim], shape[dim] * shape[dim + 1], *shape[dim + 2 :])


def from_everyone(value, axis):
    copies = jnp.broadcast_to(value, (lax.axis_size(axis), *value.shape))
    return lax.all_to_all(copies, axis, split_axis=0, concat_axis=0, tiled=True)


def gathered_copies(value, axis, dim):
    return in_order(from_everyone(value, axis), dim)


def side_by_side(arrays, axis, dim, along):
    ends, at = ([], 0)
    for a in arrays[:-1]:
        at += a.shape[along]
        ends.append(at)
    both = jnp.concatenate(arrays, axis=along)
    return tuple(jnp.split(lax.all_gather(both, axis, axis=dim, tiled=True), ends, axis=along))


def passed_along(value, axis, steps):
    count = lax.axis_size(axis)
    leading, last = (max(0, -steps), min(count, count - steps))
    return lax.ppermute(value, axis, [(source, source + steps) for source in range(leading, last)])


def split_lengths(length):
    inner = 1
    divisor = 1
    while divisor * divisor <= length:
        if length % divisor == 0:
            inner = divisor
        divisor += 1
    return (2 * length // inner, inner)


def angle_table(rows_count, cols_count, period):
    product = lax.broadcasted_iota(jnp.int32, (rows_count, cols_count), 0) * lax.broadcasted_iota(
        jnp.int32, (rows_count, cols_count), 1
    )
    theta = (product % period).astype(jnp.float32) * (2.0 * math.pi / period)
    return (jnp.cos(theta), jnp.sin(theta))


def forward_transform(signal, outer, inner):
    channels = signal.shape[0]
    precise = lax.Precision.DEFAULT
    cos_outer, sin_outer = angle_table(outer, outer, outer)
    blocks = signal.reshape(channels, outer // 2, inner)
    cos_outer = cos_outer[:, : outer // 2]
    sin_outer = sin_outer[:, : outer // 2]
    first_re = jnp.einsum("kn,cnb->ckb", cos_outer, blocks, precision=precise)
    first_im = -jnp.einsum("kn,cnb->ckb", sin_outer, blocks, precision=precise)
    cos_twist, sin_twist = angle_table(outer, inner, outer * inner)
    twist_re = first_re * cos_twist + first_im * sin_twist
    twist_im = first_im * cos_twist - first_re * sin_twist
    cos_inner, sin_inner = angle_table(inner, inner, inner)
    spec_re = jnp.einsum("ckn,nm->ckm", twist_re, cos_inner, precision=precise) + jnp.einsum(
        "ckn,nm->ckm", twist_im, sin_inner, precision=precise
    )
    spec_im = jnp.einsum("ckn,nm->ckm", twist_im, cos_inner, precision=precise) - jnp.einsum(
        "ckn,nm->ckm", twist_re, sin_inner, precision=precise
    )
    return (spec_re, spec_im)


def inverse_transform(spec_re, spec_im, outer, inner):
    channels = spec_re.shape[0]
    precise = lax.Precision.DEFAULT
    cos_inner, sin_inner = angle_table(inner, inner, inner)
    back_re = jnp.einsum("ckm,mn->ckn", spec_re, cos_inner, precision=precise) - jnp.einsum(
        "ckm,mn->ckn", spec_im, sin_inner, precision=precise
    )
    back_im = jnp.einsum("ckm,mn->ckn", spec_re, sin_inner, precision=precise) + jnp.einsum(
        "ckm,mn->ckn", spec_im, cos_inner, precision=precise
    )
    cos_twist, sin_twist = angle_table(outer, inner, outer * inner)
    turned_re = back_re * cos_twist - back_im * sin_twist
    turned_im = back_re * sin_twist + back_im * cos_twist
    cos_outer, sin_outer = angle_table(outer, outer, outer)
    cos_outer = cos_outer[: outer // 2]
    sin_outer = sin_outer[: outer // 2]
    result = jnp.einsum("nk,ckb->cnb", cos_outer, turned_re, precision=precise) - jnp.einsum(
        "nk,ckb->cnb", sin_outer, turned_im, precision=precise
    )
    result = result * (1.0 / (outer * inner))
    return result.reshape(channels, outer // 2 * inner)


def short_conv(cols, earlier, taps):
    extended = jnp.concatenate([earlier, cols], axis=1)
    return (
        taps[0][:, None] * extended[:, 2:]
        + taps[1][:, None] * extended[:, 1:-1]
        + taps[2][:, None] * extended[:, :-2]
    )


def local(tokens, w_query, w_key, w_value, short_taps, filters, skip_gain):
    gathered = gathered_copies(tokens, "tp", 1)
    pieces = side_by_side((w_query, w_key, w_value), "tok", 0, 1)
    query_cols, key_cols, value_cols = tuple(
        (
            lax.dot_general(
                piece, gathered, (((0,), (1,)), ((), ())), preferred_element_type=jnp.float32
            )
            for piece in pieces
        )
    )
    query_prev, key_prev, value_prev = passed_along(
        (query_cols[:, -2:], key_cols[:, -2:], value_cols[:, -2:]), "tok", 1
    )
    query = short_conv(query_cols, query_prev, short_taps[0]).astype(jnp.bfloat16)
    keyed = short_conv(key_cols, key_prev, short_taps[1])
    valued = short_conv(value_cols, value_prev, short_taps[2])
    key_value = (keyed * valued).astype(jnp.bfloat16)
    owned = lax.all_to_all(key_value, "tok", split_axis=0, concat_axis=1, tiled=True)
    signal = owned.astype(jnp.float32)
    length = signal.shape[1]
    outer, inner = split_lengths(length)
    unit = filters / jnp.sqrt(jnp.sum(filters * filters, axis=1, keepdims=True) + 1e-06)
    sig_re, sig_im = forward_transform(signal, outer, inner)
    filt_re, filt_im = forward_transform(unit, outer, inner)
    prod_re = sig_re * filt_re - sig_im * filt_im
    prod_im = sig_re * filt_im + sig_im * filt_re
    convolved = inverse_transform(prod_re, prod_im, outer, inner)
    mixed = (convolved + skip_gain[:, None] * signal).astype(jnp.bfloat16)
    returned = lax.all_to_all(mixed, "tok", split_axis=1, concat_axis=0, tiled=True)
    result = (query.astype(jnp.float32) * returned.astype(jnp.float32)).astype(jnp.bfloat16)
    return result.T


def solution(mesh):
    in_specs = (
        P("tok", "tp"),
        P("tok", "tp"),
        P("tok", "tp"),
        P("tok", "tp"),
        P(None, None, "tp"),
        P(("tp", "tok"), None),
        P(("tp", "tok")),
    )
    out_specs = P("tok", "tp")
    return jax.shard_map(local, mesh=mesh, in_specs=in_specs, out_specs=out_specs, check_vma=False)
```

profile of v0, /device:TPU:6, one launch (start us, length us, event | category | flops | bytes accessed | tf_op | source)
XLA Modules:
  0.0 337.4 jit_solution(7901542667537147161)
XLA Ops:
  6.5 1.6 pad_maximum_fusion.3
  8.1 1.0 copy.10
  9.2 1.2 broadcast_in_dim.2
  10.4 7.3 %all-to-all-start = ((bf16[8,128,512]{1,2,0:T(8,128)(2,1)}), bf16[8,128,512]{1,2,0:T(8,128)(2,1)S(1)}, u32[]{:S(2)}, u32[]{:S(2)}) async-start(bf16[8,128,512]{1,2,0:T(8,128)(2,1)} %broadcast_in_dim.2), calls=%async_computation | async-start | bytes 2097152 | tf_op jit(solution)/shard_map/all_to_all | solution.py:17
  17.6 1.1 multiply_reduce_fusion
  18.8 1.0 broadcast_divide_fusion
  20.1 1.0 fusion.48
  21.0 1.0 fusion.47
  23.9 23.1 %all-to-all-done = bf16[8,128,512]{1,2,0:T(8,128)(2,1)S(1)} async-done(((bf16[8,128,512]{1,2,0:T(8,128)(2,1)}), bf16[8,128,512]{1,2,0:T(8,128)(2,1)S(1)}, u32[]{:S(2)}, u32[]{:S(2)}) %all-to-all-start) | async-done | bytes 1048608 | tf_op jit(solution)/shard_map/all_to_all | solution.py:17
  47.0 217.1 %all-gather.2.cloned.1.call-done = bf16[4096,1536]{1,0:T(8,128)(2,1)} async-done(((bf16[64,1536]{1,0:T(8,128)(2,1)}), bf16[4096,1536]{1,0:T(8,128)(2,1)}) %all-gather.2.cloned.1.call-update) | async-done | bytes 12582928 | tf_op jit(solution)/shard_map/all_gather | solution.py:30
  264.1 3.0 fusion
  267.1 2.1 collective-permute-start.2
  269.1 3.0 fusion.2
  272.1 3.9 %collective-permute-start.1 = (f32[512,2]{0,1:T(2,128)S(1)}, f32[512,2]{0,1:T(2,128)S(1)}, u32[]{:S(2)}, u32[]{:S(2)}) collective-permute-start(f32[512,2]{0,1:T(2,128)S(1)} %slice.118), channel_id=1, source_target_pairs={{0,8},{8,16},{16,24},{24,32},{32,40},{40,48},{48,56},{56,64},{64,7... | collective-permute-start | bytes 12296 | tf_op jit(solution)/shard_map/ppermute | solution.py:36
  276.1 3.6 %collective-permute-done.1 = f32[512,2]{0,1:T(2,128)S(1)} collective-permute-done((f32[512,2]{0,1:T(2,128)S(1)}, f32[512,2]{0,1:T(2,128)S(1)}, u32[]{:S(2)}, u32[]{:S(2)}) %collective-permute-start.1) | collective-permute-done | bytes 4128 | tf_op jit(solution)/shard_map/ppermute | solution.py:36
  279.8 0.8 fusion.22
  280.6 1.6 copy.11
  282.2 8.4 %all-to-all-start.1 = ((bf16[64,8,128]{2,1,0:T(8,128)(2,1)}), bf16[64,8,128]{2,1,0:T(8,128)(2,1)S(1)}, u32[]{:S(2)}, u32[]{:S(2)}) async-start(bf16[64,8,128]{2,1,0:T(8,128)(2,1)} %bitcast.88), calls=%async_computation.1 | async-start | bytes 262144 | tf_op jit(solution)/shard_map/all_to_all | solution.py:129
  291.1 13.5 %all-to-all-done.1 = bf16[64,8,128]{2,1,0:T(8,128)(2,1)S(1)} async-done(((bf16[64,8,128]{2,1,0:T(8,128)(2,1)}), bf16[64,8,128]{2,1,0:T(8,128)(2,1)S(1)}, u32[]{:S(2)}, u32[]{:S(2)}) %all-to-all-start.1) | async-done | bytes 131104 | tf_op jit(solution)/shard_map/all_to_all | solution.py:129
  309.1 0.8 fusion.38
  309.9 5.8 %all-to-all-start.2 = ((bf16[8,64,128]{2,0,1:T(8,128)(2,1)}), bf16[8,64,128]{2,0,1:T(8,128)(2,1)S(1)}, u32[]{:S(2)}, u32[]{:S(2)}) async-start(bf16[8,64,128]{2,0,1:T(8,128)(2,1)} %fusion.38), calls=%async_computation.2 | async-start | bytes 262144 | tf_op jit(solution)/shard_map/all_to_all | solution.py:140
  315.7 3.3 fusion.4
  319.0 3.4 %collective-permute-start = (f32[512,2]{0,1:T(2,128)S(1)}, f32[512,2]{0,1:T(2,128)S(1)}, u32[]{:S(2)}, u32[]{:S(2)}) collective-permute-start(f32[512,2]{0,1:T(2,128)S(1)} %slice.115), channel_id=1, source_target_pairs={{0,8},{8,16},{16,24},{24,32},{32,40},{40,48},{48,56},{56,64},{64,7... | collective-permute-start | bytes 12296 | tf_op jit(solution)/shard_map/ppermute | solution.py:36
  322.4 7.3 %all-to-all-done.2 = bf16[8,64,128]{2,0,1:T(8,128)(2,1)S(1)} async-done(((bf16[8,64,128]{2,0,1:T(8,128)(2,1)}), bf16[8,64,128]{2,0,1:T(8,128)(2,1)S(1)}, u32[]{:S(2)}, u32[]{:S(2)}) %all-to-all-start.2) | async-done | bytes 131104 | tf_op jit(solution)/shard_map/all_to_all | solution.py:140
  (42 shorter events, 7.8 us)
Async XLA Ops:
  6.5 257.5 %all-gather.2.cloned.1.call-start = ((), (), s32[]{:S(2)}) async-start(), calls=%async_computation.3 | async-start | bytes 12779520 | tf_op jit(solution)/shard_map/all_gather | solution.py:30
  10.4 36.6 %all-to-all-start = ((bf16[8,128,512]{1,2,0:T(8,128)(2,1)}), bf16[8,128,512]{1,2,0:T(8,128)(2,1)S(1)}, u32[]{:S(2)}, u32[]{:S(2)}) async-start(bf16[8,128,512]{1,2,0:T(8,128)(2,1)} %broadcast_in_dim.2), calls=%async_computation | async-start | bytes 2097152 | tf_op jit(solution)/shard_map/all_to_all | solution.py:17
  47.0 235.2 %copy-start = (bf16[8,128,512]{1,2,0:T(8,128)(2,1)}, bf16[8,128,512]{1,2,0:T(8,128)(2,1)S(1)}, u32[]{:S(2)}) copy-start(bf16[8,128,512]{1,2,0:T(8,128)(2,1)S(1)} %all-to-all-done) | copy-start | bytes 3145732
  264.1 12.0 %copy-start.1 = (f32[3,3,512]{2,1,0:T(4,128)S(1)}, f32[3,3,512]{2,1,0:T(4,128)}, u32[]{:S(2)}) copy-start(f32[3,3,512]{2,1,0:T(4,128)} %param.11) | copy-start | bytes 55300
  267.1 9.0 %collective-permute-start.2 = (f32[512,2]{0,1:T(2,128)S(1)}, f32[512,2]{0,1:T(2,128)S(1)}, u32[]{:S(2)}, u32[]{:S(2)}) collective-permute-start(f32[512,2]{0,1:T(2,128)S(1)} %slice.121), channel_id=1, source_target_pairs={{0,8},{8,16},{16,24},{24,32},{32,40},{40,48},{48,56},{56,64},{64,7... | collective-permute-start | bytes 12296 | tf_op jit(solution)/shard_map/ppermute | solution.py:36
  272.1 36.9 %copy-start.2 = (f32[8]{0:T(128)S(1)}, f32[8]{0:T(128)}, u32[]{:S(2)}) copy-start(f32[8]{0:T(128)} %param.13) | copy-start | bytes 100
  272.1 7.6 %collective-permute-start.1 = (f32[512,2]{0,1:T(2,128)S(1)}, f32[512,2]{0,1:T(2,128)S(1)}, u32[]{:S(2)}, u32[]{:S(2)}) collective-permute-start(f32[512,2]{0,1:T(2,128)S(1)} %slice.118), channel_id=1, source_target_pairs={{0,8},{8,16},{16,24},{24,32},{32,40},{40,48},{48,56},{56,64},{64,7... | collective-permute-start | bytes 12296 | tf_op jit(solution)/shard_map/ppermute | solution.py:36
  282.2 22.4 %all-to-all-start.1 = ((bf16[64,8,128]{2,1,0:T(8,128)(2,1)}), bf16[64,8,128]{2,1,0:T(8,128)(2,1)S(1)}, u32[]{:S(2)}, u32[]{:S(2)}) async-start(bf16[64,8,128]{2,1,0:T(8,128)(2,1)} %bitcast.88), calls=%async_computation.1 | async-start | bytes 262144 | tf_op jit(solution)/shard_map/all_to_all | solution.py:129
  309.9 19.8 %all-to-all-start.2 = ((bf16[8,64,128]{2,0,1:T(8,128)(2,1)}), bf16[8,64,128]{2,0,1:T(8,128)(2,1)S(1)}, u32[]{:S(2)}, u32[]{:S(2)}) async-start(bf16[8,64,128]{2,0,1:T(8,128)(2,1)} %fusion.38), calls=%async_computation.2 | async-start | bytes 262144 | tf_op jit(solution)/shard_map/all_to_all | solution.py:140
  319.0 10.8 %collective-permute-start = (f32[512,2]{0,1:T(2,128)S(1)}, f32[512,2]{0,1:T(2,128)S(1)}, u32[]{:S(2)}, u32[]{:S(2)}) collective-permute-start(f32[512,2]{0,1:T(2,128)S(1)} %slice.115), channel_id=1, source_target_pairs={{0,8},{8,16},{16,24},{24,32},{32,40},{40,48},{48,56},{56,64},{64,7... | collective-permute-start | bytes 12296 | tf_op jit(solution)/shard_map/ppermute | solution.py:36
Sparse Core Ops, SparseCore 0:
  11.8 252.2 all-gather.1
where the time goes:
time: 338 us; the launch traced here: 337 us
  waiting for transfers between devices  265 us (78%)
  starting transfers between devices  30.8 us (9%)
  matrix products  15.1 us (4%)
  between operations  13.7 us (4%)
  other arithmetic  8.44 us (2%)
  local copies, waits for them, and re-layouts  4.75 us (1%)
    all_gather x1, waiting for transfers between devices, side_by_side(): lax.all_gather(both, axis, axis=dim, tiled=True)  217 us
    all_to_all x1, waiting for transfers between devices, from_everyone(): return lax.all_to_all(copies, axis, split_axis=0, concat_axis=0, tiled=True)  23.1 us
    all_to_all x1, waiting for transfers between devices, local(): lax.all_to_all(key_value, 'tok', split_axis=0, concat_axis=1, tiled=True)  13.5 us
    ppermute x3, starting transfers between devices, passed_along(): lax.ppermute(value, axis, [(source, source + steps) for source in range(l...  9.35 us
    dot_general x3, matrix products, local(): lax.dot_general(piece, gathered, (((0,), (1,)), ((), ())), preferred_elem...  9.27 us
    all_to_all x1, starting transfers between devices, local(): lax.all_to_all(key_value, 'tok', split_axis=0, concat_axis=1, tiled=True)  8.44 us
    all_to_all x1, waiting for transfers between devices, local(): lax.all_to_all(mixed, 'tok', split_axis=1, concat_axis=0, tiled=True)  7.29 us
    all_to_all x1, starting transfers between devices, from_everyone(): return lax.all_to_all(copies, axis, split_axis=0, concat_axis=0, tiled=True)  7.27 us
  transfers between devices with their start and end apart: 7, of which 5 were waited for; matrix products, arithmetic and copies ran while one was open for 5% of the time, Pallas kernels for 0%

commit v1 on v0

v1 whole, which is shorter than its diff:
```python
import functools
import math

import jax
import jax.numpy as jnp
import numpy as np
from jax import lax
from jax.experimental import pallas as pl
from jax.experimental.pallas import tpu as pltpu
from jax.sharding import Mesh
from jax.sharding import PartitionSpec as P

AXES = ("z_hi", "x", "yh", "yl", "z_lo", "core")
SIZES = (2, 4, 4, 2, 4, 2)
TOK = AXES[:4]
TP = AXES[4:]
HALO = 8
BLOCK = 128
ROWS = HALO + BLOCK
POINTS = 128
F32 = jnp.float32
BF16 = jnp.bfloat16


def exchanged(value, axes):
    return lax.all_to_all(value, axes, split_axis=0, concat_axis=0, tiled=True)


def from_everyone(value, axes):
    count = math.prod(SIZES[AXES.index(a)] for a in axes)
    return exchanged(jnp.broadcast_to(value, (count, *value.shape)), axes)


def dft_tables():
    n = np.arange(POINTS)
    full = 2.0 * np.pi * (np.outer(n, n) % POINTS) / POINTS
    cos, sin = np.cos(full), np.sin(full)
    half = POINTS // 2
    outer = np.concatenate([cos[:, :half], -sin[:, :half]], axis=0)
    inner = np.block([[cos, -sin], [sin, cos]])
    back_inner = np.block([[cos, sin], [-sin, cos]])
    back_outer = np.concatenate([cos[:half], -sin[:half]], axis=1) / POINTS**2
    twist = 2.0 * np.pi * np.outer(n, n) / POINTS**2
    as_bf16 = lambda a: jnp.asarray(a, F32).astype(BF16)
    return (
        as_bf16(outer),
        as_bf16(inner),
        as_bf16(back_inner),
        as_bf16(back_outer),
        jnp.asarray(np.cos(twist), F32),
        jnp.asarray(np.sin(twist), F32),
    )


def dot(a, b):
    return jnp.dot(a, b, preferred_element_type=F32)


def spectrum(rows, outer, inner, cos, sin):
    blocks = jnp.concatenate(
        [rows[pl.ds(c, 64, stride=8), :].astype(BF16) for c in range(8)], axis=1
    )
    first = dot(outer, blocks)
    turned = []
    for c in range(8):
        re = first[:POINTS, c * POINTS : (c + 1) * POINTS]
        im = first[POINTS:, c * POINTS : (c + 1) * POINTS]
        turned.append(
            jnp.concatenate([re * cos + im * sin, im * cos - re * sin], axis=1).astype(BF16)
        )
    return dot(jnp.concatenate(turned, axis=0), inner)


def filter_kernel(filters, outer, inner, cos, sin, spec, rows):
    taps = filters[...]
    unit = taps / jnp.sqrt(jnp.sum(taps * taps, axis=1, keepdims=True) + 1e-06)
    for b in range(64):
        rows[pl.ds(b * 8, 8), :] = unit[:, b * POINTS : (b + 1) * POINTS]
    spec[...] = spectrum(rows, outer[...], inner[...], cos[...], sin[...])


def conv_kernel(signal, spec, skip, outer, inner, back_inner, back_outer, cos, sin, mixed, rows, out):
    for z in range(2):
        rows[pl.ds(z * 256, 256), :] = signal[:, z].astype(F32).reshape(256, POINTS)
    cos_t, sin_t = cos[...], sin[...]
    sig = spectrum(rows, outer[...], inner[...], cos_t, sin_t)
    re, im = sig[:, :POINTS], sig[:, POINTS:]
    f_re, f_im = spec[:, :POINTS], spec[:, POINTS:]
    prod = jnp.concatenate([re * f_re - im * f_im, re * f_im + im * f_re], axis=1)
    back = dot(prod.astype(BF16), back_inner[...])
    turned = []
    for c in range(8):
        b_re = back[c * POINTS : (c + 1) * POINTS, :POINTS]
        b_im = back[c * POINTS : (c + 1) * POINTS, POINTS:]
        turned.append(
            jnp.concatenate([b_re * cos_t - b_im * sin_t, b_re * sin_t + b_im * cos_t], axis=0).astype(BF16)
        )
    result = dot(back_outer[...], jnp.concatenate(turned, axis=1))
    for c in range(8):
        piece = result[:, c * POINTS : (c + 1) * POINTS]
        out[pl.ds(c, 64, stride=8), :] = piece + skip[c] * rows[pl.ds(c, 64, stride=8), :]
    mixed[...] = out[...].astype(BF16).reshape(64, 8, POINTS)


def order_table(rows_are_natural):
    shape = (512, 512)
    row = lax.broadcasted_iota(jnp.int32, shape, 0)
    col = lax.broadcasted_iota(jnp.int32, shape, 1)
    grouped, natural = (col, row) if rows_are_natural else (row, col)
    z_hi, yl, xy, j = grouped // 256, (grouped // 128) % 2, (grouped // 8) % 16, grouped % 8
    return (natural == z_hi * 256 + xy * 16 + yl * 8 + j).astype(F32).astype(BF16)


def weights_kernel(w_key, w_value, w_query, out):
    table = order_table(True)
    for p, ref in enumerate((w_key, w_value, w_query)):
        sorted_cols = dot(ref[...], table).astype(BF16)
        for quarter in range(4):
            piece = sorted_cols[:, quarter * 128 : (quarter + 1) * 128]
            for yh in range(4):
                out[quarter // 2, yh, quarter % 2, :, p * 128 : (p + 1) * 128] = piece


def projected(x, w, at, width, acc):
    for tp in range(8):
        z_lo, core = tp // 2, tp % 2
        z_hi, col = tp // 4, tp % 4
        rows = x[core, z_lo].reshape(4 * ROWS, 512)
        weights = w[col, z_hi, :, :, at : at + width].reshape(512, width)
        term = dot(rows, weights)
        if tp == 0:
            acc[...] = term
        else:
            acc[...] += term


def short(acc, group, at, taps):
    top = group * ROWS + HALO
    cols = pl.ds(at, 128)
    return (
        taps[0:1] * acc[pl.ds(top, BLOCK), cols]
        + taps[1:2] * acc[pl.ds(top - 1, BLOCK), cols]
        + taps[2:3] * acc[pl.ds(top - 2, BLOCK), cols]
    )


def key_value_kernel(x, w, taps, out, acc):
    projected(x, w, 0, 256, acc)
    for group in range(4):
        keyed = short(acc, group, 0, taps[1])
        valued = short(acc, group, 128, taps[2])
        out[:, group] = (keyed * valued).T.reshape(16, 8, BLOCK).astype(BF16)


def query_kernel(x, w, taps, out, acc):
    projected(x, w, 256, 128, acc)
    for group in range(4):
        out[group] = short(acc, group, 0, taps[0]).astype(BF16)


def gate_kernel(query, returned, out):
    cols = jnp.concatenate([query[g] for g in range(4)], axis=1)
    natural = dot(cols, order_table(False))
    mixed = returned[...].astype(F32).reshape(512, BLOCK).T
    out[...] = (natural * mixed).astype(BF16)


def call(kernel, shape, dtype, args, scratch=(), in_specs=None, flops=10**8, name=None):
    whole = pl.BlockSpec(memory_space=pltpu.VMEM)
    specs = in_specs or [whole] * len(args)
    moved = sum(math.prod(a.shape) * a.dtype.itemsize for a in args)
    return pl.pallas_call(
        kernel,
        out_shape=jax.ShapeDtypeStruct(shape, dtype),
        in_specs=specs,
        out_specs=whole,
        scratch_shapes=list(scratch),
        compiler_params=pltpu.CompilerParams(vmem_limit_bytes=48 * 2**20),
        cost_estimate=pl.CostEstimate(flops=flops, bytes_accessed=moved, transcendentals=0),
        name=name,
    )(*args)


def local(tokens, w_query, w_key, w_value, short_taps, filters, skip_gain):
    count = math.prod(SIZES[:4])
    halo = lax.ppermute(tokens[-HALO:], TOK, [(i, i + 1) for i in range(count - 1)])

    sent = call(weights_kernel, (2, 4, 2, 64, 384), BF16, (w_key, w_value, w_query), name="sort_weights")
    first = exchanged(sent.reshape(16, 64, 384), ("z_hi", "yh", "yl"))
    weights = from_everyone(first, ("x",)).reshape(4, 2, 8, 64, 384)

    extended = jnp.concatenate([halo, tokens], axis=0)
    part = from_everyone(extended, ("z_lo", "z_hi", "yl"))
    features = from_everyone(part.reshape(4, 4, ROWS, 512), ("core",)).reshape(2, 4, 4, ROWS, 512)

    z_hi, yl = lax.axis_index("z_hi"), lax.axis_index("yl")
    taps = short_taps.reshape(3, 3, 2, 16, 2, 8)
    taps = lax.dynamic_index_in_dim(taps, z_hi, 2, keepdims=False)
    taps = lax.dynamic_index_in_dim(taps, yl, 3, keepdims=False).reshape(3, 3, 128)

    outer, inner, back_inner, back_outer, cos, sin = dft_tables()
    spec = call(
        filter_kernel,
        (8 * POINTS, 2 * POINTS),
        F32,
        (filters, outer, inner, cos, sin),
        (pltpu.VMEM((512, POINTS), F32),),
        name="filter_spectrum",
    )

    whole = pl.BlockSpec(memory_space=pltpu.VMEM)
    key_value = call(
        key_value_kernel,
        (16, 4, 8, BLOCK),
        BF16,
        (features, weights, taps),
        (pltpu.VMEM((4 * ROWS, 256), F32),),
        flops=2 * 544 * 4096 * 256,
        name="key_value",
    )
    owned = exchanged(key_value, ("x", "yh"))
    query = call(
        query_kernel,
        (4, BLOCK, 128),
        BF16,
        (features, weights, taps),
        (pltpu.VMEM((4 * ROWS, 128), F32),),
        flops=2 * 544 * 4096 * 128,
        name="query",
    )
    query = exchanged(query, ("z_hi", "yl"))
    smem = pl.BlockSpec(memory_space=pltpu.SMEM)
    mixed = call(
        conv_kernel,
        (64, 8, BLOCK),
        BF16,
        (owned.reshape(16, 2, 2, 8, BLOCK), spec, skip_gain, outer, inner, back_inner, back_outer, cos, sin),
        (pltpu.VMEM((512, POINTS), F32), pltpu.VMEM((512, POINTS), F32)),
        in_specs=[whole, whole, smem] + [whole] * 6,
        flops=2 * 168 * 10**6,
        name="long_conv",
    )
    returned = exchanged(mixed, TOK)
    return call(gate_kernel, (BLOCK, 512), BF16, (query, returned), name="gate")


def solution(mesh):
    fine = Mesh(mesh.devices.reshape(SIZES), AXES)
    in_specs = (
        P(TOK, TP),
        P(TOK, TP),
        P(TOK, TP),
        P(TOK, TP),
        P(None, None, TP),
        P(TP + TOK, None),
        P(TP + TOK),
    )
    return jax.shard_map(local, mesh=fine, in_specs=in_specs, out_specs=P(TOK, TP), check_vma=False)
```

time: 338 us -> 212 us (0.63)
  waiting for transfers between devices: 265 us -> 87.8 us
  blocking collectives: 0 us -> 71.3 us
  matrix products: 15.1 us -> 0 us
  between operations: 13.7 us -> 0.17 us
  Pallas kernels: 0 us -> 12.3 us
  other arithmetic: 8.44 us -> 0.01 us
  local copies, waits for them, and re-layouts: 4.75 us -> 12.5 us
  starting transfers between devices: 30.8 us -> 25.6 us
    all_gather x1 -> x0, waiting for transfers between devices: 217 us -> none  [side_by_side(): lax.all_gather(both, axis, axis=dim, tiled=True)]
    all_to_all x0 -> x3, blocking collectives: none -> 71.3 us  [exchanged(): return lax.all_to_all(value, axes, split_axis=0, concat_axis=0, tiled=True)]
    all_to_all x3 -> x4, waiting for transfers between devices: 43.9 us -> 84.1 us  [exchanged(): return lax.all_to_all(value, axes, split_axis=0, concat_axis=0, tiled=True)]
    dot_general x21 -> x0, matrix products: 15.1 us -> none  [the longest x3 9.27 us: local(): lax.dot_general(piece, gathered, (((0,), (1,)), ((), ())), preferred_elem...]
    pallas_call x0 -> x6, Pallas kernels: none -> 12.3 us  [call(): pl.pallas_call(kernel, out_shape=jax.ShapeDtypeStruct(shape, dtype), in_s...]
    ppermute x3 -> x1, starting transfers between devices: 9.35 us -> 4.07 us  [local(): lax.ppermute(tokens[-HALO:], TOK, [(i, i + 1) for i in range(count - 1)])]
    unnamed x7 -> x26, local copies, waits for them, and re-layouts: 1.04 us -> 5.99 us
    broadcast_in_dim x1 -> x3, local copies, waits for them, and re-layouts: 1.19 us -> 5.72 us  [from_everyone(): return exchanged(jnp.broadcast_to(value, (count, *value.shape)), axes)]
  transfers between devices with their start and end apart: 7 -> 5, of which waited for: 5 -> 5; matrix products, arithmetic and copies ran while one was open for 5% -> 0% of each run, Pallas kernels for 0% -> 3%
where the time goes in v1:
time: 212 us; the launch traced here: 210 us
  waiting for transfers between devices  87.8 us (41%)
  blocking collectives  71.3 us (34%)
  starting transfers between devices  25.6 us (12%)
  local copies, waits for them, and re-layouts  12.5 us (6%)
  Pallas kernels  12.3 us (6%)
    all_to_all x4, waiting for transfers between devices, exchanged(): return lax.all_to_all(value, axes, split_axis=0, concat_axis=0, tiled=True)  84.1 us
    all_to_all x3, blocking collectives, exchanged(): return lax.all_to_all(value, axes, split_axis=0, concat_axis=0, tiled=True)  71.3 us
    all_to_all x4, starting transfers between devices, exchanged(): return lax.all_to_all(value, axes, split_axis=0, concat_axis=0, tiled=True)  21.5 us
    pallas_call x6, Pallas kernels, call(): pl.pallas_call(kernel, out_shape=jax.ShapeDtypeStruct(shape, dtype), in_s...  12.3 us
    unnamed x26, local copies, waits for them, and re-layouts  5.99 us
    broadcast_in_dim x3, local copies, waits for them, and re-layouts, from_everyone(): return exchanged(jnp.broadcast_to(value, (count, *value.shape)), axes)  5.72 us
  transfers between devices with their start and end apart: 5, of which 5 were waited for; matrix products, arithmetic and copies ran while one was open for 0% of the time, Pallas kernels for 3%

profile of v1, /device:TPU:6, one launch (start us, length us, event | category | flops | bytes accessed | tf_op | source)
XLA Modules:
  0.0 209.7 jit_solution(14318521726833427097)
XLA Ops:
  0.0 0.8 copy-done.6
  2.9 40.8 %all_to_all.35 = bf16[16,64,384]{2,1,0:T(8,128)(2,1)S(1)} all-to-all(bf16[16,64,384]{2,1,0:T(8,128)(2,1)S(1)} %bitcast.8), channel_id=1, replica_groups=mesh['z_hi'=2,'x'=4,'yh'=4,'yl'=2,'z_lo'=4,'core'=2] {'z_hi','yh','yl'}, dimensions={0} | all-to-all | bytes 1572864 | tf_op jit(solution)/shard_map/all_to_all | solution.py:26
  43.7 2.2 %broadcast_in_dim.11 = bf16[4,16,64,384]{3,2,1,0:T(8,128)(2,1)} broadcast(bf16[16,64,384]{2,1,0:T(8,128)(2,1)S(1)} %all_to_all.35), dimensions={1,2,3} | broadcast | bytes 3932160 | tf_op jit(solution)/shard_map/broadcast_in_dim | solution.py:31
  45.8 4.9 %all-to-all-start.3 = ((bf16[4,16,64,384]{3,2,1,0:T(8,128)(2,1)}), bf16[4,16,64,384]{3,2,1,0:T(8,128)(2,1)S(1)}, u32[]{:S(2)}, u32[]{:S(2)}) async-start(bf16[4,16,64,384]{3,2,1,0:T(8,128)(2,1)} %broadcast_in_dim.11), calls=%async_computation.3 | async-start | bytes 6291456 | tf_op jit(solution)/shard_map/all_to_all | solution.py:26
  50.7 4.1 %collective-permute-start = (bf16[8,512]{1,0:T(8,128)(2,1)S(1)}, bf16[8,512]{1,0:T(8,128)(2,1)S(1)}, u32[]{:S(2)}, u32[]{:S(2)}) collective-permute-start(bf16[8,512]{1,0:T(8,128)(2,1)S(1)} %slice.3), channel_id=1, source_target_pairs={{0,8},{8,16},{16,24},{24,32},{32,40},{40,48},{48,56},{56,64},{64,7... | collective-permute-start | bytes 24584 | tf_op jit(solution)/shard_map/ppermute | solution.py:186
  54.8 3.7 %collective-permute-done = bf16[8,512]{1,0:T(8,128)(2,1)S(1)} collective-permute-done((bf16[8,512]{1,0:T(8,128)(2,1)S(1)}, bf16[8,512]{1,0:T(8,128)(2,1)S(1)}, u32[]{:S(2)}, u32[]{:S(2)}) %collective-permute-start) | collective-permute-done | bytes 8224 | tf_op jit(solution)/shard_map/ppermute | solution.py:186
  58.5 26.5 %all-to-all-done.3 = bf16[4,16,64,384]{3,2,1,0:T(8,128)(2,1)S(1)} async-done(((bf16[4,16,64,384]{3,2,1,0:T(8,128)(2,1)}), bf16[4,16,64,384]{3,2,1,0:T(8,128)(2,1)S(1)}, u32[]{:S(2)}, u32[]{:S(2)}) %all-to-all-start.3) | async-done | bytes 3145760 | tf_op jit(solution)/shard_map/all_to_all | solution.py:26
  85.0 1.5 broadcast_in_dim.9
  86.5 4.5 %all-to-all-start = ((bf16[16,136,512]{2,1,0:T(8,128)(2,1)}), bf16[16,136,512]{2,1,0:T(8,128)(2,1)}, u32[]{:S(2)}, u32[]{:S(2)}) async-start(bf16[16,136,512]{2,1,0:T(8,128)(2,1)} %broadcast_in_dim.9), calls=%async_computation | async-start | bytes 4456448 | tf_op jit(solution)/shard_map/all_to_all | solution.py:26
  91.9 49.8 %all-to-all-done = bf16[16,136,512]{2,1,0:T(8,128)(2,1)} async-done(((bf16[16,136,512]{2,1,0:T(8,128)(2,1)}), bf16[16,136,512]{2,1,0:T(8,128)(2,1)}, u32[]{:S(2)}, u32[]{:S(2)}) %all-to-all-start) | async-done | bytes 2228256 | tf_op jit(solution)/shard_map/all_to_all | solution.py:26
  141.7 2.0 broadcast_in_dim.10
  143.8 8.4 %all_to_all.36.x = bf16[2,4,4,136,512]{4,3,2,1,0:T(8,128)(2,1)} all-to-all(bf16[2,4,4,136,512]{4,3,2,1,0:T(8,128)(2,1)S(1)} %broadcast_in_dim.10), channel_id=1, replica_groups=mesh['z_hi'=2,'x'=4,'yh'=4,'yl'=2,'z_lo'=4,'core'=2] {'core'}, dimensions={0} | all-to-all | bytes 8912896 | tf_op jit(solution)/shard_map/all_to_all | solution.py:26
  152.1 4.4 %key_value.1 = bf16[16,4,8,128]{3,2,1,0:T(8,128)(2,1)} custom-call(bf16[2,4,4,136,512]{4,3,2,1,0:T(8,128)(2,1)} %all_to_all.36.x, bf16[4,2,8,64,384]{4,3,2,1,0:T(8,128)(2,1)S(1)} %bitcast.6, f32[3,3,128]{2,1,0:T(4,128)S(1)} %reshape.25.taps), custom_call_target="tpu_custom_call" | custom-call | flops 1140850688 | bytes 7606784 | tf_op jit(solution)/shard_map/key_value/pallas_call | solution.py:172
  156.5 8.4 %all-to-all-start.5 = ((bf16[16,4,8,128]{3,2,1,0:T(8,128)(2,1)}), bf16[16,4,8,128]{3,2,1,0:T(8,128)(2,1)S(1)}, u32[]{:S(2)}, u32[]{:S(2)}) async-start(bf16[16,4,8,128]{3,2,1,0:T(8,128)(2,1)} %key_value.1), calls=%async_computation.5 | async-start | bytes 262144 | tf_op jit(solution)/shard_map/all_to_all | solution.py:26
  164.9 4.4 %query.1 = bf16[4,128,128]{2,1,0:T(8,128)(2,1)} custom-call(bf16[2,4,4,136,512]{4,3,2,1,0:T(8,128)(2,1)} %all_to_all.36.x, bf16[4,2,8,64,384]{4,3,2,1,0:T(8,128)(2,1)S(1)} %bitcast.7, f32[3,3,128]{2,1,0:T(4,128)S(1)} %reshape.25.taps), custom_call_target="tpu_custom_call" | custom-call | flops 570425344 | bytes 7606784 | tf_op jit(solution)/shard_map/query/pallas_call | solution.py:172
  169.3 4.6 %all-to-all-done.5 = bf16[16,4,8,128]{3,2,1,0:T(8,128)(2,1)S(1)} async-done(((bf16[16,4,8,128]{3,2,1,0:T(8,128)(2,1)}), bf16[16,4,8,128]{3,2,1,0:T(8,128)(2,1)S(1)}, u32[]{:S(2)}, u32[]{:S(2)}) %all-to-all-start.5) | async-done | bytes 131104 | tf_op jit(solution)/shard_map/all_to_all | solution.py:26
  173.9 3.7 %all-to-all-start.4 = ((bf16[4,128,128]{2,1,0:T(8,128)(2,1)}), bf16[4,128,128]{2,1,0:T(8,128)(2,1)S(1)}, u32[]{:S(2)}, u32[]{:S(2)}) async-start(bf16[4,128,128]{2,1,0:T(8,128)(2,1)} %query.1), calls=%async_computation.4 | async-start | bytes 262144 | tf_op jit(solution)/shard_map/all_to_all | solution.py:26
  177.6 0.9 copy-done.1
  178.5 0.8 copy-done.4
  180.1 0.9 copy-done.5
  181.8 1.4 long_conv.1
  183.2 3.3 %all-to-all-done.4.query = bf16[4,128,128]{2,1,0:T(8,128)(2,1)S(1)} async-done(((bf16[4,128,128]{2,1,0:T(8,128)(2,1)}), bf16[4,128,128]{2,1,0:T(8,128)(2,1)S(1)}, u32[]{:S(2)}, u32[]{:S(2)}) %all-to-all-start.4) | async-done | bytes 131104 | tf_op jit(solution)/shard_map/all_to_all | solution.py:26
  186.5 22.2 %all_to_all.37.returned = bf16[64,8,128]{2,1,0:T(8,128)(2,1)S(1)} all-to-all(bf16[64,8,128]{2,1,0:T(8,128)(2,1)S(1)} %long_conv.1), channel_id=1, replica_groups=mesh['z_hi'=2,'x'=4,'yh'=4,'yl'=2,'z_lo'=4,'core'=2] {'z_hi','x','yh','yl'}, dimensions={0} | all-to-all | bytes 262144 | tf_op jit(solution)/shard_map/all_to_all | solution.py:26
  208.7 1.0 gate.1
  (29 shorter events, 4.4 us)
Async XLA Ops:
  0.0 0.8 copy-start.6
  0.8 0.8 copy-start.7
  1.7 0.8 copy-start.8
  45.8 4.9 %copy-start.11 = (bf16[128,512]{1,0:T(8,128)(2,1)S(1)}, bf16[128,512]{1,0:T(8,128)(2,1)}, u32[]{:S(2)}) copy-start(bf16[128,512]{1,0:T(8,128)(2,1)} %param.13) | copy-start | bytes 393220
  45.8 39.1 %all-to-all-start.3 = ((bf16[4,16,64,384]{3,2,1,0:T(8,128)(2,1)}), bf16[4,16,64,384]{3,2,1,0:T(8,128)(2,1)S(1)}, u32[]{:S(2)}, u32[]{:S(2)}) async-start(bf16[4,16,64,384]{3,2,1,0:T(8,128)(2,1)} %broadcast_in_dim.11), calls=%async_computation.3 | async-start | bytes 6291456 | tf_op jit(solution)/shard_map/all_to_all | solution.py:26
  50.7 7.7 %collective-permute-start = (bf16[8,512]{1,0:T(8,128)(2,1)S(1)}, bf16[8,512]{1,0:T(8,128)(2,1)S(1)}, u32[]{:S(2)}, u32[]{:S(2)}) collective-permute-start(bf16[8,512]{1,0:T(8,128)(2,1)S(1)} %slice.3), channel_id=1, source_target_pairs={{0,8},{8,16},{16,24},{24,32},{32,40},{40,48},{48,56},{56,64},{64,7... | collective-permute-start | bytes 24584 | tf_op jit(solution)/shard_map/ppermute | solution.py:186
  58.5 32.5 %copy-start.12 = (f32[3,3,512]{2,1,0:T(4,128)S(1)}, f32[3,3,512]{2,1,0:T(4,128)}, u32[]{:S(2)}) copy-start(f32[3,3,512]{2,1,0:T(4,128)} %param.17) | copy-start | bytes 55300
  86.5 55.2 %all-to-all-start = ((bf16[16,136,512]{2,1,0:T(8,128)(2,1)}), bf16[16,136,512]{2,1,0:T(8,128)(2,1)}, u32[]{:S(2)}, u32[]{:S(2)}) async-start(bf16[16,136,512]{2,1,0:T(8,128)(2,1)} %broadcast_in_dim.9), calls=%async_computation | async-start | bytes 4456448 | tf_op jit(solution)/shard_map/all_to_all | solution.py:26
  156.5 17.4 %all-to-all-start.5 = ((bf16[16,4,8,128]{3,2,1,0:T(8,128)(2,1)}), bf16[16,4,8,128]{3,2,1,0:T(8,128)(2,1)S(1)}, u32[]{:S(2)}, u32[]{:S(2)}) async-start(bf16[16,4,8,128]{3,2,1,0:T(8,128)(2,1)} %key_value.1), calls=%async_computation.5 | async-start | bytes 262144 | tf_op jit(solution)/shard_map/all_to_all | solution.py:26
  164.9 12.7 %copy-start = (bf16[256,256]{1,0:T(8,128)(2,1)S(1)}, bf16[256,256]{1,0:T(8,128)(2,1)}, u32[]{:S(2)}) copy-start(bf16[256,256]{1,0:T(8,128)(2,1)} %constant.70.inner) | copy-start | bytes 393220
  164.9 12.7 %copy-start.2 = (bf16[256,64]{1,0:T(8,128)(2,1)S(1)}, bf16[256,64]{1,0:T(8,128)(2,1)}, u32[]{:S(2)}) copy-start(bf16[256,64]{1,0:T(8,128)(2,1)} %constant.69.outer) | copy-start | bytes 98308
  164.9 12.7 %copy-start.3 = (f32[128,128]{1,0:T(8,128)S(1)}, f32[128,128]{1,0:T(8,128)}, u32[]{:S(2)}) copy-start(f32[128,128]{1,0:T(8,128)} %constant.65.clone.cos) | copy-start | bytes 196612
  164.9 15.2 %copy-start.10 = (f32[8]{0:T(128)S(1)}, f32[8]{0:T(128)}, u32[]{:S(2)}) copy-start(f32[8]{0:T(128)} %skip.1) | copy-start | bytes 100
  173.9 12.6 %all-to-all-start.4 = ((bf16[4,128,128]{2,1,0:T(8,128)(2,1)}), bf16[4,128,128]{2,1,0:T(8,128)(2,1)S(1)}, u32[]{:S(2)}, u32[]{:S(2)}) async-start(bf16[4,128,128]{2,1,0:T(8,128)(2,1)} %query.1), calls=%async_computation.4 | async-start | bytes 262144 | tf_op jit(solution)/shard_map/all_to_all | solution.py:26
  177.6 1.0 copy-start.1
  178.5 0.8 copy-start.4
  180.1 0.9 copy-start.5
  181.0 0.8 copy-start.9

commit v2 on v1

v2 whole, which is shorter than its diff:
```python
import math

import jax
import jax.numpy as jnp
import numpy as np
from jax import lax
from jax.experimental import pallas as pl
from jax.experimental.pallas import tpu as pltpu
from jax.sharding import Mesh
from jax.sharding import PartitionSpec as P

AXES = ("z_hi", "x", "yh", "yl", "z_lo", "core")
SIZES = (2, 4, 4, 2, 4, 2)
TOK = AXES[:4]
TP = AXES[4:]
HALO = 8
BLOCK = 128
ROWS = HALO + BLOCK
POINTS = 128
F32 = jnp.float32
BF16 = jnp.bfloat16


def exchanged(value, axes):
    return lax.all_to_all(value, axes, split_axis=0, concat_axis=0, tiled=True)


def from_everyone(value, axes):
    count = math.prod(SIZES[AXES.index(a)] for a in axes)
    return exchanged(jnp.broadcast_to(value, (count, *value.shape)), axes)


def dft_tables():
    n = np.arange(POINTS)
    full = 2.0 * np.pi * (np.outer(n, n) % POINTS) / POINTS
    cos, sin = np.cos(full), np.sin(full)
    half = POINTS // 2
    outer = np.concatenate([cos, -sin], axis=0)
    outer = np.concatenate([outer, outer], axis=1)
    inner = np.block([[cos, -sin], [sin, cos]])
    back_inner = np.block([[cos, sin], [-sin, cos]])
    back_outer = np.concatenate([cos[:half], -sin[:half]], axis=1) / POINTS**2
    twist = 2.0 * np.pi * np.outer(n, n) / POINTS**2
    tables = np.concatenate([inner, back_inner, outer, back_outer], axis=0)
    turns = np.concatenate([np.cos(twist), np.sin(twist)], axis=0)
    return jnp.asarray(tables, F32).astype(BF16), jnp.asarray(turns, F32)


def dot(a, b):
    return jnp.dot(a, b, preferred_element_type=F32)


def spectrum(rows, tables, turns):
    cos, sin = turns[0:POINTS], turns[POINTS:]
    blocks = jnp.concatenate(
        [rows[pl.ds(c, 64, stride=8), :].astype(BF16) for c in range(8)], axis=1
    )
    first = dot(tables[512:768, 0:64], blocks)
    turned = []
    for c in range(8):
        re = first[:POINTS, c * POINTS : (c + 1) * POINTS]
        im = first[POINTS:, c * POINTS : (c + 1) * POINTS]
        turned.append(
            jnp.concatenate([re * cos + im * sin, im * cos - re * sin], axis=1).astype(BF16)
        )
    return dot(jnp.concatenate(turned, axis=0), tables[0:256])


def filter_kernel(filters, tables, turns, spec, rows):
    taps = filters[...]
    unit = taps / jnp.sqrt(jnp.sum(taps * taps, axis=1, keepdims=True) + 1e-06)
    for b in range(64):
        rows[pl.ds(b * 8, 8), :] = unit[:, b * POINTS : (b + 1) * POINTS]
    spec[...] = spectrum(rows, tables, turns)


def conv_kernel(signal, spec, skip, tables, turns, mixed, rows, out):
    for z in range(2):
        rows[pl.ds(z * 256, 256), :] = signal[:, z].astype(F32).reshape(256, POINTS)
    cos, sin = turns[0:POINTS], turns[POINTS:]
    sig = spectrum(rows, tables, turns)
    re, im = sig[:, :POINTS], sig[:, POINTS:]
    f_re, f_im = spec[:, :POINTS], spec[:, POINTS:]
    prod = jnp.concatenate([re * f_re - im * f_im, re * f_im + im * f_re], axis=1)
    back = dot(prod.astype(BF16), tables[256:512])
    turned = []
    for c in range(8):
        b_re = back[c * POINTS : (c + 1) * POINTS, :POINTS]
        b_im = back[c * POINTS : (c + 1) * POINTS, POINTS:]
        turned.append(
            jnp.concatenate([b_re * cos - b_im * sin, b_re * sin + b_im * cos], axis=0).astype(BF16)
        )
    result = dot(tables[768:832], jnp.concatenate(turned, axis=1))
    for c in range(8):
        piece = result[:, c * POINTS : (c + 1) * POINTS]
        out[pl.ds(c, 64, stride=8), :] = piece + skip[c] * rows[pl.ds(c, 64, stride=8), :]
    mixed[...] = out[...].astype(BF16).reshape(64, 8, POINTS)


def order_table(rows_are_natural, mine=0):
    shape = (512, 512)
    row = lax.broadcasted_iota(jnp.int32, shape, 0)
    col = lax.broadcasted_iota(jnp.int32, shape, 1)
    grouped, natural = (col, row) if rows_are_natural else (row, col)
    quarter, xy, j = (grouped // 128) ^ mine, (grouped // 8) % 16, grouped % 8
    place = (quarter // 2) * 256 + xy * 16 + (quarter % 2) * 8 + j
    return (natural == place).astype(F32).astype(BF16)


def weights_kernel(w_key, w_value, w_query, out):
    table = order_table(True)
    for p, ref in enumerate((w_key, w_value, w_query)):
        sorted_cols = dot(ref[...], table).astype(BF16)
        for quarter in range(4):
            piece = sorted_cols[:, quarter * 128 : (quarter + 1) * 128]
            for yh in range(4):
                out[quarter // 2, yh, quarter % 2, :, p * 128 : (p + 1) * 128] = piece


NEAR = (0, 1, -1, 2, -2)
FAR = (3, -3, 4)


def projected(where, near, far, near_other, far_other, w, at, width, acc):
    z, core = where[0], where[1]
    acc[...] = jnp.zeros_like(acc)
    for refs, steps in (((near, near_other), NEAR), ((far, far_other), FAR)):
        for i, step in enumerate(steps):
            source = (z + step) & 7
            rows_at = pl.ds(pl.multiple_of((source >> 2) * 2 * ROWS, 2 * ROWS), 2 * ROWS)
            total = acc[rows_at, :]
            for ref, half in zip(refs, (core, 1 - core)):
                part = (source & 3) * 2 + half
                weights = w[part & 3, part >> 2, :, :, at : at + width].reshape(512, width)
                total += dot(ref[i], weights)
            acc[rows_at, :] = total


def short(acc, group, at, taps):
    top = group * ROWS + HALO
    cols = pl.ds(at, 128)
    return (
        taps[0:1] * acc[pl.ds(top, BLOCK), cols]
        + taps[1:2] * acc[pl.ds(top - 1, BLOCK), cols]
        + taps[2:3] * acc[pl.ds(top - 2, BLOCK), cols]
    )


def key_value_kernel(where, near, far, near_other, far_other, w, taps, out, acc):
    projected(where, near, far, near_other, far_other, w, 0, 256, acc)
    for group in range(4):
        keyed = short(acc, group, 0, taps[1])
        valued = short(acc, group, 128, taps[2])
        out[:, group] = (keyed * valued).T.reshape(16, 8, BLOCK).astype(BF16)


def query_kernel(where, near, far, near_other, far_other, w, taps, out, acc):
    projected(where, near, far, near_other, far_other, w, 256, 128, acc)
    for group in range(4):
        out[group ^ where[2]] = short(acc, group, 0, taps[0]).astype(BF16)


def gate_kernel(where, q0, q1, q2, q3, returned, out):
    cols = jnp.concatenate([q0[0], q1[...], q2[...], q3[...]], axis=1)
    natural = dot(cols, order_table(False, where[2]))
    mixed = returned[...].astype(F32).reshape(512, BLOCK).T
    out[...] = (natural * mixed).astype(BF16)


def call(kernel, shape, dtype, args, scratch=(), in_specs=None, flops=10**8, name=None):
    whole = pl.BlockSpec(memory_space=pltpu.VMEM)
    specs = in_specs or [whole] * len(args)
    moved = sum(math.prod(a.shape) * a.dtype.itemsize for a in args)
    return pl.pallas_call(
        kernel,
        out_shape=jax.ShapeDtypeStruct(shape, dtype),
        in_specs=specs,
        out_specs=whole,
        scratch_shapes=list(scratch),
        compiler_params=pltpu.CompilerParams(vmem_limit_bytes=48 * 2**20),
        cost_estimate=pl.CostEstimate(flops=flops, bytes_accessed=moved, transcendentals=0),
        name=name,
    )(*args)


def shifted(value, axes, step, wrap=True):
    count = math.prod(SIZES[AXES.index(a)] for a in axes)
    pairs = [(i + step, i) for i in range(count) if wrap or 0 <= i + step < count]
    return lax.ppermute(value, axes, [(source % count, i) for source, i in pairs])


def swapped(value, axes, bits):
    count = math.prod(SIZES[AXES.index(a)] for a in axes)
    return lax.ppermute(value, axes, [(i, i ^ bits) for i in range(count)])


def local(tokens, w_query, w_key, w_value, short_taps, filters, skip_gain):
    place = lax.axis_index(AXES)
    core, z_lo, yl, z_hi = place % 2, place // 2 % 4, place // 8 % 2, place // 256
    where = jnp.stack([z_hi * 4 + z_lo, core, z_hi * 2 + yl])

    sent = call(weights_kernel, (2, 4, 2, 64, 384), BF16, (w_key, w_value, w_query), name="sort_weights")
    first = exchanged(sent.reshape(16, 64, 384), ("z_hi", "yh", "yl"))
    weights = from_everyone(first, ("x",)).reshape(4, 2, 8, 64, 384)

    halo = shifted(tokens[-HALO:], TOK, -1, wrap=False)
    mine = jnp.concatenate([halo, tokens], axis=0)
    other = swapped(mine, ("yl",), 1)
    first_half = yl == 0
    pair = jnp.concatenate(
        [jnp.where(first_half, mine, other), jnp.where(first_half, other, mine)], axis=0
    )
    ring = ("z_hi", "z_lo")
    ahead, behind = shifted(pair, ring, 2), shifted(pair, ring, -2)
    near = jnp.stack([pair, shifted(pair, ring, 1), shifted(pair, ring, -1), ahead, behind])
    near_other = swapped(near, ("core",), 1)
    far = jnp.stack([shifted(ahead, ring, 1), shifted(behind, ring, -1), shifted(ahead, ring, 2)])
    far_other = swapped(far, ("core",), 1)

    taps = short_taps.reshape(3, 3, 2, 16, 2, 8)
    taps = lax.dynamic_index_in_dim(taps, z_hi, 2, keepdims=False)
    taps = lax.dynamic_index_in_dim(taps, yl, 3, keepdims=False).reshape(3, 3, 128)

    tables, turns = dft_tables()
    spec = call(
        filter_kernel,
        (8 * POINTS, 2 * POINTS),
        F32,
        (filters, tables, turns),
        (pltpu.VMEM((512, POINTS), F32),),
        name="filter_spectrum",
    )

    whole = pl.BlockSpec(memory_space=pltpu.VMEM)
    smem = pl.BlockSpec(memory_space=pltpu.SMEM)
    features = (where, near, far, near_other, far_other, weights, taps)
    key_value = call(
        key_value_kernel,
        (16, 4, 8, BLOCK),
        BF16,
        features,
        (pltpu.VMEM((4 * ROWS, 256), F32),),
        in_specs=[smem] + [whole] * 6,
        flops=2 * 544 * 4096 * 256,
        name="key_value",
    )
    owned = exchanged(key_value, ("x", "yh"))
    query = call(
        query_kernel,
        (4, BLOCK, 128),
        BF16,
        features,
        (pltpu.VMEM((4 * ROWS, 128), F32),),
        in_specs=[smem] + [whole] * 6,
        flops=2 * 544 * 4096 * 128,
        name="query",
    )
    queries = [query] + [swapped(query[bits], ("z_hi", "yl"), bits) for bits in (1, 2, 3)]
    mixed = call(
        conv_kernel,
        (64, 8, BLOCK),
        BF16,
        (owned.reshape(16, 2, 2, 8, BLOCK), spec, skip_gain, tables, turns),
        (pltpu.VMEM((512, POINTS), F32), pltpu.VMEM((512, POINTS), F32)),
        in_specs=[whole, whole, smem, whole, whole],
        flops=2 * 168 * 10**6,
        name="long_conv",
    )
    returned = exchanged(mixed, TOK)
    return call(
        gate_kernel,
        (BLOCK, 512),
        BF16,
        (where, *queries, returned),
        in_specs=[smem] + [whole] * 5,
        name="gate",
    )


def solution(mesh):
    fine = Mesh(mesh.devices.reshape(SIZES), AXES)
    in_specs = (
        P(TOK, TP),
        P(TOK, TP),
        P(TOK, TP),
        P(TOK, TP),
        P(None, None, TP),
        P(TP + TOK, None),
        P(TP + TOK),
    )
    return jax.shard_map(local, mesh=fine, in_specs=in_specs, out_specs=P(TOK, TP), check_vma=False)
```

time: 212 us -> 172 us (0.81)
  blocking collectives: 71.3 us -> 0 us
  starting transfers between devices: 25.6 us -> 87.4 us
  waiting for transfers between devices: 87.8 us -> 57.9 us
  local copies, waits for them, and re-layouts: 12.5 us -> 9.02 us
  Pallas kernels: 12.3 us -> 15.4 us
    all_to_all x4, waiting for transfers between devices: 84.1 us -> 1.65 us  [exchanged(): return lax.all_to_all(value, axes, split_axis=0, concat_axis=0, tiled=True)]
    all_to_all x3 -> x0, blocking collectives: 71.3 us -> none  [exchanged(): return lax.all_to_all(value, axes, split_axis=0, concat_axis=0, tiled=True)]
    ppermute x1 -> x14, waiting for transfers between devices: 3.66 us -> 56.3 us  [the longest x8 41.6 us: shifted(): lax.ppermute(value, axes, [(source % count, i) for source, i in pairs])]
    ppermute x1 -> x14, starting transfers between devices: 4.07 us -> 48.5 us  [the longest x8 29.6 us: shifted(): lax.ppermute(value, axes, [(source % count, i) for source, i in pairs])]
    all_to_all x4, starting transfers between devices: 21.5 us -> 38.8 us  [exchanged(): return lax.all_to_all(value, axes, split_axis=0, concat_axis=0, tiled=True)]
    broadcast_in_dim x3 -> x1, local copies, waits for them, and re-layouts: 5.72 us -> 2.21 us  [from_everyone(): return exchanged(jnp.broadcast_to(value, (count, *value.shape)), axes)]
    pallas_call x6, Pallas kernels: 12.3 us -> 15.4 us  [call(): pl.pallas_call(kernel, out_shape=jax.ShapeDtypeStruct(shape, dtype), in_s...]
    unnamed x26 -> x28, local copies, waits for them, and re-layouts: 5.99 us -> 5.98 us
  transfers between devices with their start and end apart: 5 -> 18, of which waited for: 5 -> 9; matrix products, arithmetic and copies ran while one was open for 0% -> 2% of each run, Pallas kernels for 3% -> 3%
where the time goes in v2:
time: 172 us; the launch traced here: 170 us
  starting transfers between devices  87.4 us (51%)
  waiting for transfers between devices  57.9 us (34%)
  Pallas kernels  15.4 us (9%)
  local copies, waits for them, and re-layouts  9.02 us (5%)
    ppermute x8, waiting for transfers between devices, shifted(): lax.ppermute(value, axes, [(source % count, i) for source, i in pairs])  41.6 us
    all_to_all x4, starting transfers between devices, exchanged(): return lax.all_to_all(value, axes, split_axis=0, concat_axis=0, tiled=True)  38.8 us
    ppermute x8, starting transfers between devices, shifted(): lax.ppermute(value, axes, [(source % count, i) for source, i in pairs])  29.6 us
    ppermute x6, starting transfers between devices, swapped(): return lax.ppermute(value, axes, [(i, i ^ bits) for i in range(count)])  19 us
    pallas_call x6, Pallas kernels, call(): pl.pallas_call(kernel, out_shape=jax.ShapeDtypeStruct(shape, dtype), in_s...  15.4 us
    ppermute x6, waiting for transfers between devices, swapped(): return lax.ppermute(value, axes, [(i, i ^ bits) for i in range(count)])  14.7 us
    unnamed x28, local copies, waits for them, and re-layouts  5.98 us
  transfers between devices with their start and end apart: 18, of which 9 were waited for; matrix products, arithmetic and copies ran while one was open for 2% of the time, Pallas kernels for 3%

profile of v2, /device:TPU:6, one launch (start us, length us, event | category | flops | bytes accessed | tf_op | source)
XLA Modules:
  0.0 170.5 jit_solution(14394782470531243724)
XLA Ops:
  3.8 15.6 %all-to-all-start = ((bf16[16,64,384]{2,1,0:T(8,128)(2,1)}), bf16[16,64,384]{2,1,0:T(8,128)(2,1)S(1)}, u32[]{:S(2)}, u32[]{:S(2)}) async-start(bf16[16,64,384]{2,1,0:T(8,128)(2,1)} %bitcast.11), calls=%async_computation | async-start | bytes 1572864 | tf_op jit(solution)/shard_map/all_to_all | solution.py:25
  19.5 3.8 %collective-permute-start = (bf16[8,512]{1,0:T(8,128)(2,1)S(1)}, bf16[8,512]{1,0:T(8,128)(2,1)S(1)}, u32[]{:S(2)}, u32[]{:S(2)}) collective-permute-start(bf16[8,512]{1,0:T(8,128)(2,1)S(1)} %slice.12), channel_id=1, source_target_pairs={{0,8},{8,16},{16,24},{24,32},{32,40},{40,48},{48,56},{56,64},{64,7... | collective-permute-start | bytes 24584 | tf_op jit(solution)/shard_map/ppermute | solution.py:189
  23.3 16.9 %collective-permute-done = bf16[8,512]{1,0:T(8,128)(2,1)S(1)} collective-permute-done((bf16[8,512]{1,0:T(8,128)(2,1)S(1)}, bf16[8,512]{1,0:T(8,128)(2,1)S(1)}, u32[]{:S(2)}, u32[]{:S(2)}) %collective-permute-start) | collective-permute-done | bytes 8224 | tf_op jit(solution)/shard_map/ppermute | solution.py:189
  42.2 5.0 %collective-permute-done.1 = bf16[136,512]{1,0:T(8,128)(2,1)S(1)} collective-permute-done((bf16[136,512]{1,0:T(8,128)(2,1)S(1)}, bf16[136,512]{1,0:T(8,128)(2,1)S(1)}, u32[]{:S(2)}, u32[]{:S(2)}) %collective-permute-start.1) | collective-permute-done | bytes 139296 | tf_op jit(solution)/shard_map/ppermute | solution.py:194
  47.3 7.3 %collective-permute-start.2 = (bf16[272,512]{1,0:T(8,128)(2,1)S(1)}, bf16[272,512]{1,0:T(8,128)(2,1)S(1)}, u32[]{:S(2)}, u32[]{:S(2)}) collective-permute-start(bf16[272,512]{1,0:T(8,128)(2,1)S(1)} %pad_maximum_fusion.1), channel_id=1, source_target_pairs={{2,0},{4,2},{6,4},{256,6},{258,256},{260,258},{262,260},{0,262},{3... | collective-permute-start | bytes 835592 | tf_op jit(solution)/shard_map/ppermute | solution.py:189
  58.7 7.0 %all-to-all-start.1 = ((bf16[4,16,64,384]{3,2,1,0:T(8,128)(2,1)}), bf16[4,16,64,384]{3,2,1,0:T(8,128)(2,1)}, u32[]{:S(2)}, u32[]{:S(2)}) async-start(bf16[4,16,64,384]{3,2,1,0:T(8,128)(2,1)} %broadcast_in_dim.3), calls=%async_computation.1 | async-start | bytes 6291456 | tf_op jit(solution)/shard_map/all_to_all | solution.py:25
  65.8 4.0 %collective-permute-start.4 = (bf16[272,512]{1,0:T(8,128)(2,1)S(1)}, bf16[272,512]{1,0:T(8,128)(2,1)S(1)}, u32[]{:S(2)}, u32[]{:S(2)}) collective-permute-start(bf16[272,512]{1,0:T(8,128)(2,1)S(1)} %pad_maximum_fusion.1), channel_id=1, source_target_pairs={{4,0},{6,2},{256,4},{258,6},{260,256},{262,258},{0,260},{2,262},{5... | collective-permute-start | bytes 835592 | tf_op jit(solution)/shard_map/ppermute | solution.py:189
  69.8 2.7 %collective-permute-start.5 = (bf16[272,512]{1,0:T(8,128)(2,1)S(1)}, bf16[272,512]{1,0:T(8,128)(2,1)S(1)}, u32[]{:S(2)}, u32[]{:S(2)}) collective-permute-start(bf16[272,512]{1,0:T(8,128)(2,1)S(1)} %pad_maximum_fusion.1), channel_id=1, source_target_pairs={{260,0},{262,2},{0,4},{2,6},{4,256},{6,258},{256,260},{258,262},{2... | collective-permute-start | bytes 835592 | tf_op jit(solution)/shard_map/ppermute | solution.py:189
  72.6 5.0 %collective-permute-done.4 = bf16[272,512]{1,0:T(8,128)(2,1)S(1)} collective-permute-done((bf16[272,512]{1,0:T(8,128)(2,1)S(1)}, bf16[272,512]{1,0:T(8,128)(2,1)S(1)}, u32[]{:S(2)}, u32[]{:S(2)}) %collective-permute-start.4) | collective-permute-done | bytes 278560 | tf_op jit(solution)/shard_map/ppermute | solution.py:189
  77.7 5.6 %collective-permute-done.5 = bf16[272,512]{1,0:T(8,128)(2,1)S(1)} collective-permute-done((bf16[272,512]{1,0:T(8,128)(2,1)S(1)}, bf16[272,512]{1,0:T(8,128)(2,1)S(1)}, u32[]{:S(2)}, u32[]{:S(2)}) %collective-permute-start.5) | collective-permute-done | bytes 278560 | tf_op jit(solution)/shard_map/ppermute | solution.py:189
  85.2 2.7 %collective-permute-start.8 = (bf16[272,512]{1,0:T(8,128)(2,1)S(1)}, bf16[272,512]{1,0:T(8,128)(2,1)S(1)}, u32[]{:S(2)}, u32[]{:S(2)}) collective-permute-start(bf16[272,512]{1,0:T(8,128)(2,1)S(1)} %collective-permute-done.4), channel_id=1, source_target_pairs={{4,0},{6,2},{256,4},{258,6},{260,256},{262,258},{0,260},{2,262},{5... | collective-permute-start | bytes 835592 | tf_op jit(solution)/shard_map/ppermute | solution.py:189
  88.0 3.9 %collective-permute-start.7 = (bf16[272,512]{1,0:T(8,128)(2,1)S(1)}, bf16[272,512]{1,0:T(8,128)(2,1)S(1)}, u32[]{:S(2)}, u32[]{:S(2)}) collective-permute-start(bf16[272,512]{1,0:T(8,128)(2,1)S(1)} %collective-permute-done.5), channel_id=1, source_target_pairs={{262,0},{0,2},{2,4},{4,6},{6,256},{256,258},{258,260},{260,262},{2... | collective-permute-start | bytes 835592 | tf_op jit(solution)/shard_map/ppermute | solution.py:189
  91.9 3.1 %collective-permute-start.6 = (bf16[272,512]{1,0:T(8,128)(2,1)S(1)}, bf16[272,512]{1,0:T(8,128)(2,1)S(1)}, u32[]{:S(2)}, u32[]{:S(2)}) collective-permute-start(bf16[272,512]{1,0:T(8,128)(2,1)S(1)} %collective-permute-done.4), channel_id=1, source_target_pairs={{2,0},{4,2},{6,4},{256,6},{258,256},{260,258},{262,260},{0,262},{3... | collective-permute-start | bytes 835592 | tf_op jit(solution)/shard_map/ppermute | solution.py:189
  95.0 5.3 %collective-permute-done.8 = bf16[272,512]{1,0:T(8,128)(2,1)S(1)} collective-permute-done((bf16[272,512]{1,0:T(8,128)(2,1)S(1)}, bf16[272,512]{1,0:T(8,128)(2,1)S(1)}, u32[]{:S(2)}, u32[]{:S(2)}) %collective-permute-start.8) | collective-permute-done | bytes 278560 | tf_op jit(solution)/shard_map/ppermute | solution.py:189
  100.3 8.8 %collective-permute-done.6 = bf16[272,512]{1,0:T(8,128)(2,1)S(1)} collective-permute-done((bf16[272,512]{1,0:T(8,128)(2,1)S(1)}, bf16[272,512]{1,0:T(8,128)(2,1)S(1)}, u32[]{:S(2)}, u32[]{:S(2)}) %collective-permute-start.6) | collective-permute-done | bytes 278560 | tf_op jit(solution)/shard_map/ppermute | solution.py:189
  113.4 5.2 %key_value.1 = bf16[16,4,8,128]{3,2,1,0:T(8,128)(2,1)} custom-call(s32[3]{0:T(128)S(1)} %pad_add_fusion.where, bf16[5,272,512]{2,1,0:T(8,128)(2,1)S(1)} %bitcast_dynamic-update-slice_fusion.near, bf16[3,272,512]{2,1,0:T(8,128)(2,1)S(1)} %pad_maximum_fusion.far, bf16[5,272,512]{2,1,0:T(8,128)(2,1)} %collective-permute-done.9.near_other, ...), custom_call_target="tpu_custom_call" | custom-call | flops 1140850688 | bytes 7606796 | tf_op jit(solution)/shard_map/key_value/pallas_call | solution.py:174
  118.7 6.8 %all-to-all-start.2 = ((bf16[16,4,8,128]{3,2,1,0:T(8,128)(2,1)}), bf16[16,4,8,128]{3,2,1,0:T(8,128)(2,1)}, u32[]{:S(2)}, u32[]{:S(2)}) async-start(bf16[16,4,8,128]{3,2,1,0:T(8,128)(2,1)} %key_value.1), calls=%async_computation.2 | async-start | bytes 262144 | tf_op jit(solution)/shard_map/all_to_all | solution.py:25
  128.6 4.0 %query.1.q0 = bf16[4,128,128]{2,1,0:T(8,128)(2,1)S(1)} custom-call(s32[3]{0:T(128)S(1)} %pad_add_fusion.where, bf16[5,272,512]{2,1,0:T(8,128)(2,1)S(1)} %bitcast_dynamic-update-slice_fusion.near, bf16[3,272,512]{2,1,0:T(8,128)(2,1)S(1)} %pad_maximum_fusion.far, bf16[5,272,512]{2,1,0:T(8,128)(2,1)} %collective-permute-done.9.near_other, ...), custom_call_target="tpu_custom_call" | custom-call | flops 570425344 | bytes 7606796 | tf_op jit(solution)/shard_map/query/pallas_call | solution.py:174
  135.2 2.5 %long_conv.1 = bf16[64,8,128]{2,1,0:T(8,128)(2,1)} custom-call(bf16[16,2,2,8,128]{4,3,2,1,0:T(8,128)(2,1)} %bitcast.16.signal, f32[1024,256]{1,0:T(8,128)S(1)} %filter_spectrum.1.spec, f32[8]{0:T(128)S(1)} %copy-done.9, bf16[832,256]{1,0:T(8,128)(2,1)S(1)} %copy-done.3, f32[256,128]{1,0:T(8,128)S(1)} %copy-done.4), custom_call_target="tpu_custom_call" | custom-call | flops 336000000 | bytes 1736736 | tf_op jit(solution)/shard_map/long_conv/pallas_call | solution.py:174
  137.7 9.4 %all-to-all-start.3 = ((bf16[64,8,128]{2,1,0:T(8,128)(2,1)}), bf16[64,8,128]{2,1,0:T(8,128)(2,1)S(1)}, u32[]{:S(2)}, u32[]{:S(2)}) async-start(bf16[64,8,128]{2,1,0:T(8,128)(2,1)} %long_conv.1), calls=%async_computation.3 | async-start | bytes 262144 | tf_op jit(solution)/shard_map/all_to_all | solution.py:25
  147.1 3.4 %collective-permute-start.11 = (bf16[128,128]{1,0:T(8,128)(2,1)S(1)}, bf16[128,128]{1,0:T(8,128)(2,1)S(1)}, u32[]{:S(2)}, u32[]{:S(2)}) collective-permute-start(bf16[128,128]{1,0:T(8,128)(2,1)S(1)} %get-tuple-element.9), channel_id=1, source_target_pairs={{0,8},{8,0},{256,264},{264,256},{1,9},{9,1},{257,265},{265,257},{2... | collective-permute-start | bytes 98312 | tf_op jit(solution)/shard_map/ppermute | solution.py:194
  150.5 7.5 %collective-permute-start.12 = (bf16[128,128]{1,0:T(8,128)(2,1)S(1)}, bf16[128,128]{1,0:T(8,128)(2,1)S(1)}, u32[]{:S(2)}, u32[]{:S(2)}) collective-permute-start(bf16[128,128]{1,0:T(8,128)(2,1)S(1)} %get-tuple-element.8), channel_id=1, source_target_pairs={{0,256},{8,264},{256,0},{264,8},{1,257},{9,265},{257,1},{265,9},{2... | collective-permute-start | bytes 98312 | tf_op jit(solution)/shard_map/ppermute | solution.py:194
  158.0 2.2 %collective-permute-start.13 = (bf16[128,128]{1,0:T(8,128)(2,1)S(1)}, bf16[128,128]{1,0:T(8,128)(2,1)S(1)}, u32[]{:S(2)}, u32[]{:S(2)}) collective-permute-start(bf16[128,128]{1,0:T(8,128)(2,1)S(1)} %get-tuple-element.7), channel_id=1, source_target_pairs={{0,264},{8,256},{256,8},{264,0},{1,265},{9,257},{257,9},{265,1},{2... | collective-permute-start | bytes 98312 | tf_op jit(solution)/shard_map/ppermute | solution.py:194
  160.3 8.5 %collective-permute-done.13.q3 = bf16[128,128]{1,0:T(8,128)(2,1)S(1)} collective-permute-done((bf16[128,128]{1,0:T(8,128)(2,1)S(1)}, bf16[128,128]{1,0:T(8,128)(2,1)S(1)}, u32[]{:S(2)}, u32[]{:S(2)}) %collective-permute-start.13) | collective-permute-done | bytes 32800 | tf_op jit(solution)/shard_map/ppermute | solution.py:194
  (59 shorter events, 23.7 us)
Async XLA Ops:
  2.5 17.0 %copy-start.10 = (bf16[128,512]{1,0:T(8,128)(2,1)S(1)}, bf16[128,512]{1,0:T(8,128)(2,1)}, u32[]{:S(2)}) copy-start(bf16[128,512]{1,0:T(8,128)(2,1)} %param.9) | copy-start | bytes 393220
  3.8 52.7 %all-to-all-start = ((bf16[16,64,384]{2,1,0:T(8,128)(2,1)}), bf16[16,64,384]{2,1,0:T(8,128)(2,1)S(1)}, u32[]{:S(2)}, u32[]{:S(2)}) async-start(bf16[16,64,384]{2,1,0:T(8,128)(2,1)} %bitcast.11), calls=%async_computation | async-start | bytes 1572864 | tf_op jit(solution)/shard_map/all_to_all | solution.py:25
  19.5 20.7 %collective-permute-start = (bf16[8,512]{1,0:T(8,128)(2,1)S(1)}, bf16[8,512]{1,0:T(8,128)(2,1)S(1)}, u32[]{:S(2)}, u32[]{:S(2)}) collective-permute-start(bf16[8,512]{1,0:T(8,128)(2,1)S(1)} %slice.12), channel_id=1, source_target_pairs={{0,8},{8,16},{16,24},{24,32},{32,40},{40,48},{48,56},{56,64},{64,7... | collective-permute-start | bytes 24584 | tf_op jit(solution)/shard_map/ppermute | solution.py:189
  40.3 6.9 %collective-permute-start.1 = (bf16[136,512]{1,0:T(8,128)(2,1)S(1)}, bf16[136,512]{1,0:T(8,128)(2,1)S(1)}, u32[]{:S(2)}, u32[]{:S(2)}) collective-permute-start(bf16[136,512]{1,0:T(8,128)(2,1)S(1)} %constant_dynamic-update-slice_fusion), channel_id=1, source_target_pairs={{0,8},{8,0},{1,9},{9,1},{2,10},{10,2},{3,11},{11,3},{4,12},{12,4},... | collective-permute-start | bytes 417800 | tf_op jit(solution)/shard_map/ppermute | solution.py:194
  47.3 25.3 %collective-permute-start.2 = (bf16[272,512]{1,0:T(8,128)(2,1)S(1)}, bf16[272,512]{1,0:T(8,128)(2,1)S(1)}, u32[]{:S(2)}, u32[]{:S(2)}) collective-permute-start(bf16[272,512]{1,0:T(8,128)(2,1)S(1)} %pad_maximum_fusion.1), channel_id=1, source_target_pairs={{2,0},{4,2},{6,4},{256,6},{258,256},{260,258},{262,260},{0,262},{3... | collective-permute-start | bytes 835592 | tf_op jit(solution)/shard_map/ppermute | solution.py:189
  54.6 18.0 %collective-permute-start.3 = (bf16[272,512]{1,0:T(8,128)(2,1)S(1)}, bf16[272,512]{1,0:T(8,128)(2,1)S(1)}, u32[]{:S(2)}, u32[]{:S(2)}) collective-permute-start(bf16[272,512]{1,0:T(8,128)(2,1)S(1)} %pad_maximum_fusion.1), channel_id=1, source_target_pairs={{262,0},{0,2},{2,4},{4,6},{6,256},{256,258},{258,260},{260,262},{2... | collective-permute-start | bytes 835592 | tf_op jit(solution)/shard_map/ppermute | solution.py:189
  58.7 54.7 %all-to-all-start.1 = ((bf16[4,16,64,384]{3,2,1,0:T(8,128)(2,1)}), bf16[4,16,64,384]{3,2,1,0:T(8,128)(2,1)}, u32[]{:S(2)}, u32[]{:S(2)}) async-start(bf16[4,16,64,384]{3,2,1,0:T(8,128)(2,1)} %broadcast_in_dim.3), calls=%async_computation.1 | async-start | bytes 6291456 | tf_op jit(solution)/shard_map/all_to_all | solution.py:25
  65.8 11.8 %collective-permute-start.4 = (bf16[272,512]{1,0:T(8,128)(2,1)S(1)}, bf16[272,512]{1,0:T(8,128)(2,1)S(1)}, u32[]{:S(2)}, u32[]{:S(2)}) collective-permute-start(bf16[272,512]{1,0:T(8,128)(2,1)S(1)} %pad_maximum_fusion.1), channel_id=1, source_target_pairs={{4,0},{6,2},{256,4},{258,6},{260,256},{262,258},{0,260},{2,262},{5... | collective-permute-start | bytes 835592 | tf_op jit(solution)/shard_map/ppermute | solution.py:189
  69.8 13.5 %collective-permute-start.5 = (bf16[272,512]{1,0:T(8,128)(2,1)S(1)}, bf16[272,512]{1,0:T(8,128)(2,1)S(1)}, u32[]{:S(2)}, u32[]{:S(2)}) collective-permute-start(bf16[272,512]{1,0:T(8,128)(2,1)S(1)} %pad_maximum_fusion.1), channel_id=1, source_target_pairs={{260,0},{262,2},{0,4},{2,6},{4,256},{6,258},{256,260},{258,262},{2... | collective-permute-start | bytes 835592 | tf_op jit(solution)/shard_map/ppermute | solution.py:189
  72.6 38.6 %copy-start.11 = (f32[3,3,512]{2,1,0:T(4,128)S(1)}, f32[3,3,512]{2,1,0:T(4,128)}, u32[]{:S(2)}) copy-start(f32[3,3,512]{2,1,0:T(4,128)} %param.13) | copy-start | bytes 55300
  83.3 30.1 %collective-permute-start.9 = (bf16[5,272,512]{2,1,0:T(8,128)(2,1)S(1)}, bf16[5,272,512]{2,1,0:T(8,128)(2,1)}, u32[]{:S(2)}, u32[]{:S(2)}) collective-permute-start(bf16[5,272,512]{2,1,0:T(8,128)(2,1)S(1)} %bitcast_dynamic-update-slice_fusion.near), channel_id=1, source_target_pairs={{0,1},{1,0},{2,3},{3,2},{4,5},{5,4},{6,7},{7,6},{8,9},{9,8},{10,11... | collective-permute-start | bytes 4177928 | tf_op jit(solution)/shard_map/ppermute | solution.py:194
  85.2 15.0 %collective-permute-start.8 = (bf16[272,512]{1,0:T(8,128)(2,1)S(1)}, bf16[272,512]{1,0:T(8,128)(2,1)S(1)}, u32[]{:S(2)}, u32[]{:S(2)}) collective-permute-start(bf16[272,512]{1,0:T(8,128)(2,1)S(1)} %collective-permute-done.4), channel_id=1, source_target_pairs={{4,0},{6,2},{256,4},{258,6},{260,256},{262,258},{0,260},{2,262},{5... | collective-permute-start | bytes 835592 | tf_op jit(solution)/shard_map/ppermute | solution.py:189
  88.0 12.3 %collective-permute-start.7 = (bf16[272,512]{1,0:T(8,128)(2,1)S(1)}, bf16[272,512]{1,0:T(8,128)(2,1)S(1)}, u32[]{:S(2)}, u32[]{:S(2)}) collective-permute-start(bf16[272,512]{1,0:T(8,128)(2,1)S(1)} %collective-permute-done.5), channel_id=1, source_target_pairs={{262,0},{0,2},{2,4},{4,6},{6,256},{256,258},{258,260},{260,262},{2... | collective-permute-start | bytes 835592 | tf_op jit(solution)/shard_map/ppermute | solution.py:189
  91.9 17.2 %collective-permute-start.6 = (bf16[272,512]{1,0:T(8,128)(2,1)S(1)}, bf16[272,512]{1,0:T(8,128)(2,1)S(1)}, u32[]{:S(2)}, u32[]{:S(2)}) collective-permute-start(bf16[272,512]{1,0:T(8,128)(2,1)S(1)} %collective-permute-done.4), channel_id=1, source_target_pairs={{2,0},{4,2},{6,4},{256,6},{258,256},{260,258},{262,260},{0,262},{3... | collective-permute-start | bytes 835592 | tf_op jit(solution)/shard_map/ppermute | solution.py:189
  109.2 4.2 %collective-permute-start.10 = (bf16[3,272,512]{2,1,0:T(8,128)(2,1)S(1)}, bf16[3,272,512]{2,1,0:T(8,128)(2,1)S(1)}, u32[]{:S(2)}, u32[]{:S(2)}) collective-permute-start(bf16[3,272,512]{2,1,0:T(8,128)(2,1)S(1)} %pad_maximum_fusion.far), channel_id=1, source_target_pairs={{0,1},{1,0},{2,3},{3,2},{4,5},{5,4},{6,7},{7,6},{8,9},{9,8},{10,11... | collective-permute-start | bytes 2506760 | tf_op jit(solution)/shard_map/ppermute | solution.py:194
  113.4 5.3 %copy-start = (bf16[3,272,512]{2,1,0:T(8,128)(2,1)}, bf16[3,272,512]{2,1,0:T(8,128)(2,1)S(1)}, u32[]{:S(2)}) copy-start(bf16[3,272,512]{2,1,0:T(8,128)(2,1)S(1)} %collective-permute-done.10.far_other) | copy-start | bytes 2506756
  113.4 12.0 %copy-start.4 = (f32[256,128]{1,0:T(8,128)S(1)}, f32[256,128]{1,0:T(8,128)}, u32[]{:S(2)}) copy-start(f32[256,128]{1,0:T(8,128)} %constant.129.clone.turns) | copy-start | bytes 393220
  118.7 15.5 %all-to-all-start.2 = ((bf16[16,4,8,128]{3,2,1,0:T(8,128)(2,1)}), bf16[16,4,8,128]{3,2,1,0:T(8,128)(2,1)}, u32[]{:S(2)}, u32[]{:S(2)}) async-start(bf16[16,4,8,128]{3,2,1,0:T(8,128)(2,1)} %key_value.1), calls=%async_computation.2 | async-start | bytes 262144 | tf_op jit(solution)/shard_map/all_to_all | solution.py:25
  127.4 1.1 copy-start.1
  128.6 5.7 %copy-start.9 = (f32[8]{0:T(128)S(1)}, f32[8]{0:T(128)}, u32[]{:S(2)}) copy-start(f32[8]{0:T(128)} %skip.1) | copy-start | bytes 100
  137.7 31.1 %all-to-all-start.3 = ((bf16[64,8,128]{2,1,0:T(8,128)(2,1)}), bf16[64,8,128]{2,1,0:T(8,128)(2,1)S(1)}, u32[]{:S(2)}, u32[]{:S(2)}) async-start(bf16[64,8,128]{2,1,0:T(8,128)(2,1)} %long_conv.1), calls=%async_computation.3 | async-start | bytes 262144 | tf_op jit(solution)/shard_map/all_to_all | solution.py:25
  147.1 13.1 %collective-permute-start.11 = (bf16[128,128]{1,0:T(8,128)(2,1)S(1)}, bf16[128,128]{1,0:T(8,128)(2,1)S(1)}, u32[]{:S(2)}, u32[]{:S(2)}) collective-permute-start(bf16[128,128]{1,0:T(8,128)(2,1)S(1)} %get-tuple-element.9), channel_id=1, source_target_pairs={{0,8},{8,0},{256,264},{264,256},{1,9},{9,1},{257,265},{265,257},{2... | collective-permute-start | bytes 98312 | tf_op jit(solution)/shard_map/ppermute | solution.py:194
  150.5 9.8 %collective-permute-start.12 = (bf16[128,128]{1,0:T(8,128)(2,1)S(1)}, bf16[128,128]{1,0:T(8,128)(2,1)S(1)}, u32[]{:S(2)}, u32[]{:S(2)}) collective-permute-start(bf16[128,128]{1,0:T(8,128)(2,1)S(1)} %get-tuple-element.8), channel_id=1, source_target_pairs={{0,256},{8,264},{256,0},{264,8},{1,257},{9,265},{257,1},{265,9},{2... | collective-permute-start | bytes 98312 | tf_op jit(solution)/shard_map/ppermute | solution.py:194
  158.0 10.8 %collective-permute-start.13 = (bf16[128,128]{1,0:T(8,128)(2,1)S(1)}, bf16[128,128]{1,0:T(8,128)(2,1)S(1)}, u32[]{:S(2)}, u32[]{:S(2)}) collective-permute-start(bf16[128,128]{1,0:T(8,128)(2,1)S(1)} %get-tuple-element.7), channel_id=1, source_target_pairs={{0,264},{8,256},{256,8},{264,0},{1,265},{9,257},{257,9},{265,1},{2... | collective-permute-start | bytes 98312 | tf_op jit(solution)/shard_map/ppermute | solution.py:194
  (6 other events, 5.5 us)

commit v3 on v2

--- a/solution.py
+++ b/solution.py
@@ -177,7 +177,7 @@
         in_specs=specs,
         out_specs=whole,
         scratch_shapes=list(scratch),
-        compiler_params=pltpu.CompilerParams(vmem_limit_bytes=48 * 2**20),
+        compiler_params=pltpu.CompilerParams(vmem_limit_bytes=20 * 2**20),
         cost_estimate=pl.CostEstimate(flops=flops, bytes_accessed=moved, transcendentals=0),
         name=name,
     )(*args)
@@ -194,6 +194,13 @@
     return lax.ppermute(value, axes, [(i, i ^ bits) for i in range(count)])
 
 
+def both_halves(blocks, yl):
+    other = swapped(blocks, ("yl",), 1)
+    first = yl == 0
+    halves = [jnp.where(first, blocks, other), jnp.where(first, other, blocks)]
+    return jnp.concatenate(halves, axis=1)
+
+
 def local(tokens, w_query, w_key, w_value, short_taps, filters, skip_gain):
     place = lax.axis_index(AXES)
     core, z_lo, yl, z_hi = place % 2, place // 2 % 4, place // 8 % 2, place // 256
@@ -201,20 +208,16 @@
 
     sent = call(weights_kernel, (2, 4, 2, 64, 384), BF16, (w_key, w_value, w_query), name="sort_weights")
     first = exchanged(sent.reshape(16, 64, 384), ("z_hi", "yh", "yl"))
-    weights = from_everyone(first, ("x",)).reshape(4, 2, 8, 64, 384)
 
     halo = shifted(tokens[-HALO:], TOK, -1, wrap=False)
     mine = jnp.concatenate([halo, tokens], axis=0)
-    other = swapped(mine, ("yl",), 1)
-    first_half = yl == 0
-    pair = jnp.concatenate(
-        [jnp.where(first_half, mine, other), jnp.where(first_half, other, mine)], axis=0
-    )
     ring = ("z_hi", "z_lo")
-    ahead, behind = shifted(pair, ring, 2), shifted(pair, ring, -2)
-    near = jnp.stack([pair, shifted(pair, ring, 1), shifted(pair, ring, -1), ahead, behind])
+    ahead, behind = shifted(mine, ring, 2), shifted(mine, ring, -2)
+    near = both_halves(jnp.stack([mine, shifted(mine, ring, 1), shifted(mine, ring, -1), ahead, behind]), yl)
     near_other = swapped(near, ("core",), 1)
-    far = jnp.stack([shifted(ahead, ring, 1), shifted(behind, ring, -1), shifted(ahead, ring, 2)])
+    far = both_halves(
+        jnp.stack([shifted(ahead, ring, 1), shifted(behind, ring, -1), shifted(ahead, ring, 2)]), yl
+    )
     far_other = swapped(far, ("core",), 1)
 
     taps = short_taps.reshape(3, 3, 2, 16, 2, 8)
@@ -231,6 +234,9 @@
         name="filter_spectrum",
     )
 
+    first, spec, taps = lax.optimization_barrier((first, spec, taps))
+    weights = from_everyone(first, ("x",)).reshape(4, 2, 8, 64, 384)
+
     whole = pl.BlockSpec(memory_space=pltpu.VMEM)
     smem = pl.BlockSpec(memory_space=pltpu.SMEM)
     features = (where, near, far, near_other, far_other, weights, taps)
@@ -256,6 +262,7 @@
         name="query",
     )
     queries = [query] + [swapped(query[bits], ("z_hi", "yl"), bits) for bits in (1, 2, 3)]
+    owned, *queries = lax.optimization_barrier((owned, *queries))
     mixed = call(
         conv_kernel,
         (64, 8, BLOCK),

time: 172 us -> 174 us (1.012)
  waiting for transfers between devices: 57.9 us -> 31 us
  blocking collectives: 0 us -> 26.4 us
  other arithmetic: 0.23 us -> 5.92 us
  starting transfers between devices: 87.4 us -> 81.9 us
  local copies, waits for them, and re-layouts: 9.02 us -> 12.9 us
    all_to_all x0 -> x1, blocking collectives: none -> 26.4 us  [exchanged(): return lax.all_to_all(value, axes, split_axis=0, concat_axis=0, tiled=True)]
    ppermute x8, waiting for transfers between devices: 41.6 us -> 21.3 us  [shifted(): lax.ppermute(value, axes, [(source % count, i) for source, i in pairs])]
    all_to_all x4 -> x3, starting transfers between devices: 38.8 us -> 28.7 us  [exchanged(): return lax.all_to_all(value, axes, split_axis=0, concat_axis=0, tiled=True)]
    ppermute x6 -> x7, waiting for transfers between devices: 14.7 us -> 9.68 us  [swapped(): return lax.ppermute(value, axes, [(i, i ^ bits) for i in range(count)])]
    ppermute x6 -> x7, starting transfers between devices: 19 us -> 23 us  [swapped(): return lax.ppermute(value, axes, [(i, i ^ bits) for i in range(count)])]
    unnamed x28 -> x33, local copies, waits for them, and re-layouts: 5.98 us -> 8.49 us
    select_n x1 -> x2, other arithmetic: 0.02 us -> 2.52 us  [both_halves(): halves = [jnp.where(first, blocks, other), jnp.where(first, other, blocks)]]
    concatenate x1 -> x2, other arithmetic: 0.02 us -> 2.23 us  [both_halves(): return jnp.concatenate(halves, axis=1)]
  transfers between devices with their start and end apart: 18 -> 18, of which waited for: 9 -> 8; matrix products, arithmetic and copies ran while one was open for 2% -> 7% of each run, Pallas kernels for 3% -> 3%
where the time goes in v3:
time: 174 us; the launch traced here: 173 us
  starting transfers between devices  81.9 us (47%)
  waiting for transfers between devices  31 us (18%)
  blocking collectives  26.4 us (15%)
  Pallas kernels  13.9 us (8%)
  local copies, waits for them, and re-layouts  12.9 us (7%)
  other arithmetic  5.92 us (3%)
    ppermute x8, starting transfers between devices, shifted(): lax.ppermute(value, axes, [(source % count, i) for source, i in pairs])  30.2 us
    all_to_all x3, starting transfers between devices, exchanged(): return lax.all_to_all(value, axes, split_axis=0, concat_axis=0, tiled=True)  28.7 us
    all_to_all x1, blocking collectives, exchanged(): return lax.all_to_all(value, axes, split_axis=0, concat_axis=0, tiled=True)  26.4 us
    ppermute x7, starting transfers between devices, swapped(): return lax.ppermute(value, axes, [(i, i ^ bits) for i in range(count)])  23 us
    ppermute x8, waiting for transfers between devices, shifted(): lax.ppermute(value, axes, [(source % count, i) for source, i in pairs])  21.3 us
    pallas_call x6, Pallas kernels, call(): pl.pallas_call(kernel, out_shape=jax.ShapeDtypeStruct(shape, dtype), in_s...  13.9 us
    ppermute x7, waiting for transfers between devices, swapped(): return lax.ppermute(value, axes, [(i, i ^ bits) for i in range(count)])  9.68 us
    unnamed x33, local copies, waits for them, and re-layouts  8.49 us
  transfers between devices with their start and end apart: 18, of which 8 were waited for; matrix products, arithmetic and copies ran while one was open for 7% of the time, Pallas kernels for 3%

profile of v3, /device:TPU:6, one launch (start us, length us, event | category | flops | bytes accessed | tf_op | source)
XLA Modules:
  0.0 172.5 jit_solution(12143910367501459155)
XLA Ops:
  0.7 3.5 %collective-permute-start = (bf16[8,512]{1,0:T(8,128)(2,1)S(1)}, bf16[8,512]{1,0:T(8,128)(2,1)S(1)}, u32[]{:S(2)}, u32[]{:S(2)}) collective-permute-start(bf16[8,512]{1,0:T(8,128)(2,1)S(1)} %slice.12), channel_id=1, source_target_pairs={{0,8},{8,16},{16,24},{24,32},{32,40},{40,48},{48,56},{56,64},{64,7... | collective-permute-start | bytes 24584 | tf_op jit(solution)/shard_map/ppermute | solution.py:189
  8.0 14.9 %all-to-all-start = ((bf16[16,64,384]{2,1,0:T(8,128)(2,1)}), bf16[16,64,384]{2,1,0:T(8,128)(2,1)S(1)}, u32[]{:S(2)}, u32[]{:S(2)}) async-start(bf16[16,64,384]{2,1,0:T(8,128)(2,1)} %bitcast.11), calls=%async_computation | async-start | bytes 1572864 | tf_op jit(solution)/shard_map/all_to_all | solution.py:25
  23.0 4.3 %collective-permute-start.4 = (bf16[136,512]{1,0:T(8,128)(2,1)S(1)}, bf16[136,512]{1,0:T(8,128)(2,1)S(1)}, u32[]{:S(2)}, u32[]{:S(2)}) collective-permute-start(bf16[136,512]{1,0:T(8,128)(2,1)S(1)} %constant_dynamic-update-slice_fusion), channel_id=1, source_target_pairs={{260,0},{262,2},{0,4},{2,6},{4,256},{6,258},{256,260},{258,262},{2... | collective-permute-start | bytes 417800 | tf_op jit(solution)/shard_map/ppermute | solution.py:189
  27.2 5.4 %collective-permute-start.3 = (bf16[136,512]{1,0:T(8,128)(2,1)S(1)}, bf16[136,512]{1,0:T(8,128)(2,1)S(1)}, u32[]{:S(2)}, u32[]{:S(2)}) collective-permute-start(bf16[136,512]{1,0:T(8,128)(2,1)S(1)} %constant_dynamic-update-slice_fusion), channel_id=1, source_target_pairs={{4,0},{6,2},{256,4},{258,6},{260,256},{262,258},{0,260},{2,262},{5... | collective-permute-start | bytes 417800 | tf_op jit(solution)/shard_map/ppermute | solution.py:189
  32.6 3.4 %collective-permute-start.2 = (bf16[136,512]{1,0:T(8,128)(2,1)S(1)}, bf16[136,512]{1,0:T(8,128)(2,1)S(1)}, u32[]{:S(2)}, u32[]{:S(2)}) collective-permute-start(bf16[136,512]{1,0:T(8,128)(2,1)S(1)} %constant_dynamic-update-slice_fusion), channel_id=1, source_target_pairs={{262,0},{0,2},{2,4},{4,6},{6,256},{256,258},{258,260},{260,262},{2... | collective-permute-start | bytes 417800 | tf_op jit(solution)/shard_map/ppermute | solution.py:189
  36.0 3.7 %collective-permute-start.1 = (bf16[136,512]{1,0:T(8,128)(2,1)S(1)}, bf16[136,512]{1,0:T(8,128)(2,1)S(1)}, u32[]{:S(2)}, u32[]{:S(2)}) collective-permute-start(bf16[136,512]{1,0:T(8,128)(2,1)S(1)} %constant_dynamic-update-slice_fusion), channel_id=1, source_target_pairs={{2,0},{4,2},{6,4},{256,6},{258,256},{260,258},{262,260},{0,262},{3... | collective-permute-start | bytes 417800 | tf_op jit(solution)/shard_map/ppermute | solution.py:189
  40.4 11.8 %collective-permute-done.1 = bf16[136,512]{1,0:T(8,128)(2,1)S(1)} collective-permute-done((bf16[136,512]{1,0:T(8,128)(2,1)S(1)}, bf16[136,512]{1,0:T(8,128)(2,1)S(1)}, u32[]{:S(2)}, u32[]{:S(2)}) %collective-permute-start.1) | collective-permute-done | bytes 139296 | tf_op jit(solution)/shard_map/ppermute | solution.py:189
  57.3 3.4 %collective-permute-start.5 = (bf16[5,136,512]{2,1,0:T(8,128)(2,1)}, bf16[5,136,512]{2,1,0:T(8,128)(2,1)}, u32[]{:S(2)}, u32[]{:S(2)}) collective-permute-start(bf16[5,136,512]{2,1,0:T(8,128)(2,1)} %bitcast_dynamic-update-slice_fusion), channel_id=1, source_target_pairs={{0,8},{8,0},{1,9},{9,1},{2,10},{10,2},{3,11},{11,3},{4,12},{12,4},... | collective-permute-start | bytes 2088968 | tf_op jit(solution)/shard_map/ppermute | solution.py:194
  65.5 4.8 %all-to-all-start.1 = ((bf16[4,16,64,384]{3,2,1,0:T(8,128)(2,1)}), bf16[4,16,64,384]{3,2,1,0:T(8,128)(2,1)S(1)}, u32[]{:S(2)}, u32[]{:S(2)}) async-start(bf16[4,16,64,384]{3,2,1,0:T(8,128)(2,1)} %broadcast_in_dim.3), calls=%async_computation.1 | async-start | bytes 6291456 | tf_op jit(solution)/shard_map/all_to_all | solution.py:25
  70.3 3.1 %collective-permute-start.7 = (bf16[136,512]{1,0:T(8,128)(2,1)}, bf16[136,512]{1,0:T(8,128)(2,1)}, u32[]{:S(2)}, u32[]{:S(2)}) collective-permute-start(bf16[136,512]{1,0:T(8,128)(2,1)} %copy-done.12), channel_id=1, source_target_pairs={{262,0},{0,2},{2,4},{4,6},{6,256},{256,258},{258,260},{260,262},{2... | collective-permute-start | bytes 417800 | tf_op jit(solution)/shard_map/ppermute | solution.py:189
  73.4 3.5 %collective-permute-start.8 = (bf16[136,512]{1,0:T(8,128)(2,1)}, bf16[136,512]{1,0:T(8,128)(2,1)}, u32[]{:S(2)}, u32[]{:S(2)}) collective-permute-start(bf16[136,512]{1,0:T(8,128)(2,1)} %copy-done.11), channel_id=1, source_target_pairs={{4,0},{6,2},{256,4},{258,6},{260,256},{262,258},{0,260},{2,262},{5... | collective-permute-start | bytes 417800 | tf_op jit(solution)/shard_map/ppermute | solution.py:189
  76.9 3.4 %collective-permute-start.6 = (bf16[136,512]{1,0:T(8,128)(2,1)}, bf16[136,512]{1,0:T(8,128)(2,1)}, u32[]{:S(2)}, u32[]{:S(2)}) collective-permute-start(bf16[136,512]{1,0:T(8,128)(2,1)} %copy-done.11), channel_id=1, source_target_pairs={{2,0},{4,2},{6,4},{256,6},{258,256},{260,258},{262,260},{0,262},{3... | collective-permute-start | bytes 417800 | tf_op jit(solution)/shard_map/ppermute | solution.py:189
  80.4 4.5 %collective-permute-done.8 = bf16[136,512]{1,0:T(8,128)(2,1)} collective-permute-done((bf16[136,512]{1,0:T(8,128)(2,1)}, bf16[136,512]{1,0:T(8,128)(2,1)}, u32[]{:S(2)}, u32[]{:S(2)}) %collective-permute-start.8) | collective-permute-done | bytes 139296 | tf_op jit(solution)/shard_map/ppermute | solution.py:189
  84.9 2.6 %collective-permute-done.6 = bf16[136,512]{1,0:T(8,128)(2,1)} collective-permute-done((bf16[136,512]{1,0:T(8,128)(2,1)}, bf16[136,512]{1,0:T(8,128)(2,1)}, u32[]{:S(2)}, u32[]{:S(2)}) %collective-permute-start.6) | collective-permute-done | bytes 139296 | tf_op jit(solution)/shard_map/ppermute | solution.py:189
  88.6 2.7 %collective-permute-start.9 = (bf16[3,136,512]{2,1,0:T(8,128)(2,1)S(1)}, bf16[3,136,512]{2,1,0:T(8,128)(2,1)S(1)}, u32[]{:S(2)}, u32[]{:S(2)}) collective-permute-start(bf16[3,136,512]{2,1,0:T(8,128)(2,1)S(1)} %pad_maximum_fusion.2), channel_id=1, source_target_pairs={{0,8},{8,0},{1,9},{9,1},{2,10},{10,2},{3,11},{11,3},{4,12},{12,4},... | collective-permute-start | bytes 1253384 | tf_op jit(solution)/shard_map/ppermute | solution.py:194
  95.8 4.5 %collective-permute-done.9 = bf16[3,136,512]{2,1,0:T(8,128)(2,1)S(1)} collective-permute-done((bf16[3,136,512]{2,1,0:T(8,128)(2,1)S(1)}, bf16[3,136,512]{2,1,0:T(8,128)(2,1)S(1)}, u32[]{:S(2)}, u32[]{:S(2)}) %collective-permute-start.9) | collective-permute-done | bytes 417824 | tf_op jit(solution)/shard_map/ppermute | solution.py:194
  104.5 2.5 %collective-permute-done.11.far_other = bf16[3,272,512]{2,1,0:T(8,128)(2,1)} collective-permute-done((bf16[3,272,512]{2,1,0:T(8,128)(2,1)}, bf16[3,272,512]{2,1,0:T(8,128)(2,1)}, u32[]{:S(2)}, u32[]{:S(2)}) %collective-permute-start.11) | collective-permute-done | bytes 835616 | tf_op jit(solution)/shard_map/ppermute | solution.py:194
  107.1 4.9 %key_value.1 = bf16[16,4,8,128]{3,2,1,0:T(8,128)(2,1)} custom-call(s32[3]{0:T(128)S(1)} %pad_add_fusion.where, bf16[5,272,512]{2,1,0:T(8,128)(2,1)} %pad_maximum_fusion.near, bf16[3,272,512]{2,1,0:T(8,128)(2,1)} %pad_maximum_fusion.1.far, bf16[5,272,512]{2,1,0:T(8,128)(2,1)} %collective-permute-done.10.near_other, ...), custom_call_target="tpu_custom_call" | custom-call | flops 1140850688 | bytes 7606796 | tf_op jit(solution)/shard_map/key_value/pallas_call | solution.py:174
  112.0 9.1 %all-to-all-start.2 = ((bf16[16,4,8,128]{3,2,1,0:T(8,128)(2,1)}), bf16[16,4,8,128]{3,2,1,0:T(8,128)(2,1)S(1)}, u32[]{:S(2)}, u32[]{:S(2)}) async-start(bf16[16,4,8,128]{3,2,1,0:T(8,128)(2,1)} %key_value.1), calls=%async_computation.2 | async-start | bytes 262144 | tf_op jit(solution)/shard_map/all_to_all | solution.py:25
  121.0 3.9 %query.1.q0 = bf16[4,128,128]{2,1,0:T(8,128)(2,1)S(1)} custom-call(s32[3]{0:T(128)S(1)} %pad_add_fusion.where, bf16[5,272,512]{2,1,0:T(8,128)(2,1)} %pad_maximum_fusion.near, bf16[3,272,512]{2,1,0:T(8,128)(2,1)} %pad_maximum_fusion.1.far, bf16[5,272,512]{2,1,0:T(8,128)(2,1)} %collective-permute-done.10.near_other, ...), custom_call_target="tpu_custom_call" | custom-call | flops 570425344 | bytes 7606796 | tf_op jit(solution)/shard_map/query/pallas_call | solution.py:174
  125.0 5.1 %collective-permute-start.14 = (bf16[128,128]{1,0:T(8,128)(2,1)S(1)}, bf16[128,128]{1,0:T(8,128)(2,1)S(1)}, u32[]{:S(2)}, u32[]{:S(2)}) collective-permute-start(bf16[128,128]{1,0:T(8,128)(2,1)S(1)} %get-tuple-element.25), channel_id=1, source_target_pairs={{0,264},{8,256},{256,8},{264,0},{1,265},{9,257},{257,9},{265,1},{2... | collective-permute-start | bytes 98312 | tf_op jit(solution)/shard_map/ppermute | solution.py:194
  130.1 4.8 %collective-permute-start.13 = (bf16[128,128]{1,0:T(8,128)(2,1)S(1)}, bf16[128,128]{1,0:T(8,128)(2,1)S(1)}, u32[]{:S(2)}, u32[]{:S(2)}) collective-permute-start(bf16[128,128]{1,0:T(8,128)(2,1)S(1)} %get-tuple-element.26), channel_id=1, source_target_pairs={{0,256},{8,264},{256,0},{264,8},{1,257},{9,265},{257,1},{265,9},{2... | collective-permute-start | bytes 98312 | tf_op jit(solution)/shard_map/ppermute | solution.py:194
  134.9 3.2 %collective-permute-start.12 = (bf16[128,128]{1,0:T(8,128)(2,1)S(1)}, bf16[128,128]{1,0:T(8,128)(2,1)S(1)}, u32[]{:S(2)}, u32[]{:S(2)}) collective-permute-start(bf16[128,128]{1,0:T(8,128)(2,1)S(1)} %get-tuple-element.27), channel_id=1, source_target_pairs={{0,8},{8,0},{256,264},{264,256},{1,9},{9,1},{257,265},{265,257},{2... | collective-permute-start | bytes 98312 | tf_op jit(solution)/shard_map/ppermute | solution.py:194
  144.4 26.4 %all_to_all.20.returned = bf16[64,8,128]{2,1,0:T(8,128)(2,1)S(1)} all-to-all(bf16[64,8,128]{2,1,0:T(8,128)(2,1)S(1)} %long_conv.1), channel_id=1, replica_groups=mesh['z_hi'=2,'x'=4,'yh'=4,'yl'=2,'z_lo'=4,'core'=2] {'z_hi','x','yh','yl'}, dimensions={0} | all-to-all | bytes 262144 | tf_op jit(solution)/shard_map/all_to_all | solution.py:25
  (66 shorter events, 32.8 us)
Async XLA Ops:
  0.7 22.2 %collective-permute-start = (bf16[8,512]{1,0:T(8,128)(2,1)S(1)}, bf16[8,512]{1,0:T(8,128)(2,1)S(1)}, u32[]{:S(2)}, u32[]{:S(2)}) collective-permute-start(bf16[8,512]{1,0:T(8,128)(2,1)S(1)} %slice.12), channel_id=1, source_target_pairs={{0,8},{8,16},{16,24},{24,32},{32,40},{40,48},{48,56},{56,64},{64,7... | collective-permute-start | bytes 24584 | tf_op jit(solution)/shard_map/ppermute | solution.py:189
  6.7 16.2 %copy-start.10 = (bf16[128,512]{1,0:T(8,128)(2,1)S(1)}, bf16[128,512]{1,0:T(8,128)(2,1)}, u32[]{:S(2)}) copy-start(bf16[128,512]{1,0:T(8,128)(2,1)} %param.9) | copy-start | bytes 393220
  8.0 52.8 %copy-start.13 = (f32[3,3,512]{2,1,0:T(4,128)S(1)}, f32[3,3,512]{2,1,0:T(4,128)}, u32[]{:S(2)}) copy-start(f32[3,3,512]{2,1,0:T(4,128)} %param.13) | copy-start | bytes 55300
  8.0 53.6 %copy-start.2 = (bf16[832,256]{1,0:T(8,128)(2,1)S(1)}, bf16[832,256]{1,0:T(8,128)(2,1)}, u32[]{:S(2)}) copy-start(bf16[832,256]{1,0:T(8,128)(2,1)} %constant.132.tables) | copy-start | bytes 1277956
  8.0 53.6 %copy-start.4 = (f32[256,128]{1,0:T(8,128)S(1)}, f32[256,128]{1,0:T(8,128)}, u32[]{:S(2)}) copy-start(f32[256,128]{1,0:T(8,128)} %constant.129.clone.turns) | copy-start | bytes 393220
  8.0 53.6 %copy-start.5 = (f32[8,8192]{1,0:T(8,128)S(1)}, f32[8,8192]{1,0:T(8,128)}, u32[]{:S(2)}) copy-start(f32[8,8192]{1,0:T(8,128)} %filters.1) | copy-start | bytes 786436
  8.0 55.4 %all-to-all-start = ((bf16[16,64,384]{2,1,0:T(8,128)(2,1)}), bf16[16,64,384]{2,1,0:T(8,128)(2,1)S(1)}, u32[]{:S(2)}, u32[]{:S(2)}) async-start(bf16[16,64,384]{2,1,0:T(8,128)(2,1)} %bitcast.11), calls=%async_computation | async-start | bytes 1572864 | tf_op jit(solution)/shard_map/all_to_all | solution.py:25
  23.0 33.7 %collective-permute-start.4 = (bf16[136,512]{1,0:T(8,128)(2,1)S(1)}, bf16[136,512]{1,0:T(8,128)(2,1)S(1)}, u32[]{:S(2)}, u32[]{:S(2)}) collective-permute-start(bf16[136,512]{1,0:T(8,128)(2,1)S(1)} %constant_dynamic-update-slice_fusion), channel_id=1, source_target_pairs={{260,0},{262,2},{0,4},{2,6},{4,256},{6,258},{256,260},{258,262},{2... | collective-permute-start | bytes 417800 | tf_op jit(solution)/shard_map/ppermute | solution.py:189
  27.2 28.7 %collective-permute-start.3 = (bf16[136,512]{1,0:T(8,128)(2,1)S(1)}, bf16[136,512]{1,0:T(8,128)(2,1)S(1)}, u32[]{:S(2)}, u32[]{:S(2)}) collective-permute-start(bf16[136,512]{1,0:T(8,128)(2,1)S(1)} %constant_dynamic-update-slice_fusion), channel_id=1, source_target_pairs={{4,0},{6,2},{256,4},{258,6},{260,256},{262,258},{0,260},{2,262},{5... | collective-permute-start | bytes 417800 | tf_op jit(solution)/shard_map/ppermute | solution.py:189
  32.6 22.6 %collective-permute-start.2 = (bf16[136,512]{1,0:T(8,128)(2,1)S(1)}, bf16[136,512]{1,0:T(8,128)(2,1)S(1)}, u32[]{:S(2)}, u32[]{:S(2)}) collective-permute-start(bf16[136,512]{1,0:T(8,128)(2,1)S(1)} %constant_dynamic-update-slice_fusion), channel_id=1, source_target_pairs={{262,0},{0,2},{2,4},{4,6},{6,256},{256,258},{258,260},{260,262},{2... | collective-permute-start | bytes 417800 | tf_op jit(solution)/shard_map/ppermute | solution.py:189
  36.0 16.1 %collective-permute-start.1 = (bf16[136,512]{1,0:T(8,128)(2,1)S(1)}, bf16[136,512]{1,0:T(8,128)(2,1)S(1)}, u32[]{:S(2)}, u32[]{:S(2)}) collective-permute-start(bf16[136,512]{1,0:T(8,128)(2,1)S(1)} %constant_dynamic-update-slice_fusion), channel_id=1, source_target_pairs={{2,0},{4,2},{6,4},{256,6},{258,256},{260,258},{262,260},{0,262},{3... | collective-permute-start | bytes 417800 | tf_op jit(solution)/shard_map/ppermute | solution.py:189
  57.3 33.9 %collective-permute-start.5 = (bf16[5,136,512]{2,1,0:T(8,128)(2,1)}, bf16[5,136,512]{2,1,0:T(8,128)(2,1)}, u32[]{:S(2)}, u32[]{:S(2)}) collective-permute-start(bf16[5,136,512]{2,1,0:T(8,128)(2,1)} %bitcast_dynamic-update-slice_fusion), channel_id=1, source_target_pairs={{0,8},{8,0},{1,9},{9,1},{2,10},{10,2},{3,11},{11,3},{4,12},{12,4},... | collective-permute-start | bytes 2088968 | tf_op jit(solution)/shard_map/ppermute | solution.py:194
  65.5 41.6 %all-to-all-start.1 = ((bf16[4,16,64,384]{3,2,1,0:T(8,128)(2,1)}), bf16[4,16,64,384]{3,2,1,0:T(8,128)(2,1)S(1)}, u32[]{:S(2)}, u32[]{:S(2)}) async-start(bf16[4,16,64,384]{3,2,1,0:T(8,128)(2,1)} %broadcast_in_dim.3), calls=%async_computation.1 | async-start | bytes 6291456 | tf_op jit(solution)/shard_map/all_to_all | solution.py:25
  70.3 10.1 %collective-permute-start.7 = (bf16[136,512]{1,0:T(8,128)(2,1)}, bf16[136,512]{1,0:T(8,128)(2,1)}, u32[]{:S(2)}, u32[]{:S(2)}) collective-permute-start(bf16[136,512]{1,0:T(8,128)(2,1)} %copy-done.12), channel_id=1, source_target_pairs={{262,0},{0,2},{2,4},{4,6},{6,256},{256,258},{258,260},{260,262},{2... | collective-permute-start | bytes 417800 | tf_op jit(solution)/shard_map/ppermute | solution.py:189
  73.4 11.5 %collective-permute-start.8 = (bf16[136,512]{1,0:T(8,128)(2,1)}, bf16[136,512]{1,0:T(8,128)(2,1)}, u32[]{:S(2)}, u32[]{:S(2)}) collective-permute-start(bf16[136,512]{1,0:T(8,128)(2,1)} %copy-done.11), channel_id=1, source_target_pairs={{4,0},{6,2},{256,4},{258,6},{260,256},{262,258},{0,260},{2,262},{5... | collective-permute-start | bytes 417800 | tf_op jit(solution)/shard_map/ppermute | solution.py:189
  76.9 10.6 %collective-permute-start.6 = (bf16[136,512]{1,0:T(8,128)(2,1)}, bf16[136,512]{1,0:T(8,128)(2,1)}, u32[]{:S(2)}, u32[]{:S(2)}) collective-permute-start(bf16[136,512]{1,0:T(8,128)(2,1)} %copy-done.11), channel_id=1, source_target_pairs={{2,0},{4,2},{6,4},{256,6},{258,256},{260,258},{262,260},{0,262},{3... | collective-permute-start | bytes 417800 | tf_op jit(solution)/shard_map/ppermute | solution.py:189
  88.6 11.8 %collective-permute-start.9 = (bf16[3,136,512]{2,1,0:T(8,128)(2,1)S(1)}, bf16[3,136,512]{2,1,0:T(8,128)(2,1)S(1)}, u32[]{:S(2)}, u32[]{:S(2)}) collective-permute-start(bf16[3,136,512]{2,1,0:T(8,128)(2,1)S(1)} %pad_maximum_fusion.2), channel_id=1, source_target_pairs={{0,8},{8,0},{1,9},{9,1},{2,10},{10,2},{3,11},{11,3},{4,12},{12,4},... | collective-permute-start | bytes 1253384 | tf_op jit(solution)/shard_map/ppermute | solution.py:194
  93.9 13.2 %collective-permute-start.10 = (bf16[5,272,512]{2,1,0:T(8,128)(2,1)}, bf16[5,272,512]{2,1,0:T(8,128)(2,1)}, u32[]{:S(2)}, u32[]{:S(2)}) collective-permute-start(bf16[5,272,512]{2,1,0:T(8,128)(2,1)} %pad_maximum_fusion.near), channel_id=1, source_target_pairs={{0,1},{1,0},{2,3},{3,2},{4,5},{5,4},{6,7},{7,6},{8,9},{9,8},{10,11... | collective-permute-start | bytes 4177928 | tf_op jit(solution)/shard_map/ppermute | solution.py:194
  102.5 4.6 %collective-permute-start.11 = (bf16[3,272,512]{2,1,0:T(8,128)(2,1)}, bf16[3,272,512]{2,1,0:T(8,128)(2,1)}, u32[]{:S(2)}, u32[]{:S(2)}) collective-permute-start(bf16[3,272,512]{2,1,0:T(8,128)(2,1)} %pad_maximum_fusion.1.far), channel_id=1, source_target_pairs={{0,1},{1,0},{2,3},{3,2},{4,5},{5,4},{6,7},{7,6},{8,9},{9,8},{10,11... | collective-permute-start | bytes 2506760 | tf_op jit(solution)/shard_map/ppermute | solution.py:194
  112.0 28.8 %all-to-all-start.2 = ((bf16[16,4,8,128]{3,2,1,0:T(8,128)(2,1)}), bf16[16,4,8,128]{3,2,1,0:T(8,128)(2,1)S(1)}, u32[]{:S(2)}, u32[]{:S(2)}) async-start(bf16[16,4,8,128]{3,2,1,0:T(8,128)(2,1)} %key_value.1), calls=%async_computation.2 | async-start | bytes 262144 | tf_op jit(solution)/shard_map/all_to_all | solution.py:25
  121.0 19.7 %copy-start.9 = (f32[8]{0:T(128)S(1)}, f32[8]{0:T(128)}, u32[]{:S(2)}) copy-start(f32[8]{0:T(128)} %skip.1) | copy-start | bytes 100
  125.0 13.1 %collective-permute-start.14 = (bf16[128,128]{1,0:T(8,128)(2,1)S(1)}, bf16[128,128]{1,0:T(8,128)(2,1)S(1)}, u32[]{:S(2)}, u32[]{:S(2)}) collective-permute-start(bf16[128,128]{1,0:T(8,128)(2,1)S(1)} %get-tuple-element.25), channel_id=1, source_target_pairs={{0,264},{8,256},{256,8},{264,0},{1,265},{9,257},{257,9},{265,1},{2... | collective-permute-start | bytes 98312 | tf_op jit(solution)/shard_map/ppermute | solution.py:194
  130.1 10.0 %collective-permute-start.13 = (bf16[128,128]{1,0:T(8,128)(2,1)S(1)}, bf16[128,128]{1,0:T(8,128)(2,1)S(1)}, u32[]{:S(2)}, u32[]{:S(2)}) collective-permute-start(bf16[128,128]{1,0:T(8,128)(2,1)S(1)} %get-tuple-element.26), channel_id=1, source_target_pairs={{0,256},{8,264},{256,0},{264,8},{1,257},{9,265},{257,1},{265,9},{2... | collective-permute-start | bytes 98312 | tf_op jit(solution)/shard_map/ppermute | solution.py:194
  134.9 5.8 %collective-permute-start.12 = (bf16[128,128]{1,0:T(8,128)(2,1)S(1)}, bf16[128,128]{1,0:T(8,128)(2,1)S(1)}, u32[]{:S(2)}, u32[]{:S(2)}) collective-permute-start(bf16[128,128]{1,0:T(8,128)(2,1)S(1)} %get-tuple-element.27), channel_id=1, source_target_pairs={{0,8},{8,0},{256,264},{264,256},{1,9},{9,1},{257,265},{265,257},{2... | collective-permute-start | bytes 98312 | tf_op jit(solution)/shard_map/ppermute | solution.py:194
  (8 other events, 14.7 us)

commit v4 on v2

--- a/solution.py
+++ b/solution.py
@@ -66,7 +66,9 @@
     return dot(jnp.concatenate(turned, axis=0), tables[0:256])
 
 
-def filter_kernel(filters, tables, turns, spec, rows):
+def filter_kernel(filters, tables, turns, spec, tables_out, turns_out, rows):
+    tables_out[...] = tables[...]
+    turns_out[...] = turns[...]
     taps = filters[...]
     unit = taps / jnp.sqrt(jnp.sum(taps * taps, axis=1, keepdims=True) + 1e-06)
     for b in range(64):
@@ -114,26 +116,37 @@
         for quarter in range(4):
             piece = sorted_cols[:, quarter * 128 : (quarter + 1) * 128]
             for yh in range(4):
-                out[quarter // 2, yh, quarter % 2, :, p * 128 : (p + 1) * 128] = piece
-
-
-NEAR = (0, 1, -1, 2, -2)
-FAR = (3, -3, 4)
-
-
-def projected(where, near, far, near_other, far_other, w, at, width, acc):
+                out[quarter // 2, yh, quarter % 2, p] = piece
+
+
+def fetched(sources, held, sems):
+    copies = [pltpu.make_async_copy(a, b, sems.at[i]) for i, (a, b) in enumerate(zip(sources, held))]
+    for copy in copies:
+        copy.start()
+    return copies
+
+
+def projected(where, features, w, acc, ready):
     z, core = where[0], where[1]
-    acc[...] = jnp.zeros_like(acc)
-    for refs, steps in (((near, near_other), NEAR), ((far, far_other), FAR)):
-        for i, step in enumerate(steps):
-            source = (z + step) & 7
-            rows_at = pl.ds(pl.multiple_of((source >> 2) * 2 * ROWS, 2 * ROWS), 2 * ROWS)
-            total = acc[rows_at, :]
-            for ref, half in zip(refs, (core, 1 - core)):
-                part = (source & 3) * 2 + half
-                weights = w[part & 3, part >> 2, :, :, at : at + width].reshape(512, width)
-                total += dot(ref[i], weights)
-            acc[rows_at, :] = total
+    for i, (half, low) in enumerate((h, l) for h in range(2) for l in (0, 2, 1, 3)):
+        if i % 2 == 0:
+            for parity in range(2):
+                ready[half * 4 + parity * 2 + low % 2].wait()
+        part = ((z ^ low) & 3) * 2 + (core ^ half)
+        pieces = [
+            features[half * 4 + parity * 2 + low % 2][(low // 2) * 2 : (low // 2) * 2 + 2]
+            for parity in range(2)
+        ]
+        rows = jnp.concatenate([p.reshape(2 * ROWS, 512) for p in pieces], axis=0)
+        term = dot(rows, w(part))
+        if i == 0:
+            acc[...] = term
+        else:
+            acc[...] += term
+
+
+def group_of(where, i):
+    return ((i % 2) * 2 + i // 2) ^ where[2]
 
 
 def short(acc, group, at, taps):
@@ -146,18 +159,34 @@
     )
 
 
-def key_value_kernel(where, near, far, near_other, far_other, w, taps, out, acc):
-    projected(where, near, far, near_other, far_other, w, 0, 256, acc)
-    for group in range(4):
-        keyed = short(acc, group, 0, taps[1])
-        valued = short(acc, group, 128, taps[2])
-        out[:, group] = (keyed * valued).T.reshape(16, 8, BLOCK).astype(BF16)
-
-
-def query_kernel(where, near, far, near_other, far_other, w, taps, out, acc):
-    projected(where, near, far, near_other, far_other, w, 256, 128, acc)
-    for group in range(4):
-        out[group ^ where[2]] = short(acc, group, 0, taps[0]).astype(BF16)
+def key_value_kernel(where, *refs):
+    sources, (w, taps, out), held, (acc, sems) = refs[:8], refs[8:11], refs[11:19], refs[19:]
+    copies = fetched(sources, held, sems)
+
+    def weights(part):
+        block = w[part & 3, part >> 2]
+        return jnp.concatenate([block[:, p].reshape(512, 128) for p in range(2)], axis=1)
+
+    projected(where, held, weights, acc, copies)
+    for i in range(4):
+        keyed = short(acc, i, 0, taps[1])
+        valued = short(acc, i, 128, taps[2])
+        out[:, group_of(where, i)] = (keyed * valued).T.reshape(16, 8, BLOCK).astype(BF16)
+
+
+def query_kernel(where, *refs):
+    sources, (taps, out), held, (w, acc, sems) = refs[:12], refs[12:14], refs[14:22], refs[22:]
+    targets = [w.at[d] for d in range(4)] + list(held)
+    copies = fetched(sources[8:] + sources[:8], targets, sems)
+    for copy in copies[:4]:
+        copy.wait()
+
+    def weights(part):
+        return w[(part & 3) ^ where[3], part >> 2].reshape(512, 128)
+
+    projected(where, held, weights, acc, copies[4:])
+    for i in range(4):
+        out[(i % 2) * 2 + i // 2] = short(acc, i, 0, taps[0]).astype(BF16)
 
 
 def gate_kernel(where, q0, q1, q2, q3, returned, out):
@@ -167,26 +196,25 @@
     out[...] = (natural * mixed).astype(BF16)
 
 
-def call(kernel, shape, dtype, args, scratch=(), in_specs=None, flops=10**8, name=None):
+def call(kernel, out_shape, args, scratch=(), in_specs=None, flops=10**8, name=None):
     whole = pl.BlockSpec(memory_space=pltpu.VMEM)
     specs = in_specs or [whole] * len(args)
     moved = sum(math.prod(a.shape) * a.dtype.itemsize for a in args)
     return pl.pallas_call(
         kernel,
-        out_shape=jax.ShapeDtypeStruct(shape, dtype),
+        out_shape=out_shape,
         in_specs=specs,
-        out_specs=whole,
+        out_specs=jax.tree.map(lambda _: whole, out_shape),
         scratch_shapes=list(scratch),
-        compiler_params=pltpu.CompilerParams(vmem_limit_bytes=48 * 2**20),
+        compiler_params=pltpu.CompilerParams(vmem_limit_bytes=20 * 2**20),
         cost_estimate=pl.CostEstimate(flops=flops, bytes_accessed=moved, transcendentals=0),
         name=name,
     )(*args)
 
 
-def shifted(value, axes, step, wrap=True):
+def of_previous(value, axes):
     count = math.prod(SIZES[AXES.index(a)] for a in axes)
-    pairs = [(i + step, i) for i in range(count) if wrap or 0 <= i + step < count]
-    return lax.ppermute(value, axes, [(source % count, i) for source, i in pairs])
+    return lax.ppermute(value, axes, [(i, i + 1) for i in range(count - 1)])
 
 
 def swapped(value, axes, bits):
@@ -195,71 +223,82 @@
 
 
 def local(tokens, w_query, w_key, w_value, short_taps, filters, skip_gain):
+    shape = jax.ShapeDtypeStruct
+    whole = pl.BlockSpec(memory_space=pltpu.VMEM)
+    smem = pl.BlockSpec(memory_space=pltpu.SMEM)
     place = lax.axis_index(AXES)
-    core, z_lo, yl, z_hi = place % 2, place // 2 % 4, place // 8 % 2, place // 256
-    where = jnp.stack([z_hi * 4 + z_lo, core, z_hi * 2 + yl])
-
-    sent = call(weights_kernel, (2, 4, 2, 64, 384), BF16, (w_key, w_value, w_query), name="sort_weights")
-    first = exchanged(sent.reshape(16, 64, 384), ("z_hi", "yh", "yl"))
-    weights = from_everyone(first, ("x",)).reshape(4, 2, 8, 64, 384)
-
-    halo = shifted(tokens[-HALO:], TOK, -1, wrap=False)
-    mine = jnp.concatenate([halo, tokens], axis=0)
-    other = swapped(mine, ("yl",), 1)
-    first_half = yl == 0
-    pair = jnp.concatenate(
-        [jnp.where(first_half, mine, other), jnp.where(first_half, other, mine)], axis=0
-    )
+    core, z_lo, yl, x, z_hi = place % 2, place // 2 % 4, place // 8 % 2, place // 64 % 4, place // 256
+    where = jnp.stack([z_hi * 4 + z_lo, core, z_hi * 2 + yl, x])
+
+    halo = of_previous(tokens[-HALO:], TOK)
+    sent = call(
+        weights_kernel, shape((2, 4, 2, 3, 64, 128), BF16), (w_key, w_value, w_query), name="sort_weights"
+    )
+    sent, halo = lax.optimization_barrier((sent, halo))
+    first = exchanged(sent.reshape(16, 3, 64, 128), ("z_hi", "yh", "yl"))
+
     ring = ("z_hi", "z_lo")
-    ahead, behind = shifted(pair, ring, 2), shifted(pair, ring, -2)
-    near = jnp.stack([pair, shifted(pair, ring, 1), shifted(pair, ring, -1), ahead, behind])
-    near_other = swapped(near, ("core",), 1)
-    far = jnp.stack([shifted(ahead, ring, 1), shifted(behind, ring, -1), shifted(ahead, ring, 2)])
-    far_other = swapped(far, ("core",), 1)
+    mine = jnp.concatenate([halo, tokens], axis=0)[None]
+    two = jnp.concatenate([mine, swapped(mine, ring, 4)], axis=0)
+    even = jnp.concatenate([two, swapped(two, ring, 2)], axis=0)
+    odd = swapped(even, ring, 1)
+    even_y = swapped(even, ("yl",), 1)
+    odd_y = swapped(odd, ("yl",), 1)
+    ours = (even, odd, even_y, odd_y)
+    features = ours + tuple(swapped(v, ("core",), 1) for v in ours)
 
     taps = short_taps.reshape(3, 3, 2, 16, 2, 8)
     taps = lax.dynamic_index_in_dim(taps, z_hi, 2, keepdims=False)
     taps = lax.dynamic_index_in_dim(taps, yl, 3, keepdims=False).reshape(3, 3, 128)
 
+    first, taps, where = lax.optimization_barrier((first, taps, where))
+    weights = from_everyone(first[:, :2], ("x",)).reshape(4, 2, 8, 2, 64, 128)
+    first_query, _ = lax.optimization_barrier((first[:, 2], odd_y))
+    first_query = first_query.reshape(2, 8, 64, 128)
+    query_weights = [first_query] + [swapped(first_query, ("x",), d) for d in (1, 2, 3)]
+
+    anywhere = pl.BlockSpec(memory_space=pl.ANY)
+    kept = [pltpu.with_memory_space_constraint(v, pltpu.HBM) for v in features]
+    blocks = [pltpu.VMEM((4, ROWS, 512), BF16)] * 8
+    key_value = call(
+        key_value_kernel,
+        shape((16, 4, 8, BLOCK), BF16),
+        (where, *kept, weights, taps),
+        blocks + [pltpu.VMEM((4 * ROWS, 256), F32), pltpu.SemaphoreType.DMA((8,))],
+        in_specs=[smem] + [anywhere] * 8 + [whole] * 2,
+        flops=2 * 544 * 4096 * 256,
+        name="key_value",
+    )
+    key_value, query_weights[0] = lax.optimization_barrier((key_value, query_weights[0]))
+    owned = exchanged(key_value, ("x", "yh"))
+    query = call(
+        query_kernel,
+        shape((4, BLOCK, 128), BF16),
+        (where, *kept, *query_weights, taps),
+        blocks
+        + [
+            pltpu.VMEM((4, 2, 8, 64, 128), BF16),
+            pltpu.VMEM((4 * ROWS, 128), F32),
+            pltpu.SemaphoreType.DMA((12,)),
+        ],
+        in_specs=[smem] + [anywhere] * 12 + [whole],
+        flops=2 * 544 * 4096 * 128,
+        name="query",
+    )
     tables, turns = dft_tables()
-    spec = call(
+    filters, _ = lax.optimization_barrier((filters, key_value))
+    spec, tables, turns = call(
         filter_kernel,
-        (8 * POINTS, 2 * POINTS),
-        F32,
+        (shape((8 * POINTS, 2 * POINTS), F32), shape(tables.shape, BF16), shape(turns.shape, F32)),
         (filters, tables, turns),
         (pltpu.VMEM((512, POINTS), F32),),
         name="filter_spectrum",
     )
-
-    whole = pl.BlockSpec(memory_space=pltpu.VMEM)
-    smem = pl.BlockSpec(memory_space=pltpu.SMEM)
-    features = (where, near, far, near_other, far_other, weights, taps)
-    key_value = call(
-        key_value_kernel,
-        (16, 4, 8, BLOCK),
-        BF16,
-        features,
-        (pltpu.VMEM((4 * ROWS, 256), F32),),
-        in_specs=[smem] + [whole] * 6,
-        flops=2 * 544 * 4096 * 256,
-        name="key_value",
-    )
-    owned = exchanged(key_value, ("x", "yh"))
-    query = call(
-        query_kernel,
-        (4, BLOCK, 128),
-        BF16,
-        features,
-        (pltpu.VMEM((4 * ROWS, 128), F32),),
-        in_specs=[smem] + [whole] * 6,
-        flops=2 * 544 * 4096 * 128,
-        name="query",
-    )
     queries = [query] + [swapped(query[bits], ("z_hi", "yl"), bits) for bits in (1, 2, 3)]
+    owned, queries[1], spec = lax.optimization_barrier((owned, queries[1], spec))
     mixed = call(
         conv_kernel,
-        (64, 8, BLOCK),
-        BF16,
+        shape((64, 8, BLOCK), BF16),
         (owned.reshape(16, 2, 2, 8, BLOCK), spec, skip_gain, tables, turns),
         (pltpu.VMEM((512, POINTS), F32), pltpu.VMEM((512, POINTS), F32)),
         in_specs=[whole, whole, smem, whole, whole],
@@ -269,8 +308,7 @@
     returned = exchanged(mixed, TOK)
     return call(
         gate_kernel,
-        (BLOCK, 512),
-        BF16,
+        shape((BLOCK, 512), BF16),
         (where, *queries, returned),
         in_specs=[smem] + [whole] * 5,
         name="gate",

time: 172 us -> 179 us (1.041)
  starting transfers between devices: 87.4 us -> 96.2 us
    ppermute x6 -> x15, waiting for transfers between devices: 14.7 us -> 56.8 us  [swapped(): return lax.ppermute(value, axes, [(i, i ^ bits) for i in range(count)])]
    ppermute x8 -> x1, waiting for transfers between devices: 41.6 us -> 0.38 us  [of_previous(): return lax.ppermute(value, axes, [(i, i + 1) for i in range(count - 1)])]
    ppermute x6 -> x15, starting transfers between devices: 19 us -> 52.9 us  [swapped(): return lax.ppermute(value, axes, [(i, i ^ bits) for i in range(count)])]
    ppermute x8 -> x1, starting transfers between devices: 29.6 us -> 3.47 us  [of_previous(): return lax.ppermute(value, axes, [(i, i + 1) for i in range(count - 1)])]
    unnamed x28 -> x32, local copies, waits for them, and re-layouts: 5.98 us -> 3.38 us
  transfers between devices with their start and end apart: 18 -> 20, of which waited for: 9 -> 8; matrix products, arithmetic and copies ran while one was open for 2% -> 2% of each run, Pallas kernels for 3% -> 7%
where the time goes in v4:
time: 179 us; the launch traced here: 178 us
  starting transfers between devices  96.2 us (54%)
  waiting for transfers between devices  57.2 us (32%)
  Pallas kernels  16.1 us (9%)
  local copies, waits for them, and re-layouts  7.78 us (4%)
    ppermute x15, waiting for transfers between devices, swapped(): return lax.ppermute(value, axes, [(i, i ^ bits) for i in range(count)])  56.8 us
    ppermute x15, starting transfers between devices, swapped(): return lax.ppermute(value, axes, [(i, i ^ bits) for i in range(count)])  52.9 us
    all_to_all x4, starting transfers between devices, exchanged(): return lax.all_to_all(value, axes, split_axis=0, concat_axis=0, tiled=True)  39.9 us
    pallas_call x6, Pallas kernels, call(): pl.pallas_call(kernel, out_shape=out_shape, in_specs=specs, out_specs=jax...  16.1 us
  transfers between devices with their start and end apart: 20, of which 8 were waited for; matrix products, arithmetic and copies ran while one was open for 2% of the time, Pallas kernels for 7%

profile of v4, /device:TPU:6, one launch (start us, length us, event | category | flops | bytes accessed | tf_op | source)
XLA Modules:
  0.0 178.1 jit_solution(13750838389448118271)
XLA Ops:
  0.7 3.5 %collective-permute-start = (bf16[8,512]{1,0:T(8,128)(2,1)S(1)}, bf16[8,512]{1,0:T(8,128)(2,1)S(1)}, u32[]{:S(2)}, u32[]{:S(2)}) collective-permute-start(bf16[8,512]{1,0:T(8,128)(2,1)S(1)} %slice.18), channel_id=1, source_target_pairs={{0,8},{8,16},{16,24},{24,32},{32,40},{40,48},{48,56},{56,64},{64,7... | collective-permute-start | bytes 24584 | tf_op jit(solution)/shard_map/ppermute | solution.py:217
  8.3 14.8 %all-to-all-start = ((bf16[16,3,64,128]{3,2,1,0:T(8,128)(2,1)}), bf16[16,3,64,128]{3,2,1,0:T(8,128)(2,1)S(1)}, u32[]{:S(2)}, u32[]{:S(2)}) async-start(bf16[16,3,64,128]{3,2,1,0:T(8,128)(2,1)} %bitcast), calls=%async_computation | async-start | bytes 1572864 | tf_op jit(solution)/shard_map/all_to_all | solution.py:25
  23.1 7.7 %collective-permute-start.1 = (bf16[1,136,512]{2,1,0:T(8,128)(2,1)S(1)}, bf16[1,136,512]{2,1,0:T(8,128)(2,1)S(1)}, u32[]{:S(2)}, u32[]{:S(2)}) collective-permute-start(bf16[1,136,512]{2,1,0:T(8,128)(2,1)S(1)} %maximum_bitcast_fusion), channel_id=1, source_target_pairs={{0,256},{2,258},{4,260},{6,262},{256,0},{258,2},{260,4},{262,6},{1... | collective-permute-start | bytes 417800 | tf_op jit(solution)/shard_map/ppermute | solution.py:222
  30.9 21.3 %collective-permute-done.1 = bf16[1,136,512]{2,1,0:T(8,128)(2,1)S(1)} collective-permute-done((bf16[1,136,512]{2,1,0:T(8,128)(2,1)S(1)}, bf16[1,136,512]{2,1,0:T(8,128)(2,1)S(1)}, u32[]{:S(2)}, u32[]{:S(2)}) %collective-permute-start.1) | collective-permute-done | bytes 139296 | tf_op jit(solution)/shard_map/ppermute | solution.py:222
  52.2 4.3 %collective-permute-start.2 = (bf16[2,136,512]{2,1,0:T(8,128)(2,1)S(1)}, bf16[2,136,512]{2,1,0:T(8,128)(2,1)S(1)}, u32[]{:S(2)}, u32[]{:S(2)}) collective-permute-start(bf16[2,136,512]{2,1,0:T(8,128)(2,1)S(1)} %pad_maximum_fusion.1), channel_id=1, source_target_pairs={{0,4},{2,6},{4,0},{6,2},{256,260},{258,262},{260,256},{262,258},{1... | collective-permute-start | bytes 835592 | tf_op jit(solution)/shard_map/ppermute | solution.py:222
  57.5 10.9 %collective-permute-done.2 = bf16[2,136,512]{2,1,0:T(8,128)(2,1)S(1)} collective-permute-done((bf16[2,136,512]{2,1,0:T(8,128)(2,1)S(1)}, bf16[2,136,512]{2,1,0:T(8,128)(2,1)S(1)}, u32[]{:S(2)}, u32[]{:S(2)}) %collective-permute-start.2) | collective-permute-done | bytes 278560 | tf_op jit(solution)/shard_map/ppermute | solution.py:222
  72.4 5.4 %all-to-all-start.1 = ((bf16[4,16,2,64,128]{4,3,2,1,0:T(8,128)(2,1)}), bf16[4,16,2,64,128]{4,3,2,1,0:T(8,128)(2,1)S(1)}, u32[]{:S(2)}, u32[]{:S(2)}) async-start(bf16[4,16,2,64,128]{4,3,2,1,0:T(8,128)(2,1)} %broadcast_in_dim.7), calls=%async_computation.1 | async-start | bytes 4194304 | tf_op jit(solution)/shard_map/all_to_all | solution.py:25
  77.8 3.6 %collective-permute-start.4 = (bf16[4,136,512]{2,1,0:T(8,128)(2,1)S(1)}, bf16[4,136,512]{2,1,0:T(8,128)(2,1)S(1)}, u32[]{:S(2)}, u32[]{:S(2)}) collective-permute-start(bf16[4,136,512]{2,1,0:T(8,128)(2,1)S(1)} %pad_maximum_fusion.refs_0_), channel_id=1, source_target_pairs={{0,8},{8,0},{1,9},{9,1},{2,10},{10,2},{3,11},{11,3},{4,12},{12,4},... | collective-permute-start | bytes 1671176 | tf_op jit(solution)/shard_map/ppermute | solution.py:222
  81.4 3.7 %collective-permute-done.3.refs_1_ = bf16[4,136,512]{2,1,0:T(8,128)(2,1)} collective-permute-done((bf16[4,136,512]{2,1,0:T(8,128)(2,1)S(1)}, bf16[4,136,512]{2,1,0:T(8,128)(2,1)}, u32[]{:S(2)}, u32[]{:S(2)}) %collective-permute-start.3) | collective-permute-done | bytes 557088 | tf_op jit(solution)/shard_map/ppermute | solution.py:222
  85.0 3.8 %collective-permute-start.5 = (bf16[4,136,512]{2,1,0:T(8,128)(2,1)}, bf16[4,136,512]{2,1,0:T(8,128)(2,1)S(1)}, u32[]{:S(2)}, u32[]{:S(2)}) collective-permute-start(bf16[4,136,512]{2,1,0:T(8,128)(2,1)} %collective-permute-done.3.refs_1_), channel_id=1, source_target_pairs={{0,8},{8,0},{1,9},{9,1},{2,10},{10,2},{3,11},{11,3},{4,12},{12,4},... | collective-permute-start | bytes 1671176 | tf_op jit(solution)/shard_map/ppermute | solution.py:222
  90.8 2.4 %collective-permute-start.7 = (bf16[4,136,512]{2,1,0:T(8,128)(2,1)}, bf16[4,136,512]{2,1,0:T(8,128)(2,1)S(1)}, u32[]{:S(2)}, u32[]{:S(2)}) collective-permute-start(bf16[4,136,512]{2,1,0:T(8,128)(2,1)} %collective-permute-done.3.refs_1_), channel_id=1, source_target_pairs={{0,1},{1,0},{2,3},{3,2},{4,5},{5,4},{6,7},{7,6},{8,9},{9,8},{10,11... | collective-permute-start | bytes 1671176 | tf_op jit(solution)/shard_map/ppermute | solution.py:222
  97.1 8.8 %collective-permute-done.5.refs_3_ = bf16[4,136,512]{2,1,0:T(8,128)(2,1)S(1)} collective-permute-done((bf16[4,136,512]{2,1,0:T(8,128)(2,1)}, bf16[4,136,512]{2,1,0:T(8,128)(2,1)S(1)}, u32[]{:S(2)}, u32[]{:S(2)}) %collective-permute-start.5) | collective-permute-done | bytes 557088 | tf_op jit(solution)/shard_map/ppermute | solution.py:222
  108.8 2.8 %collective-permute-start.10 = (bf16[2,8,64,128]{3,2,1,0:T(8,128)(2,1)S(1)}, bf16[2,8,64,128]{3,2,1,0:T(8,128)(2,1)S(1)}, u32[]{:S(2)}, u32[]{:S(2)}) collective-permute-start(bf16[2,8,64,128]{3,2,1,0:T(8,128)(2,1)S(1)} %bitcast.21), channel_id=1, source_target_pairs={{0,64},{64,0},{128,192},{192,128},{1,65},{65,1},{129,193},{193,129... | collective-permute-start | bytes 786440 | tf_op jit(solution)/shard_map/ppermute | solution.py:222
  111.6 2.8 %collective-permute-start.11 = (bf16[2,8,64,128]{3,2,1,0:T(8,128)(2,1)S(1)}, bf16[2,8,64,128]{3,2,1,0:T(8,128)(2,1)S(1)}, u32[]{:S(2)}, u32[]{:S(2)}) collective-permute-start(bf16[2,8,64,128]{3,2,1,0:T(8,128)(2,1)S(1)} %bitcast.22), channel_id=1, source_target_pairs={{0,128},{64,192},{128,0},{192,64},{1,129},{65,193},{129,1},{193,65... | collective-permute-start | bytes 786440 | tf_op jit(solution)/shard_map/ppermute | solution.py:222
  114.4 4.8 %collective-permute-start.12 = (bf16[2,8,64,128]{3,2,1,0:T(8,128)(2,1)S(1)}, bf16[2,8,64,128]{3,2,1,0:T(8,128)(2,1)S(1)}, u32[]{:S(2)}, u32[]{:S(2)}) collective-permute-start(bf16[2,8,64,128]{3,2,1,0:T(8,128)(2,1)S(1)} %bitcast.23), channel_id=1, source_target_pairs={{0,192},{64,128},{128,64},{192,0},{1,193},{65,129},{129,65},{193,1... | collective-permute-start | bytes 786440 | tf_op jit(solution)/shard_map/ppermute | solution.py:222
  120.1 5.5 %key_value.1 = bf16[16,4,8,128]{3,2,1,0:T(8,128)(2,1)} custom-call(s32[4]{0:T(128)S(1)} %pad_add_fusion.where, bf16[4,136,512]{2,1,0:T(8,128)(2,1)} %copy-done.7, bf16[4,136,512]{2,1,0:T(8,128)(2,1)} %collective-permute-done.3.refs_1_, bf16[4,136,512]{2,1,0:T(8,128)(2,1)} %copy-done.9, bf16[4,136,512]{2,1,0:T(8,128)(2,1)} %copy-done.10, ...), custom_call_target="tpu_custom_call" | custom-call | flops 1140850688 | bytes 6558224 | tf_op jit(solution)/shard_map/key_value/pallas_call | solution.py:203
  125.6 9.2 %all-to-all-start.2 = ((bf16[16,4,8,128]{3,2,1,0:T(8,128)(2,1)}), bf16[16,4,8,128]{3,2,1,0:T(8,128)(2,1)S(1)}, u32[]{:S(2)}, u32[]{:S(2)}) async-start(bf16[16,4,8,128]{3,2,1,0:T(8,128)(2,1)} %key_value.1), calls=%async_computation.2 | async-start | bytes 262144 | tf_op jit(solution)/shard_map/all_to_all | solution.py:25
  134.9 4.9 %query.1.q0 = bf16[4,128,128]{2,1,0:T(8,128)(2,1)S(1)} custom-call(s32[4]{0:T(128)S(1)} %pad_add_fusion.where, bf16[4,136,512]{2,1,0:T(8,128)(2,1)} %copy-done.7, bf16[4,136,512]{2,1,0:T(8,128)(2,1)} %collective-permute-done.3.refs_1_, bf16[4,136,512]{2,1,0:T(8,128)(2,1)} %copy-done.9, bf16[4,136,512]{2,1,0:T(8,128)(2,1)} %copy-done.10, ...), custom_call_target="tpu_custom_call" | custom-call | flops 570425344 | bytes 5509648 | tf_op jit(solution)/shard_map/query/pallas_call | solution.py:203
  139.8 2.3 %collective-permute-start.13 = (bf16[128,128]{1,0:T(8,128)(2,1)S(1)}, bf16[128,128]{1,0:T(8,128)(2,1)S(1)}, u32[]{:S(2)}, u32[]{:S(2)}) collective-permute-start(bf16[128,128]{1,0:T(8,128)(2,1)S(1)} %get-tuple-element.37), channel_id=1, source_target_pairs={{0,8},{8,0},{256,264},{264,256},{1,9},{9,1},{257,265},{265,257},{2... | collective-permute-start | bytes 98312 | tf_op jit(solution)/shard_map/ppermute | solution.py:222
  142.9 2.7 %collective-permute-done.13.q1 = bf16[128,128]{1,0:T(8,128)(2,1)S(1)} collective-permute-done((bf16[128,128]{1,0:T(8,128)(2,1)S(1)}, bf16[128,128]{1,0:T(8,128)(2,1)S(1)}, u32[]{:S(2)}, u32[]{:S(2)}) %collective-permute-start.13) | collective-permute-done | bytes 32800 | tf_op jit(solution)/shard_map/ppermute | solution.py:222
  147.7 10.5 %all-to-all-start.3 = ((bf16[64,8,128]{2,1,0:T(8,128)(2,1)}), bf16[64,8,128]{2,1,0:T(8,128)(2,1)S(1)}, u32[]{:S(2)}, u32[]{:S(2)}) async-start(bf16[64,8,128]{2,1,0:T(8,128)(2,1)} %long_conv.1), calls=%async_computation.3 | async-start | bytes 262144 | tf_op jit(solution)/shard_map/all_to_all | solution.py:25
  158.3 7.5 %collective-permute-start.14 = (bf16[128,128]{1,0:T(8,128)(2,1)S(1)}, bf16[128,128]{1,0:T(8,128)(2,1)S(1)}, u32[]{:S(2)}, u32[]{:S(2)}) collective-permute-start(bf16[128,128]{1,0:T(8,128)(2,1)S(1)} %get-tuple-element.36), channel_id=1, source_target_pairs={{0,256},{8,264},{256,0},{264,8},{1,257},{9,265},{257,1},{265,9},{2... | collective-permute-start | bytes 98312 | tf_op jit(solution)/shard_map/ppermute | solution.py:222
  165.8 3.2 %collective-permute-start.15 = (bf16[128,128]{1,0:T(8,128)(2,1)S(1)}, bf16[128,128]{1,0:T(8,128)(2,1)S(1)}, u32[]{:S(2)}, u32[]{:S(2)}) collective-permute-start(bf16[128,128]{1,0:T(8,128)(2,1)S(1)} %get-tuple-element.35), channel_id=1, source_target_pairs={{0,264},{8,256},{256,8},{264,0},{1,265},{9,257},{257,9},{265,1},{2... | collective-permute-start | bytes 98312 | tf_op jit(solution)/shard_map/ppermute | solution.py:222
  169.0 7.4 %collective-permute-done.15.q3 = bf16[128,128]{1,0:T(8,128)(2,1)S(1)} collective-permute-done((bf16[128,128]{1,0:T(8,128)(2,1)S(1)}, bf16[128,128]{1,0:T(8,128)(2,1)S(1)}, u32[]{:S(2)}, u32[]{:S(2)}) %collective-permute-start.15) | collective-permute-done | bytes 32800 | tf_op jit(solution)/shard_map/ppermute | solution.py:222
  (66 shorter events, 23.8 us)
Async XLA Ops:
  0.7 7.6 %collective-permute-start = (bf16[8,512]{1,0:T(8,128)(2,1)S(1)}, bf16[8,512]{1,0:T(8,128)(2,1)S(1)}, u32[]{:S(2)}, u32[]{:S(2)}) collective-permute-start(bf16[8,512]{1,0:T(8,128)(2,1)S(1)} %slice.18), channel_id=1, source_target_pairs={{0,8},{8,16},{16,24},{24,32},{32,40},{40,48},{48,56},{56,64},{64,7... | collective-permute-start | bytes 24584 | tf_op jit(solution)/shard_map/ppermute | solution.py:217
  6.7 16.4 %copy-start.14 = (bf16[128,512]{1,0:T(8,128)(2,1)S(1)}, bf16[128,512]{1,0:T(8,128)(2,1)}, u32[]{:S(2)}) copy-start(bf16[128,512]{1,0:T(8,128)(2,1)} %param.9) | copy-start | bytes 393220
  6.7 49.9 %copy-start.15 = (f32[3,3,512]{2,1,0:T(4,128)S(1)}, f32[3,3,512]{2,1,0:T(4,128)}, u32[]{:S(2)}) copy-start(f32[3,3,512]{2,1,0:T(4,128)} %param.13) | copy-start | bytes 55300
  8.3 62.1 %all-to-all-start = ((bf16[16,3,64,128]{3,2,1,0:T(8,128)(2,1)}), bf16[16,3,64,128]{3,2,1,0:T(8,128)(2,1)S(1)}, u32[]{:S(2)}, u32[]{:S(2)}) async-start(bf16[16,3,64,128]{3,2,1,0:T(8,128)(2,1)} %bitcast), calls=%async_computation | async-start | bytes 1572864 | tf_op jit(solution)/shard_map/all_to_all | solution.py:25
  23.1 29.0 %collective-permute-start.1 = (bf16[1,136,512]{2,1,0:T(8,128)(2,1)S(1)}, bf16[1,136,512]{2,1,0:T(8,128)(2,1)S(1)}, u32[]{:S(2)}, u32[]{:S(2)}) collective-permute-start(bf16[1,136,512]{2,1,0:T(8,128)(2,1)S(1)} %maximum_bitcast_fusion), channel_id=1, source_target_pairs={{0,256},{2,258},{4,260},{6,262},{256,0},{258,2},{260,4},{262,6},{1... | collective-permute-start | bytes 417800 | tf_op jit(solution)/shard_map/ppermute | solution.py:222
  52.2 16.2 %collective-permute-start.2 = (bf16[2,136,512]{2,1,0:T(8,128)(2,1)S(1)}, bf16[2,136,512]{2,1,0:T(8,128)(2,1)S(1)}, u32[]{:S(2)}, u32[]{:S(2)}) collective-permute-start(bf16[2,136,512]{2,1,0:T(8,128)(2,1)S(1)} %pad_maximum_fusion.1), channel_id=1, source_target_pairs={{0,4},{2,6},{4,0},{6,2},{256,260},{258,262},{260,256},{262,258},{1... | collective-permute-start | bytes 835592 | tf_op jit(solution)/shard_map/ppermute | solution.py:222
  68.5 20.4 %copy-start.7 = (bf16[4,136,512]{2,1,0:T(8,128)(2,1)}, bf16[4,136,512]{2,1,0:T(8,128)(2,1)S(1)}, u32[]{:S(2)}) copy-start(bf16[4,136,512]{2,1,0:T(8,128)(2,1)S(1)} %pad_maximum_fusion.refs_0_) | copy-start | bytes 1671172
  68.5 16.5 %collective-permute-start.3 = (bf16[4,136,512]{2,1,0:T(8,128)(2,1)S(1)}, bf16[4,136,512]{2,1,0:T(8,128)(2,1)}, u32[]{:S(2)}, u32[]{:S(2)}) collective-permute-start(bf16[4,136,512]{2,1,0:T(8,128)(2,1)S(1)} %pad_maximum_fusion.refs_0_), channel_id=1, source_target_pairs={{0,2},{2,0},{4,6},{6,4},{256,258},{258,256},{260,262},{262,260},{1... | collective-permute-start | bytes 1671176 | tf_op jit(solution)/shard_map/ppermute | solution.py:222
  72.4 47.7 %all-to-all-start.1 = ((bf16[4,16,2,64,128]{4,3,2,1,0:T(8,128)(2,1)}), bf16[4,16,2,64,128]{4,3,2,1,0:T(8,128)(2,1)S(1)}, u32[]{:S(2)}, u32[]{:S(2)}) async-start(bf16[4,16,2,64,128]{4,3,2,1,0:T(8,128)(2,1)} %broadcast_in_dim.7), calls=%async_computation.1 | async-start | bytes 4194304 | tf_op jit(solution)/shard_map/all_to_all | solution.py:25
  77.8 17.4 %collective-permute-start.4 = (bf16[4,136,512]{2,1,0:T(8,128)(2,1)S(1)}, bf16[4,136,512]{2,1,0:T(8,128)(2,1)S(1)}, u32[]{:S(2)}, u32[]{:S(2)}) collective-permute-start(bf16[4,136,512]{2,1,0:T(8,128)(2,1)S(1)} %pad_maximum_fusion.refs_0_), channel_id=1, source_target_pairs={{0,8},{8,0},{1,9},{9,1},{2,10},{10,2},{3,11},{11,3},{4,12},{12,4},... | collective-permute-start | bytes 1671176 | tf_op jit(solution)/shard_map/ppermute | solution.py:222
  85.0 20.9 %collective-permute-start.5 = (bf16[4,136,512]{2,1,0:T(8,128)(2,1)}, bf16[4,136,512]{2,1,0:T(8,128)(2,1)S(1)}, u32[]{:S(2)}, u32[]{:S(2)}) collective-permute-start(bf16[4,136,512]{2,1,0:T(8,128)(2,1)} %collective-permute-done.3.refs_1_), channel_id=1, source_target_pairs={{0,8},{8,0},{1,9},{9,1},{2,10},{10,2},{3,11},{11,3},{4,12},{12,4},... | collective-permute-start | bytes 1671176 | tf_op jit(solution)/shard_map/ppermute | solution.py:222
  88.9 22.7 %collective-permute-start.6 = (bf16[4,136,512]{2,1,0:T(8,128)(2,1)S(1)}, bf16[4,136,512]{2,1,0:T(8,128)(2,1)S(1)}, u32[]{:S(2)}, u32[]{:S(2)}) collective-permute-start(bf16[4,136,512]{2,1,0:T(8,128)(2,1)S(1)} %pad_maximum_fusion.refs_0_), channel_id=1, source_target_pairs={{0,1},{1,0},{2,3},{3,2},{4,5},{5,4},{6,7},{7,6},{8,9},{9,8},{10,11... | collective-permute-start | bytes 1671176 | tf_op jit(solution)/shard_map/ppermute | solution.py:222
  90.8 23.6 %collective-permute-start.7 = (bf16[4,136,512]{2,1,0:T(8,128)(2,1)}, bf16[4,136,512]{2,1,0:T(8,128)(2,1)S(1)}, u32[]{:S(2)}, u32[]{:S(2)}) collective-permute-start(bf16[4,136,512]{2,1,0:T(8,128)(2,1)} %collective-permute-done.3.refs_1_), channel_id=1, source_target_pairs={{0,1},{1,0},{2,3},{3,2},{4,5},{5,4},{6,7},{7,6},{8,9},{9,8},{10,11... | collective-permute-start | bytes 1671176 | tf_op jit(solution)/shard_map/ppermute | solution.py:222
  95.2 24.1 %copy-start.9 = (bf16[4,136,512]{2,1,0:T(8,128)(2,1)}, bf16[4,136,512]{2,1,0:T(8,128)(2,1)S(1)}, u32[]{:S(2)}) copy-start(bf16[4,136,512]{2,1,0:T(8,128)(2,1)S(1)} %collective-permute-done.4.refs_2_) | copy-start | bytes 1671172
  95.2 24.1 %collective-permute-start.8 = (bf16[4,136,512]{2,1,0:T(8,128)(2,1)S(1)}, bf16[4,136,512]{2,1,0:T(8,128)(2,1)S(1)}, u32[]{:S(2)}, u32[]{:S(2)}) collective-permute-start(bf16[4,136,512]{2,1,0:T(8,128)(2,1)S(1)} %collective-permute-done.4.refs_2_), channel_id=1, source_target_pairs={{0,1},{1,0},{2,3},{3,2},{4,5},{5,4},{6,7},{7,6},{8,9},{9,8},{10,11... | collective-permute-start | bytes 1671176 | tf_op jit(solution)/shard_map/ppermute | solution.py:222
  105.9 14.3 %collective-permute-start.9 = (bf16[4,136,512]{2,1,0:T(8,128)(2,1)S(1)}, bf16[4,136,512]{2,1,0:T(8,128)(2,1)}, u32[]{:S(2)}, u32[]{:S(2)}) collective-permute-start(bf16[4,136,512]{2,1,0:T(8,128)(2,1)S(1)} %collective-permute-done.5.refs_3_), channel_id=1, source_target_pairs={{0,1},{1,0},{2,3},{3,2},{4,5},{5,4},{6,7},{7,6},{8,9},{9,8},{10,11... | collective-permute-start | bytes 1671176 | tf_op jit(solution)/shard_map/ppermute | solution.py:222
  108.8 26.1 %collective-permute-start.10 = (bf16[2,8,64,128]{3,2,1,0:T(8,128)(2,1)S(1)}, bf16[2,8,64,128]{3,2,1,0:T(8,128)(2,1)S(1)}, u32[]{:S(2)}, u32[]{:S(2)}) collective-permute-start(bf16[2,8,64,128]{3,2,1,0:T(8,128)(2,1)S(1)} %bitcast.21), channel_id=1, source_target_pairs={{0,64},{64,0},{128,192},{192,128},{1,65},{65,1},{129,193},{193,129... | collective-permute-start | bytes 786440 | tf_op jit(solution)/shard_map/ppermute | solution.py:222
  111.6 23.3 %collective-permute-start.11 = (bf16[2,8,64,128]{3,2,1,0:T(8,128)(2,1)S(1)}, bf16[2,8,64,128]{3,2,1,0:T(8,128)(2,1)S(1)}, u32[]{:S(2)}, u32[]{:S(2)}) collective-permute-start(bf16[2,8,64,128]{3,2,1,0:T(8,128)(2,1)S(1)} %bitcast.22), channel_id=1, source_target_pairs={{0,128},{64,192},{128,0},{192,64},{1,129},{65,193},{129,1},{193,65... | collective-permute-start | bytes 786440 | tf_op jit(solution)/shard_map/ppermute | solution.py:222
  114.4 20.5 %collective-permute-start.12 = (bf16[2,8,64,128]{3,2,1,0:T(8,128)(2,1)S(1)}, bf16[2,8,64,128]{3,2,1,0:T(8,128)(2,1)S(1)}, u32[]{:S(2)}, u32[]{:S(2)}) collective-permute-start(bf16[2,8,64,128]{3,2,1,0:T(8,128)(2,1)S(1)} %bitcast.23), channel_id=1, source_target_pairs={{0,192},{64,128},{128,64},{192,0},{1,193},{65,129},{129,65},{193,1... | collective-permute-start | bytes 786440 | tf_op jit(solution)/shard_map/ppermute | solution.py:222
  125.6 20.0 %all-to-all-start.2 = ((bf16[16,4,8,128]{3,2,1,0:T(8,128)(2,1)}), bf16[16,4,8,128]{3,2,1,0:T(8,128)(2,1)S(1)}, u32[]{:S(2)}, u32[]{:S(2)}) async-start(bf16[16,4,8,128]{3,2,1,0:T(8,128)(2,1)} %key_value.1), calls=%async_computation.2 | async-start | bytes 262144 | tf_op jit(solution)/shard_map/all_to_all | solution.py:25
  139.8 5.8 %collective-permute-start.13 = (bf16[128,128]{1,0:T(8,128)(2,1)S(1)}, bf16[128,128]{1,0:T(8,128)(2,1)S(1)}, u32[]{:S(2)}, u32[]{:S(2)}) collective-permute-start(bf16[128,128]{1,0:T(8,128)(2,1)S(1)} %get-tuple-element.37), channel_id=1, source_target_pairs={{0,8},{8,0},{256,264},{264,256},{1,9},{9,1},{257,265},{265,257},{2... | collective-permute-start | bytes 98312 | tf_op jit(solution)/shard_map/ppermute | solution.py:222
  147.7 28.7 %all-to-all-start.3 = ((bf16[64,8,128]{2,1,0:T(8,128)(2,1)}), bf16[64,8,128]{2,1,0:T(8,128)(2,1)S(1)}, u32[]{:S(2)}, u32[]{:S(2)}) async-start(bf16[64,8,128]{2,1,0:T(8,128)(2,1)} %long_conv.1), calls=%async_computation.3 | async-start | bytes 262144 | tf_op jit(solution)/shard_map/all_to_all | solution.py:25
  158.3 10.7 %collective-permute-start.14 = (bf16[128,128]{1,0:T(8,128)(2,1)S(1)}, bf16[128,128]{1,0:T(8,128)(2,1)S(1)}, u32[]{:S(2)}, u32[]{:S(2)}) collective-permute-start(bf16[128,128]{1,0:T(8,128)(2,1)S(1)} %get-tuple-element.36), channel_id=1, source_target_pairs={{0,256},{8,264},{256,0},{264,8},{1,257},{9,265},{257,1},{265,9},{2... | collective-permute-start | bytes 98312 | tf_op jit(solution)/shard_map/ppermute | solution.py:222
  165.8 10.6 %collective-permute-start.15 = (bf16[128,128]{1,0:T(8,128)(2,1)S(1)}, bf16[128,128]{1,0:T(8,128)(2,1)S(1)}, u32[]{:S(2)}, u32[]{:S(2)}) collective-permute-start(bf16[128,128]{1,0:T(8,128)(2,1)S(1)} %get-tuple-element.35), channel_id=1, source_target_pairs={{0,264},{8,256},{256,8},{264,0},{1,265},{9,257},{257,9},{265,1},{2... | collective-permute-start | bytes 98312 | tf_op jit(solution)/shard_map/ppermute | solution.py:222
  (12 other events, 63.9 us)

commit v5 on v4

--- a/solution.py
+++ b/solution.py
@@ -25,9 +25,12 @@
     return lax.all_to_all(value, axes, split_axis=0, concat_axis=0, tiled=True)
 
 
-def from_everyone(value, axes):
+def from_everyone(value, axes, apart=()):
     count = math.prod(SIZES[AXES.index(a)] for a in axes)
-    return exchanged(jnp.broadcast_to(value, (count, *value.shape)), axes)
+    copies = jnp.broadcast_to(value, (count, *value.shape))
+    if apart:
+        copies = copies.reshape(-1, *value.shape[1:])
+    return exchanged(copies, axes + apart)
 
 
 def dft_tables():
@@ -109,14 +112,18 @@
     return (natural == place).astype(F32).astype(BF16)
 
 
-def weights_kernel(w_key, w_value, w_query, out):
+def weights_kernel(where, w_key, w_value, w_query, mine, theirs, held, sems):
+    copies = fetched((w_key, w_value, w_query), [held.at[p] for p in range(3)], sems)
     table = order_table(True)
-    for p, ref in enumerate((w_key, w_value, w_query)):
-        sorted_cols = dot(ref[...], table).astype(BF16)
-        for quarter in range(4):
-            piece = sorted_cols[:, quarter * 128 : (quarter + 1) * 128]
-            for yh in range(4):
-                out[quarter // 2, yh, quarter % 2, p] = piece
+    lower = where[2] < 2
+    for p in range(3):
+        copies[p].wait()
+        cols = dot(held[p], table)
+        ours = jnp.where(lower, cols[:, :256], cols[:, 256:]).astype(BF16)
+        others = jnp.where(lower, cols[:, 256:], cols[:, :256]).astype(BF16)
+        for yl in range(2):
+            mine[yl, p] = ours[:, yl * 128 : (yl + 1) * 128]
+            theirs[yl, p] = others[:, yl * 128 : (yl + 1) * 128]
 
 
 def fetched(sources, held, sems):
@@ -160,14 +167,15 @@
 
 
 def key_value_kernel(where, *refs):
-    sources, (w, taps, out), held, (acc, sems) = refs[:8], refs[8:11], refs[11:19], refs[19:]
-    copies = fetched(sources, held, sems)
+    sources, (taps, out), (w, *held), (acc, sems) = refs[:9], refs[9:11], refs[11:20], refs[20:]
+    copies = fetched((sources[0].at[:, :, :, 0:2], *sources[1:]), (w, *held), sems)
+    copies[0].wait()
 
     def weights(part):
-        block = w[part & 3, part >> 2]
+        block = w[part & 3, :, (part >> 2) ^ where[3]]
         return jnp.concatenate([block[:, p].reshape(512, 128) for p in range(2)], axis=1)
 
-    projected(where, held, weights, acc, copies)
+    projected(where, held, weights, acc, copies[1:])
     for i in range(4):
         keyed = short(acc, i, 0, taps[1])
         valued = short(acc, i, 128, taps[2])
@@ -175,28 +183,26 @@
 
 
 def query_kernel(where, *refs):
-    sources, (taps, out), held, (w, acc, sems) = refs[:12], refs[12:14], refs[14:22], refs[22:]
-    targets = [w.at[d] for d in range(4)] + list(held)
-    copies = fetched(sources[8:] + sources[:8], targets, sems)
-    for copy in copies[:4]:
-        copy.wait()
+    sources, (taps, out), (w, *held), (acc, sems) = refs[:9], refs[9:11], refs[11:20], refs[20:]
+    copies = fetched((sources[0].at[:, :, :, 2], *sources[1:]), (w, *held), sems)
+    copies[0].wait()
 
     def weights(part):
-        return w[(part & 3) ^ where[3], part >> 2].reshape(512, 128)
-
-    projected(where, held, weights, acc, copies[4:])
+        return w[part & 3, :, (part >> 2) ^ where[3]].reshape(512, 128)
+
+    projected(where, held, weights, acc, copies[1:])
     for i in range(4):
-        out[(i % 2) * 2 + i // 2] = short(acc, i, 0, taps[0]).astype(BF16)
-
-
-def gate_kernel(where, q0, q1, q2, q3, returned, out):
-    cols = jnp.concatenate([q0[0], q1[...], q2[...], q3[...]], axis=1)
+        out[i // 2, i % 2] = short(acc, i, 0, taps[0]).astype(BF16)
+
+
+def gate_kernel(where, query, near, far, returned, out):
+    cols = jnp.concatenate([query[0, 0], near[0], far[0], far[1]], axis=1)
     natural = dot(cols, order_table(False, where[2]))
     mixed = returned[...].astype(F32).reshape(512, BLOCK).T
     out[...] = (natural * mixed).astype(BF16)
 
 
-def call(kernel, out_shape, args, scratch=(), in_specs=None, flops=10**8, name=None):
+def call(kernel, out_shape, args, scratch=(), in_specs=None, flops=10**8):
     whole = pl.BlockSpec(memory_space=pltpu.VMEM)
     specs = in_specs or [whole] * len(args)
     moved = sum(math.prod(a.shape) * a.dtype.itemsize for a in args)
@@ -208,7 +214,6 @@
         scratch_shapes=list(scratch),
         compiler_params=pltpu.CompilerParams(vmem_limit_bytes=20 * 2**20),
         cost_estimate=pl.CostEstimate(flops=flops, bytes_accessed=moved, transcendentals=0),
-        name=name,
     )(*args)
 
 
@@ -222,69 +227,71 @@
     return lax.ppermute(value, axes, [(i, i ^ bits) for i in range(count)])
 
 
-def local(tokens, w_query, w_key, w_value, short_taps, filters, skip_gain):
+def mixer(tokens, w_query, w_key, w_value, short_taps, filters, skip_gain):
     shape = jax.ShapeDtypeStruct
     whole = pl.BlockSpec(memory_space=pltpu.VMEM)
     smem = pl.BlockSpec(memory_space=pltpu.SMEM)
     place = lax.axis_index(AXES)
-    core, z_lo, yl, x, z_hi = place % 2, place // 2 % 4, place // 8 % 2, place // 64 % 4, place // 256
-    where = jnp.stack([z_hi * 4 + z_lo, core, z_hi * 2 + yl, x])
-
+    core, z_lo, yl, z_hi = place % 2, place // 2 % 4, place // 8 % 2, place // 256
+    where = jnp.stack([z_hi * 4 + z_lo, core, z_hi * 2 + yl, z_hi])
+
+    anywhere = pl.BlockSpec(memory_space=pl.ANY)
     halo = of_previous(tokens[-HALO:], TOK)
-    sent = call(
-        weights_kernel, shape((2, 4, 2, 3, 64, 128), BF16), (w_key, w_value, w_query), name="sort_weights"
-    )
-    sent, halo = lax.optimization_barrier((sent, halo))
-    first = exchanged(sent.reshape(16, 3, 64, 128), ("z_hi", "yh", "yl"))
+    part = shape((2, 3, 64, 128), BF16)
+    own, others = call(
+        weights_kernel,
+        (part, part),
+        (where, *(pltpu.with_memory_space_constraint(w, pltpu.HBM) for w in (w_key, w_value, w_query))),
+        (pltpu.VMEM((3, 64, 512), BF16), pltpu.SemaphoreType.DMA((3,))),
+        in_specs=[smem] + [anywhere] * 3,
+    )
+    others, halo = lax.optimization_barrier((others, halo))
+    got = swapped(others, ("z_hi",), 1)
+    first = from_everyone(jnp.stack([own, got], axis=1), ("yh",), ("yl",))
 
     ring = ("z_hi", "z_lo")
     mine = jnp.concatenate([halo, tokens], axis=0)[None]
-    two = jnp.concatenate([mine, swapped(mine, ring, 4)], axis=0)
+    far_block = swapped(mine, ring, 4)
+    two = jnp.concatenate([mine, far_block], axis=0)
     even = jnp.concatenate([two, swapped(two, ring, 2)], axis=0)
+    taps = short_taps.reshape(3, 3, 2, 16, 2, 8)
+    taps = lax.dynamic_index_in_dim(taps, z_hi, 2, keepdims=False)
+    taps = lax.dynamic_index_in_dim(taps, yl, 3, keepdims=False).reshape(3, 3, 128)
+
+    first, taps, where, _ = lax.optimization_barrier((first, taps, where, even))
+    weights = from_everyone(first, ("x",))
     odd = swapped(even, ring, 1)
     even_y = swapped(even, ("yl",), 1)
     odd_y = swapped(odd, ("yl",), 1)
     ours = (even, odd, even_y, odd_y)
     features = ours + tuple(swapped(v, ("core",), 1) for v in ours)
 
-    taps = short_taps.reshape(3, 3, 2, 16, 2, 8)
-    taps = lax.dynamic_index_in_dim(taps, z_hi, 2, keepdims=False)
-    taps = lax.dynamic_index_in_dim(taps, yl, 3, keepdims=False).reshape(3, 3, 128)
-
-    first, taps, where = lax.optimization_barrier((first, taps, where))
-    weights = from_everyone(first[:, :2], ("x",)).reshape(4, 2, 8, 2, 64, 128)
-    first_query, _ = lax.optimization_barrier((first[:, 2], odd_y))
-    first_query = first_query.reshape(2, 8, 64, 128)
-    query_weights = [first_query] + [swapped(first_query, ("x",), d) for d in (1, 2, 3)]
-
-    anywhere = pl.BlockSpec(memory_space=pl.ANY)
-    kept = [pltpu.with_memory_space_constraint(v, pltpu.HBM) for v in features]
+
+    kept = [pltpu.with_memory_space_constraint(v, pltpu.HBM) for v in (weights, *features)]
     blocks = [pltpu.VMEM((4, ROWS, 512), BF16)] * 8
     key_value = call(
         key_value_kernel,
         shape((16, 4, 8, BLOCK), BF16),
-        (where, *kept, weights, taps),
-        blocks + [pltpu.VMEM((4 * ROWS, 256), F32), pltpu.SemaphoreType.DMA((8,))],
-        in_specs=[smem] + [anywhere] * 8 + [whole] * 2,
+        (where, *kept, taps),
+        [pltpu.VMEM((4, 8, 2, 2, 64, 128), BF16)]
+        + blocks
+        + [pltpu.VMEM((4 * ROWS, 256), F32), pltpu.SemaphoreType.DMA((9,))],
+        in_specs=[smem] + [anywhere] * 9 + [whole],
         flops=2 * 544 * 4096 * 256,
-        name="key_value",
-    )
-    key_value, query_weights[0] = lax.optimization_barrier((key_value, query_weights[0]))
+    )
     owned = exchanged(key_value, ("x", "yh"))
+    key_value, taps = lax.optimization_barrier((key_value, taps))
     query = call(
         query_kernel,
-        shape((4, BLOCK, 128), BF16),
-        (where, *kept, *query_weights, taps),
-        blocks
-        + [
-            pltpu.VMEM((4, 2, 8, 64, 128), BF16),
-            pltpu.VMEM((4 * ROWS, 128), F32),
-            pltpu.SemaphoreType.DMA((12,)),
-        ],
-        in_specs=[smem] + [anywhere] * 12 + [whole],
+        shape((2, 2, BLOCK, 128), BF16),
+        (where, *kept, taps),
+        [pltpu.VMEM((4, 8, 2, 64, 128), BF16)]
+        + blocks
+        + [pltpu.VMEM((4 * ROWS, 128), F32), pltpu.SemaphoreType.DMA((9,))],
+        in_specs=[smem] + [anywhere] * 9 + [whole],
         flops=2 * 544 * 4096 * 128,
-        name="query",
-    )
+    )
+    near = swapped(query[1], ("yl",), 1)
     tables, turns = dft_tables()
     filters, _ = lax.optimization_barrier((filters, key_value))
     spec, tables, turns = call(
@@ -292,10 +299,9 @@
         (shape((8 * POINTS, 2 * POINTS), F32), shape(tables.shape, BF16), shape(turns.shape, F32)),
         (filters, tables, turns),
         (pltpu.VMEM((512, POINTS), F32),),
-        name="filter_spectrum",
-    )
-    queries = [query] + [swapped(query[bits], ("z_hi", "yl"), bits) for bits in (1, 2, 3)]
-    owned, queries[1], spec = lax.optimization_barrier((owned, queries[1], spec))
+    )
+    owned, near, spec = lax.optimization_barrier((owned, near, spec))
+    far = swapped(jnp.stack([query[0, 1], near[1]]), ("z_hi",), 1)
     mixed = call(
         conv_kernel,
         shape((64, 8, BLOCK), BF16),
@@ -303,15 +309,13 @@
         (pltpu.VMEM((512, POINTS), F32), pltpu.VMEM((512, POINTS), F32)),
         in_specs=[whole, whole, smem, whole, whole],
         flops=2 * 168 * 10**6,
-        name="long_conv",
     )
     returned = exchanged(mixed, TOK)
     return call(
         gate_kernel,
         shape((BLOCK, 512), BF16),
-        (where, *queries, returned),
-        in_specs=[smem] + [whole] * 5,
-        name="gate",
+        (where, query, near, far, returned),
+        in_specs=[smem] + [whole] * 4,
     )
 
 
@@ -326,4 +330,4 @@
         P(TP + TOK, None),
         P(TP + TOK),
     )
-    return jax.shard_map(local, mesh=fine, in_specs=in_specs, out_specs=P(TOK, TP), check_vma=False)
+    return jax.shard_map(mixer, mesh=fine, in_specs=in_specs, out_specs=P(TOK, TP), check_vma=False)

time: 179 us -> 164 us (0.916)
  waiting for transfers between devices: 57.2 us -> 42.8 us
    ppermute x15 -> x12, waiting for transfers between devices: 56.8 us -> 35.5 us  [swapped(): return lax.ppermute(value, axes, [(i, i ^ bits) for i in range(count)])]
    all_to_all x4, waiting for transfers between devices: 0.01 us -> 5.33 us  [exchanged(): return lax.all_to_all(value, axes, split_axis=0, concat_axis=0, tiled=True)]
    ppermute x15 -> x12, starting transfers between devices: 52.9 us -> 50.6 us  [swapped(): return lax.ppermute(value, axes, [(i, i ^ bits) for i in range(count)])]
    broadcast_in_dim x1 -> x2, local copies, waits for them, and re-layouts: 1.89 us -> 3.59 us  [from_everyone(): copies = jnp.broadcast_to(value, (count, *value.shape))]
  transfers between devices with their start and end apart: 20 -> 17, of which waited for: 8 -> 11; matrix products, arithmetic and copies ran while one was open for 2% -> 1% of each run, Pallas kernels for 7% -> 5%
where the time goes in v5:
time: 164 us; the launch traced here: 163 us
  starting transfers between devices  94.7 us (58%)
  waiting for transfers between devices  42.8 us (26%)
  Pallas kernels  17.7 us (11%)
  local copies, waits for them, and re-layouts  6.89 us (4%)
    ppermute x12, starting transfers between devices, swapped(): return lax.ppermute(value, axes, [(i, i ^ bits) for i in range(count)])  50.6 us
    all_to_all x4, starting transfers between devices, exchanged(): return lax.all_to_all(value, axes, split_axis=0, concat_axis=0, tiled=True)  40.7 us
    ppermute x12, waiting for transfers between devices, swapped(): return lax.ppermute(value, axes, [(i, i ^ bits) for i in range(count)])  35.5 us
    pallas_call x6, Pallas kernels, call(): pl.pallas_call(kernel, out_shape=out_shape, in_specs=specs, out_specs=jax...  17.7 us
    all_to_all x4, waiting for transfers between devices, exchanged(): return lax.all_to_all(value, axes, split_axis=0, concat_axis=0, tiled=True)  5.33 us
    broadcast_in_dim x2, local copies, waits for them, and re-layouts, from_everyone(): copies = jnp.broadcast_to(value, (count, *value.shape))  3.59 us
    ppermute x1, starting transfers between devices, of_previous(): return lax.ppermute(value, axes, [(i, i + 1) for i in range(count - 1)])  3.47 us
  transfers between devices with their start and end apart: 17, of which 11 were waited for; matrix products, arithmetic and copies ran while one was open for 1% of the time, Pallas kernels for 5%

profile of v5, /device:TPU:6, one launch (start us, length us, event | category | flops | bytes accessed | tf_op | source)
XLA Modules:
  0.0 162.9 jit_solution(10802196688174769089)
XLA Ops:
  0.8 3.5 %collective-permute-start = (bf16[8,512]{1,0:T(8,128)(2,1)S(1)}, bf16[8,512]{1,0:T(8,128)(2,1)S(1)}, u32[]{:S(2)}, u32[]{:S(2)}) collective-permute-start(bf16[8,512]{1,0:T(8,128)(2,1)S(1)} %slice.12), channel_id=1, source_target_pairs={{0,8},{8,16},{16,24},{24,32},{32,40},{40,48},{48,56},{56,64},{64,7... | collective-permute-start | bytes 24584 | tf_op jit(solution)/shard_map/ppermute | solution.py:222
  8.4 10.9 %collective-permute-start.1 = (bf16[2,3,64,128]{3,2,1,0:T(8,128)(2,1)S(1)}, bf16[2,3,64,128]{3,2,1,0:T(8,128)(2,1)S(1)}, u32[]{:S(2)}, u32[]{:S(2)}) collective-permute-start(bf16[2,3,64,128]{3,2,1,0:T(8,128)(2,1)S(1)} %get-tuple-element.21), channel_id=1, source_target_pairs={{0,256},{256,0},{1,257},{257,1},{2,258},{258,2},{3,259},{259,3},{4... | collective-permute-start | bytes 294920 | tf_op jit(solution)/shard_map/ppermute | solution.py:227
  19.3 3.2 %collective-permute-done.1 = bf16[2,3,64,128]{3,2,1,0:T(8,128)(2,1)S(1)} collective-permute-done((bf16[2,3,64,128]{3,2,1,0:T(8,128)(2,1)S(1)}, bf16[2,3,64,128]{3,2,1,0:T(8,128)(2,1)S(1)}, u32[]{:S(2)}, u32[]{:S(2)}) %collective-permute-start.1) | collective-permute-done | bytes 98336 | tf_op jit(solution)/shard_map/ppermute | solution.py:227
  23.7 6.7 %all-to-all-start = ((bf16[8,2,3,64,128]{4,3,2,1,0:T(8,128)(2,1)}), bf16[8,2,3,64,128]{4,3,2,1,0:T(8,128)(2,1)S(1)}, u32[]{:S(2)}, u32[]{:S(2)}) async-start(bf16[8,2,3,64,128]{4,3,2,1,0:T(8,128)(2,1)} %bitcast.6), calls=%async_computation | async-start | bytes 1572864 | tf_op jit(solution)/shard_map/all_to_all | solution.py:25
  30.4 7.7 %collective-permute-start.2 = (bf16[1,136,512]{2,1,0:T(8,128)(2,1)S(1)}, bf16[1,136,512]{2,1,0:T(8,128)(2,1)S(1)}, u32[]{:S(2)}, u32[]{:S(2)}) collective-permute-start(bf16[1,136,512]{2,1,0:T(8,128)(2,1)S(1)} %maximum_bitcast_fusion), channel_id=1, source_target_pairs={{0,256},{2,258},{4,260},{6,262},{256,0},{258,2},{260,4},{262,6},{1... | collective-permute-start | bytes 417800 | tf_op jit(solution)/shard_map/ppermute | solution.py:227
  38.2 4.6 %collective-permute-done.2 = bf16[1,136,512]{2,1,0:T(8,128)(2,1)S(1)} collective-permute-done((bf16[1,136,512]{2,1,0:T(8,128)(2,1)S(1)}, bf16[1,136,512]{2,1,0:T(8,128)(2,1)S(1)}, u32[]{:S(2)}, u32[]{:S(2)}) %collective-permute-start.2) | collective-permute-done | bytes 139296 | tf_op jit(solution)/shard_map/ppermute | solution.py:227
  42.8 5.1 %collective-permute-start.3 = (bf16[2,136,512]{2,1,0:T(8,128)(2,1)S(1)}, bf16[2,136,512]{2,1,0:T(8,128)(2,1)S(1)}, u32[]{:S(2)}, u32[]{:S(2)}) collective-permute-start(bf16[2,136,512]{2,1,0:T(8,128)(2,1)S(1)} %pad_maximum_fusion.1), channel_id=1, source_target_pairs={{0,4},{2,6},{4,0},{6,2},{256,260},{258,262},{260,256},{262,258},{1... | collective-permute-start | bytes 835592 | tf_op jit(solution)/shard_map/ppermute | solution.py:227
  48.8 7.9 %collective-permute-done.3 = bf16[2,136,512]{2,1,0:T(8,128)(2,1)S(1)} collective-permute-done((bf16[2,136,512]{2,1,0:T(8,128)(2,1)S(1)}, bf16[2,136,512]{2,1,0:T(8,128)(2,1)S(1)}, u32[]{:S(2)}, u32[]{:S(2)}) %collective-permute-start.3) | collective-permute-done | bytes 278560 | tf_op jit(solution)/shard_map/ppermute | solution.py:227
  56.7 2.5 %broadcast_in_dim.11 = bf16[4,8,2,3,64,128]{5,4,3,2,1,0:T(8,128)(2,1)} broadcast(bf16[8,2,3,64,128]{4,3,2,1,0:T(8,128)(2,1)S(1)} %all-to-all-done), dimensions={1,2,3,4,5} | broadcast | bytes 3932160 | tf_op jit(solution)/shard_map/broadcast_in_dim | solution.py:30
  59.2 7.8 %all-to-all-start.1 = ((bf16[4,8,2,3,64,128]{5,4,3,2,1,0:T(8,128)(2,1)}), bf16[4,8,2,3,64,128]{5,4,3,2,1,0:T(8,128)(2,1)}, u32[]{:S(2)}, u32[]{:S(2)}) async-start(bf16[4,8,2,3,64,128]{5,4,3,2,1,0:T(8,128)(2,1)} %broadcast_in_dim.11), calls=%async_computation.1 | async-start | bytes 6291456 | tf_op jit(solution)/shard_map/all_to_all | solution.py:25
  69.0 3.5 %collective-permute-start.5 = (bf16[4,136,512]{2,1,0:T(8,128)(2,1)S(1)}, bf16[4,136,512]{2,1,0:T(8,128)(2,1)S(1)}, u32[]{:S(2)}, u32[]{:S(2)}) collective-permute-start(bf16[4,136,512]{2,1,0:T(8,128)(2,1)S(1)} %pad_maximum_fusion.refs_1_), channel_id=1, source_target_pairs={{0,8},{8,0},{1,9},{9,1},{2,10},{10,2},{3,11},{11,3},{4,12},{12,4},... | collective-permute-start | bytes 1671176 | tf_op jit(solution)/shard_map/ppermute | solution.py:227
  72.5 9.2 %collective-permute-done.4.refs_2_ = bf16[4,136,512]{2,1,0:T(8,128)(2,1)S(1)} collective-permute-done((bf16[4,136,512]{2,1,0:T(8,128)(2,1)S(1)}, bf16[4,136,512]{2,1,0:T(8,128)(2,1)S(1)}, u32[]{:S(2)}, u32[]{:S(2)}) %collective-permute-start.4) | collective-permute-done | bytes 557088 | tf_op jit(solution)/shard_map/ppermute | solution.py:227
  81.7 3.3 %collective-permute-start.6 = (bf16[4,136,512]{2,1,0:T(8,128)(2,1)S(1)}, bf16[4,136,512]{2,1,0:T(8,128)(2,1)S(1)}, u32[]{:S(2)}, u32[]{:S(2)}) collective-permute-start(bf16[4,136,512]{2,1,0:T(8,128)(2,1)S(1)} %collective-permute-done.4.refs_2_), channel_id=1, source_target_pairs={{0,8},{8,0},{1,9},{9,1},{2,10},{10,2},{3,11},{11,3},{4,12},{12,4},... | collective-permute-start | bytes 1671176 | tf_op jit(solution)/shard_map/ppermute | solution.py:227
  86.9 2.4 %collective-permute-start.8 = (bf16[4,136,512]{2,1,0:T(8,128)(2,1)S(1)}, bf16[4,136,512]{2,1,0:T(8,128)(2,1)S(1)}, u32[]{:S(2)}, u32[]{:S(2)}) collective-permute-start(bf16[4,136,512]{2,1,0:T(8,128)(2,1)S(1)} %collective-permute-done.4.refs_2_), channel_id=1, source_target_pairs={{0,1},{1,0},{2,3},{3,2},{4,5},{5,4},{6,7},{7,6},{8,9},{9,8},{10,11... | collective-permute-start | bytes 1671176 | tf_op jit(solution)/shard_map/ppermute | solution.py:227
  91.3 4.3 %collective-permute-done.6.refs_4_ = bf16[4,136,512]{2,1,0:T(8,128)(2,1)S(1)} collective-permute-done((bf16[4,136,512]{2,1,0:T(8,128)(2,1)S(1)}, bf16[4,136,512]{2,1,0:T(8,128)(2,1)S(1)}, u32[]{:S(2)}, u32[]{:S(2)}) %collective-permute-start.6) | collective-permute-done | bytes 557088 | tf_op jit(solution)/shard_map/ppermute | solution.py:227
  101.6 6.1 %shard_map.92 = bf16[16,4,8,128]{3,2,1,0:T(8,128)(2,1)} custom-call(s32[4]{0:T(128)S(1)} %pad_add_fusion.where, bf16[4,8,2,3,64,128]{5,4,3,2,1,0:T(8,128)(2,1)} %all-to-all-done.1.refs_0_, bf16[4,136,512]{2,1,0:T(8,128)(2,1)} %copy-done.4, bf16[4,136,512]{2,1,0:T(8,128)(2,1)} %copy-done.5, bf16[4,136,512]{2,1,0:T(8,128)(2,1)} %copy-done.6, ...), custom_call_target="tpu_custom_call" | custom-call | flops 1140850688 | bytes 7606800 | tf_op jit(solution)/shard_map/pallas_call | solution.py:209
  107.7 9.3 %all-to-all-start.2 = ((bf16[16,4,8,128]{3,2,1,0:T(8,128)(2,1)}), bf16[16,4,8,128]{3,2,1,0:T(8,128)(2,1)S(1)}, u32[]{:S(2)}, u32[]{:S(2)}) async-start(bf16[16,4,8,128]{3,2,1,0:T(8,128)(2,1)} %shard_map.92), calls=%async_computation.2 | async-start | bytes 262144 | tf_op jit(solution)/shard_map/all_to_all | solution.py:25
  117.1 5.1 %shard_map.93.query = bf16[2,2,128,128]{3,2,1,0:T(8,128)(2,1)S(1)} custom-call(s32[4]{0:T(128)S(1)} %pad_add_fusion.where, bf16[4,8,2,3,64,128]{5,4,3,2,1,0:T(8,128)(2,1)} %all-to-all-done.1.refs_0_, bf16[4,136,512]{2,1,0:T(8,128)(2,1)} %copy-done.4, bf16[4,136,512]{2,1,0:T(8,128)(2,1)} %copy-done.5, bf16[4,136,512]{2,1,0:T(8,128)(2,1)} %copy-done.6, ...), custom_call_target="tpu_custom_call" | custom-call | flops 570425344 | bytes 7606800 | tf_op jit(solution)/shard_map/pallas_call | solution.py:209
  122.2 2.5 %collective-permute-start.11 = (bf16[2,128,128]{2,1,0:T(8,128)(2,1)S(1)}, bf16[2,128,128]{2,1,0:T(8,128)(2,1)S(1)}, u32[]{:S(2)}, u32[]{:S(2)}) collective-permute-start(bf16[2,128,128]{2,1,0:T(8,128)(2,1)S(1)} %slice_bitcast_fusion), channel_id=1, source_target_pairs={{0,8},{8,0},{1,9},{9,1},{2,10},{10,2},{3,11},{11,3},{4,12},{12,4},... | collective-permute-start | bytes 196616 | tf_op jit(solution)/shard_map/ppermute | solution.py:227
  125.4 2.9 %collective-permute-done.11.near = bf16[2,128,128]{2,1,0:T(8,128)(2,1)S(1)} collective-permute-done((bf16[2,128,128]{2,1,0:T(8,128)(2,1)S(1)}, bf16[2,128,128]{2,1,0:T(8,128)(2,1)S(1)}, u32[]{:S(2)}, u32[]{:S(2)}) %collective-permute-start.11) | collective-permute-done | bytes 65568 | tf_op jit(solution)/shard_map/ppermute | solution.py:227
  130.5 16.8 %all-to-all-start.3 = ((bf16[64,8,128]{2,1,0:T(8,128)(2,1)}), bf16[64,8,128]{2,1,0:T(8,128)(2,1)S(1)}, u32[]{:S(2)}, u32[]{:S(2)}) async-start(bf16[64,8,128]{2,1,0:T(8,128)(2,1)} %shard_map.95), calls=%async_computation.3 | async-start | bytes 262144 | tf_op jit(solution)/shard_map/all_to_all | solution.py:25
  147.3 7.5 %collective-permute-start.12 = (bf16[2,128,128]{2,1,0:T(8,128)(2,1)S(1)}, bf16[2,128,128]{2,1,0:T(8,128)(2,1)S(1)}, u32[]{:S(2)}, u32[]{:S(2)}) collective-permute-start(bf16[2,128,128]{2,1,0:T(8,128)(2,1)S(1)} %pad_maximum_fusion.3), channel_id=1, source_target_pairs={{0,256},{256,0},{1,257},{257,1},{2,258},{258,2},{3,259},{259,3},{4... | collective-permute-start | bytes 196616 | tf_op jit(solution)/shard_map/ppermute | solution.py:227
  154.8 3.1 %collective-permute-done.12.far = bf16[2,128,128]{2,1,0:T(8,128)(2,1)S(1)} collective-permute-done((bf16[2,128,128]{2,1,0:T(8,128)(2,1)S(1)}, bf16[2,128,128]{2,1,0:T(8,128)(2,1)S(1)}, u32[]{:S(2)}, u32[]{:S(2)}) %collective-permute-start.12) | collective-permute-done | bytes 65568 | tf_op jit(solution)/shard_map/ppermute | solution.py:227
  157.9 3.3 %all-to-all-done.3.returned = bf16[64,8,128]{2,1,0:T(8,128)(2,1)S(1)} async-done(((bf16[64,8,128]{2,1,0:T(8,128)(2,1)}), bf16[64,8,128]{2,1,0:T(8,128)(2,1)S(1)}, u32[]{:S(2)}, u32[]{:S(2)}) %all-to-all-start.3) | async-done | bytes 131104 | tf_op jit(solution)/shard_map/all_to_all | solution.py:25
  (58 shorter events, 23.2 us)
Async XLA Ops:
  0.0 30.4 %copy-start.11 = (bf16[128,512]{1,0:T(8,128)(2,1)S(1)}, bf16[128,512]{1,0:T(8,128)(2,1)}, u32[]{:S(2)}) copy-start(bf16[128,512]{1,0:T(8,128)(2,1)} %param.9) | copy-start | bytes 393220
  0.0 47.9 %copy-start.12 = (f32[3,3,512]{2,1,0:T(4,128)S(1)}, f32[3,3,512]{2,1,0:T(4,128)}, u32[]{:S(2)}) copy-start(f32[3,3,512]{2,1,0:T(4,128)} %param.13) | copy-start | bytes 55300
  0.8 7.6 %collective-permute-start = (bf16[8,512]{1,0:T(8,128)(2,1)S(1)}, bf16[8,512]{1,0:T(8,128)(2,1)S(1)}, u32[]{:S(2)}, u32[]{:S(2)}) collective-permute-start(bf16[8,512]{1,0:T(8,128)(2,1)S(1)} %slice.12), channel_id=1, source_target_pairs={{0,8},{8,16},{16,24},{24,32},{32,40},{40,48},{48,56},{56,64},{64,7... | collective-permute-start | bytes 24584 | tf_op jit(solution)/shard_map/ppermute | solution.py:222
  8.4 14.1 %collective-permute-start.1 = (bf16[2,3,64,128]{3,2,1,0:T(8,128)(2,1)S(1)}, bf16[2,3,64,128]{3,2,1,0:T(8,128)(2,1)S(1)}, u32[]{:S(2)}, u32[]{:S(2)}) collective-permute-start(bf16[2,3,64,128]{3,2,1,0:T(8,128)(2,1)S(1)} %get-tuple-element.21), channel_id=1, source_target_pairs={{0,256},{256,0},{1,257},{257,1},{2,258},{258,2},{3,259},{259,3},{4... | collective-permute-start | bytes 294920 | tf_op jit(solution)/shard_map/ppermute | solution.py:227
  23.7 33.1 %all-to-all-start = ((bf16[8,2,3,64,128]{4,3,2,1,0:T(8,128)(2,1)}), bf16[8,2,3,64,128]{4,3,2,1,0:T(8,128)(2,1)S(1)}, u32[]{:S(2)}, u32[]{:S(2)}) async-start(bf16[8,2,3,64,128]{4,3,2,1,0:T(8,128)(2,1)} %bitcast.6), calls=%async_computation | async-start | bytes 1572864 | tf_op jit(solution)/shard_map/all_to_all | solution.py:25
  30.4 12.4 %collective-permute-start.2 = (bf16[1,136,512]{2,1,0:T(8,128)(2,1)S(1)}, bf16[1,136,512]{2,1,0:T(8,128)(2,1)S(1)}, u32[]{:S(2)}, u32[]{:S(2)}) collective-permute-start(bf16[1,136,512]{2,1,0:T(8,128)(2,1)S(1)} %maximum_bitcast_fusion), channel_id=1, source_target_pairs={{0,256},{2,258},{4,260},{6,262},{256,0},{258,2},{260,4},{262,6},{1... | collective-permute-start | bytes 417800 | tf_op jit(solution)/shard_map/ppermute | solution.py:227
  42.8 13.9 %collective-permute-start.3 = (bf16[2,136,512]{2,1,0:T(8,128)(2,1)S(1)}, bf16[2,136,512]{2,1,0:T(8,128)(2,1)S(1)}, u32[]{:S(2)}, u32[]{:S(2)}) collective-permute-start(bf16[2,136,512]{2,1,0:T(8,128)(2,1)S(1)} %pad_maximum_fusion.1), channel_id=1, source_target_pairs={{0,4},{2,6},{4,0},{6,2},{256,260},{258,262},{260,256},{262,258},{1... | collective-permute-start | bytes 835592 | tf_op jit(solution)/shard_map/ppermute | solution.py:227
  56.7 28.3 %copy-start.4 = (bf16[4,136,512]{2,1,0:T(8,128)(2,1)}, bf16[4,136,512]{2,1,0:T(8,128)(2,1)S(1)}, u32[]{:S(2)}) copy-start(bf16[4,136,512]{2,1,0:T(8,128)(2,1)S(1)} %pad_maximum_fusion.refs_1_) | copy-start | bytes 1671172
  59.2 42.3 %all-to-all-start.1 = ((bf16[4,8,2,3,64,128]{5,4,3,2,1,0:T(8,128)(2,1)}), bf16[4,8,2,3,64,128]{5,4,3,2,1,0:T(8,128)(2,1)}, u32[]{:S(2)}, u32[]{:S(2)}) async-start(bf16[4,8,2,3,64,128]{5,4,3,2,1,0:T(8,128)(2,1)} %broadcast_in_dim.11), calls=%async_computation.1 | async-start | bytes 6291456 | tf_op jit(solution)/shard_map/all_to_all | solution.py:25
  67.1 14.6 %collective-permute-start.4 = (bf16[4,136,512]{2,1,0:T(8,128)(2,1)S(1)}, bf16[4,136,512]{2,1,0:T(8,128)(2,1)S(1)}, u32[]{:S(2)}, u32[]{:S(2)}) collective-permute-start(bf16[4,136,512]{2,1,0:T(8,128)(2,1)S(1)} %pad_maximum_fusion.refs_1_), channel_id=1, source_target_pairs={{0,2},{2,0},{4,6},{6,4},{256,258},{258,256},{260,262},{262,260},{1... | collective-permute-start | bytes 1671176 | tf_op jit(solution)/shard_map/ppermute | solution.py:227
  69.0 20.4 %collective-permute-start.5 = (bf16[4,136,512]{2,1,0:T(8,128)(2,1)S(1)}, bf16[4,136,512]{2,1,0:T(8,128)(2,1)S(1)}, u32[]{:S(2)}, u32[]{:S(2)}) collective-permute-start(bf16[4,136,512]{2,1,0:T(8,128)(2,1)S(1)} %pad_maximum_fusion.refs_1_), channel_id=1, source_target_pairs={{0,8},{8,0},{1,9},{9,1},{2,10},{10,2},{3,11},{11,3},{4,12},{12,4},... | collective-permute-start | bytes 1671176 | tf_op jit(solution)/shard_map/ppermute | solution.py:227
  81.7 19.9 %copy-start.5 = (bf16[4,136,512]{2,1,0:T(8,128)(2,1)}, bf16[4,136,512]{2,1,0:T(8,128)(2,1)S(1)}, u32[]{:S(2)}) copy-start(bf16[4,136,512]{2,1,0:T(8,128)(2,1)S(1)} %collective-permute-done.4.refs_2_) | copy-start | bytes 1671172
  81.7 13.9 %collective-permute-start.6 = (bf16[4,136,512]{2,1,0:T(8,128)(2,1)S(1)}, bf16[4,136,512]{2,1,0:T(8,128)(2,1)S(1)}, u32[]{:S(2)}, u32[]{:S(2)}) collective-permute-start(bf16[4,136,512]{2,1,0:T(8,128)(2,1)S(1)} %collective-permute-done.4.refs_2_), channel_id=1, source_target_pairs={{0,8},{8,0},{1,9},{9,1},{2,10},{10,2},{3,11},{11,3},{4,12},{12,4},... | collective-permute-start | bytes 1671176 | tf_op jit(solution)/shard_map/ppermute | solution.py:227
  85.0 12.5 %collective-permute-start.7 = (bf16[4,136,512]{2,1,0:T(8,128)(2,1)S(1)}, bf16[4,136,512]{2,1,0:T(8,128)(2,1)S(1)}, u32[]{:S(2)}, u32[]{:S(2)}) collective-permute-start(bf16[4,136,512]{2,1,0:T(8,128)(2,1)S(1)} %pad_maximum_fusion.refs_1_), channel_id=1, source_target_pairs={{0,1},{1,0},{2,3},{3,2},{4,5},{5,4},{6,7},{7,6},{8,9},{9,8},{10,11... | collective-permute-start | bytes 1671176 | tf_op jit(solution)/shard_map/ppermute | solution.py:227
  86.9 10.6 %collective-permute-start.8 = (bf16[4,136,512]{2,1,0:T(8,128)(2,1)S(1)}, bf16[4,136,512]{2,1,0:T(8,128)(2,1)S(1)}, u32[]{:S(2)}, u32[]{:S(2)}) collective-permute-start(bf16[4,136,512]{2,1,0:T(8,128)(2,1)S(1)} %collective-permute-done.4.refs_2_), channel_id=1, source_target_pairs={{0,1},{1,0},{2,3},{3,2},{4,5},{5,4},{6,7},{7,6},{8,9},{9,8},{10,11... | collective-permute-start | bytes 1671176 | tf_op jit(solution)/shard_map/ppermute | solution.py:227
  89.4 12.2 %copy-start.6 = (bf16[4,136,512]{2,1,0:T(8,128)(2,1)}, bf16[4,136,512]{2,1,0:T(8,128)(2,1)S(1)}, u32[]{:S(2)}) copy-start(bf16[4,136,512]{2,1,0:T(8,128)(2,1)S(1)} %collective-permute-done.5.refs_3_) | copy-start | bytes 1671172
  89.4 8.2 %collective-permute-start.9 = (bf16[4,136,512]{2,1,0:T(8,128)(2,1)S(1)}, bf16[4,136,512]{2,1,0:T(8,128)(2,1)S(1)}, u32[]{:S(2)}, u32[]{:S(2)}) collective-permute-start(bf16[4,136,512]{2,1,0:T(8,128)(2,1)S(1)} %collective-permute-done.5.refs_3_), channel_id=1, source_target_pairs={{0,1},{1,0},{2,3},{3,2},{4,5},{5,4},{6,7},{7,6},{8,9},{9,8},{10,11... | collective-permute-start | bytes 1671176 | tf_op jit(solution)/shard_map/ppermute | solution.py:227
  95.6 4.0 %collective-permute-start.10 = (bf16[4,136,512]{2,1,0:T(8,128)(2,1)S(1)}, bf16[4,136,512]{2,1,0:T(8,128)(2,1)}, u32[]{:S(2)}, u32[]{:S(2)}) collective-permute-start(bf16[4,136,512]{2,1,0:T(8,128)(2,1)S(1)} %collective-permute-done.6.refs_4_), channel_id=1, source_target_pairs={{0,1},{1,0},{2,3},{3,2},{4,5},{5,4},{6,7},{7,6},{8,9},{9,8},{10,11... | collective-permute-start | bytes 1671176 | tf_op jit(solution)/shard_map/ppermute | solution.py:227
  107.7 20.6 %all-to-all-start.2 = ((bf16[16,4,8,128]{3,2,1,0:T(8,128)(2,1)}), bf16[16,4,8,128]{3,2,1,0:T(8,128)(2,1)S(1)}, u32[]{:S(2)}, u32[]{:S(2)}) async-start(bf16[16,4,8,128]{3,2,1,0:T(8,128)(2,1)} %shard_map.92), calls=%async_computation.2 | async-start | bytes 262144 | tf_op jit(solution)/shard_map/all_to_all | solution.py:25
  117.1 7.6 %copy-start.1 = (f32[8,8192]{1,0:T(8,128)S(1)}, f32[8,8192]{1,0:T(8,128)}, u32[]{:S(2)}) copy-start(f32[8,8192]{1,0:T(8,128)} %filters) | copy-start | bytes 786436
  117.1 11.3 %copy-start.3 = (f32[8]{0:T(128)S(1)}, f32[8]{0:T(128)}, u32[]{:S(2)}) copy-start(f32[8]{0:T(128)} %skip.1) | copy-start | bytes 100
  122.2 6.2 %collective-permute-start.11 = (bf16[2,128,128]{2,1,0:T(8,128)(2,1)S(1)}, bf16[2,128,128]{2,1,0:T(8,128)(2,1)S(1)}, u32[]{:S(2)}, u32[]{:S(2)}) collective-permute-start(bf16[2,128,128]{2,1,0:T(8,128)(2,1)S(1)} %slice_bitcast_fusion), channel_id=1, source_target_pairs={{0,8},{8,0},{1,9},{9,1},{2,10},{10,2},{3,11},{11,3},{4,12},{12,4},... | collective-permute-start | bytes 196616 | tf_op jit(solution)/shard_map/ppermute | solution.py:227
  130.5 30.7 %all-to-all-start.3 = ((bf16[64,8,128]{2,1,0:T(8,128)(2,1)}), bf16[64,8,128]{2,1,0:T(8,128)(2,1)S(1)}, u32[]{:S(2)}, u32[]{:S(2)}) async-start(bf16[64,8,128]{2,1,0:T(8,128)(2,1)} %shard_map.95), calls=%async_computation.3 | async-start | bytes 262144 | tf_op jit(solution)/shard_map/all_to_all | solution.py:25
  147.3 10.6 %collective-permute-start.12 = (bf16[2,128,128]{2,1,0:T(8,128)(2,1)S(1)}, bf16[2,128,128]{2,1,0:T(8,128)(2,1)S(1)}, u32[]{:S(2)}, u32[]{:S(2)}) collective-permute-start(bf16[2,128,128]{2,1,0:T(8,128)(2,1)S(1)} %pad_maximum_fusion.3), channel_id=1, source_target_pairs={{0,256},{256,0},{1,257},{257,1},{2,258},{258,2},{3,259},{259,3},{4... | collective-permute-start | bytes 196616 | tf_op jit(solution)/shard_map/ppermute | solution.py:227
  (6 other events, 27.1 us)

commit v6 on v5

--- a/solution.py
+++ b/solution.py
@@ -134,22 +134,24 @@
 
 
 def projected(where, features, w, acc, ready):
-    z, core = where[0], where[1]
     for i, (half, low) in enumerate((h, l) for h in range(2) for l in (0, 2, 1, 3)):
         if i % 2 == 0:
-            for parity in range(2):
-                ready[half * 4 + parity * 2 + low % 2].wait()
-        part = ((z ^ low) & 3) * 2 + (core ^ half)
+            for copy in ready(i // 2):
+                copy.wait()
         pieces = [
             features[half * 4 + parity * 2 + low % 2][(low // 2) * 2 : (low // 2) * 2 + 2]
             for parity in range(2)
         ]
         rows = jnp.concatenate([p.reshape(2 * ROWS, 512) for p in pieces], axis=0)
-        term = dot(rows, w(part))
+        term = dot(rows, w(i // 2, part_of(where, half, low)))
         if i == 0:
             acc[...] = term
         else:
             acc[...] += term
+
+
+def part_of(where, half, low):
+    return ((where[0] ^ low) & 3) * 2 + (where[1] ^ half)
 
 
 def group_of(where, i):
@@ -168,14 +170,20 @@
 
 def key_value_kernel(where, *refs):
     sources, (taps, out), (w, *held), (acc, sems) = refs[:9], refs[9:11], refs[11:20], refs[20:]
-    copies = fetched((sources[0].at[:, :, :, 0:2], *sources[1:]), (w, *held), sems)
-    copies[0].wait()
-
-    def weights(part):
-        block = w[part & 3, :, (part >> 2) ^ where[3]]
-        return jnp.concatenate([block[:, p].reshape(512, 128) for p in range(2)], axis=1)
-
-    projected(where, held, weights, acc, copies[1:])
+    pairs = [(half, low) for half in range(2) for low in range(2)]
+    columns = [sources[0].at[part_of(where, half, low) & 3] for half, low in pairs]
+    order = [half * 4 + parity * 2 + low for half, low in pairs for parity in range(2)]
+    froms, targets = [], []
+    for j in range(4):
+        froms += [columns[j], sources[1 + order[2 * j]], sources[1 + order[2 * j + 1]]]
+        targets += [w.at[j], held[order[2 * j]], held[order[2 * j + 1]]]
+    copies = fetched(froms, targets, sems)
+
+    def weights(j, part):
+        z_hi = (part >> 2) ^ where[3]
+        return jnp.concatenate([w[j, :, p, z_hi].reshape(512, 128) for p in range(2)], axis=1)
+
+    projected(where, held, weights, acc, lambda j: copies[3 * j : 3 * j + 3])
     for i in range(4):
         keyed = short(acc, i, 0, taps[1])
         valued = short(acc, i, 128, taps[2])
@@ -183,14 +191,13 @@
 
 
 def query_kernel(where, *refs):
-    sources, (taps, out), (w, *held), (acc, sems) = refs[:9], refs[9:11], refs[11:20], refs[20:]
-    copies = fetched((sources[0].at[:, :, :, 2], *sources[1:]), (w, *held), sems)
-    copies[0].wait()
-
-    def weights(part):
-        return w[part & 3, :, (part >> 2) ^ where[3]].reshape(512, 128)
-
-    projected(where, held, weights, acc, copies[1:])
+    sources, (taps, out), (w, *held), (acc, sems) = refs[:12], refs[12:14], refs[14:23], refs[23:]
+    copies = fetched(sources, [w.at[d] for d in range(4)] + held, sems)
+
+    def weights(j, part):
+        return w[(part & 3) ^ where[4], :, (part >> 2) ^ where[3]].reshape(512, 128)
+
+    projected(where, held, weights, acc, lambda j: copies if j == 0 else [])
     for i in range(4):
         out[i // 2, i % 2] = short(acc, i, 0, taps[0]).astype(BF16)
 
@@ -232,8 +239,8 @@
     whole = pl.BlockSpec(memory_space=pltpu.VMEM)
     smem = pl.BlockSpec(memory_space=pltpu.SMEM)
     place = lax.axis_index(AXES)
-    core, z_lo, yl, z_hi = place % 2, place // 2 % 4, place // 8 % 2, place // 256
-    where = jnp.stack([z_hi * 4 + z_lo, core, z_hi * 2 + yl, z_hi])
+    core, z_lo, yl, x, z_hi = place % 2, place // 2 % 4, place // 8 % 2, place // 64 % 4, place // 256
+    where = jnp.stack([z_hi * 4 + z_lo, core, z_hi * 2 + yl, z_hi, x])
 
     anywhere = pl.BlockSpec(memory_space=pl.ANY)
     halo = of_previous(tokens[-HALO:], TOK)
@@ -247,7 +254,7 @@
     )
     others, halo = lax.optimization_barrier((others, halo))
     got = swapped(others, ("z_hi",), 1)
-    first = from_everyone(jnp.stack([own, got], axis=1), ("yh",), ("yl",))
+    first = from_everyone(jnp.stack([own, got], axis=2), ("yh",), ("yl",))
 
     ring = ("z_hi", "z_lo")
     mine = jnp.concatenate([halo, tokens], axis=0)[None]
@@ -259,23 +266,26 @@
     taps = lax.dynamic_index_in_dim(taps, yl, 3, keepdims=False).reshape(3, 3, 128)
 
     first, taps, where, _ = lax.optimization_barrier((first, taps, where, even))
-    weights = from_everyone(first, ("x",))
+    weights = from_everyone(first[:, :2], ("x",))
     odd = swapped(even, ring, 1)
     even_y = swapped(even, ("yl",), 1)
     odd_y = swapped(odd, ("yl",), 1)
     ours = (even, odd, even_y, odd_y)
-    features = ours + tuple(swapped(v, ("core",), 1) for v in ours)
-
-
-    kept = [pltpu.with_memory_space_constraint(v, pltpu.HBM) for v in (weights, *features)]
+    features = [swapped(v, ("core",), 1) for v in ours[:3]]
+    features.append(swapped(odd_y, ("core",), 1))
+    features = (*ours, *features)
+    query_weights = [first[:, 2]]
+    query_weights += [swapped(query_weights[0], ("x",), d) for d in (1, 2, 3)]
+
+    kept = [pltpu.with_memory_space_constraint(v, pltpu.HBM) for v in features]
     blocks = [pltpu.VMEM((4, ROWS, 512), BF16)] * 8
     key_value = call(
         key_value_kernel,
         shape((16, 4, 8, BLOCK), BF16),
-        (where, *kept, taps),
+        (where, weights, *kept, taps),
         [pltpu.VMEM((4, 8, 2, 2, 64, 128), BF16)]
         + blocks
-        + [pltpu.VMEM((4 * ROWS, 256), F32), pltpu.SemaphoreType.DMA((9,))],
+        + [pltpu.VMEM((4 * ROWS, 256), F32), pltpu.SemaphoreType.DMA((12,))],
         in_specs=[smem] + [anywhere] * 9 + [whole],
         flops=2 * 544 * 4096 * 256,
     )
@@ -284,11 +294,11 @@
     query = call(
         query_kernel,
         shape((2, 2, BLOCK, 128), BF16),
-        (where, *kept, taps),
+        (where, *query_weights, *kept, taps),
         [pltpu.VMEM((4, 8, 2, 64, 128), BF16)]
         + blocks
-        + [pltpu.VMEM((4 * ROWS, 128), F32), pltpu.SemaphoreType.DMA((9,))],
-        in_specs=[smem] + [anywhere] * 9 + [whole],
+        + [pltpu.VMEM((4 * ROWS, 128), F32), pltpu.SemaphoreType.DMA((12,))],
+        in_specs=[smem] + [anywhere] * 12 + [whole],
         flops=2 * 544 * 4096 * 128,
     )
     near = swapped(query[1], ("yl",), 1)
@@ -312,10 +322,7 @@
     )
     returned = exchanged(mixed, TOK)
     return call(
-        gate_kernel,
-        shape((BLOCK, 512), BF16),
-        (where, query, near, far, returned),
-        in_specs=[smem] + [whole] * 4,
+        gate_kernel, shape((BLOCK, 512), BF16), (where, query, near, far, returned), in_specs=[smem] + [whole] * 4
     )
 
 

time: 164 us -> 171 us (1.043)
  starting transfers between devices: 94.7 us -> 105 us
    ppermute x12 -> x15, starting transfers between devices: 50.6 us -> 61.4 us  [swapped(): return lax.ppermute(value, axes, [(i, i ^ bits) for i in range(count)])]
    all_to_all x4, waiting for transfers between devices: 5.33 us -> 3.19 us  [exchanged(): return lax.all_to_all(value, axes, split_axis=0, concat_axis=0, tiled=True)]
    ppermute x12 -> x15, waiting for transfers between devices: 35.5 us -> 36.3 us  [swapped(): return lax.ppermute(value, axes, [(i, i ^ bits) for i in range(count)])]
  transfers between devices with their start and end apart: 17 -> 20, of which waited for: 11 -> 9; matrix products, arithmetic and copies ran while one was open for 1% -> 2% of each run, Pallas kernels for 5% -> 7%
where the time goes in v6:
time: 171 us; the launch traced here: 170 us
  starting transfers between devices  105 us (61%)
  waiting for transfers between devices  41.5 us (24%)
  Pallas kernels  16.3 us (10%)
  local copies, waits for them, and re-layouts  6.58 us (4%)
    ppermute x15, starting transfers between devices, swapped(): return lax.ppermute(value, axes, [(i, i ^ bits) for i in range(count)])  61.4 us
    all_to_all x4, starting transfers between devices, exchanged(): return lax.all_to_all(value, axes, split_axis=0, concat_axis=0, tiled=True)  39.8 us
    ppermute x15, waiting for transfers between devices, swapped(): return lax.ppermute(value, axes, [(i, i ^ bits) for i in range(count)])  36.3 us
    pallas_call x6, Pallas kernels, call(): pl.pallas_call(kernel, out_shape=out_shape, in_specs=specs, out_specs=jax...  16.3 us
    ppermute x1, starting transfers between devices, of_previous(): return lax.ppermute(value, axes, [(i, i + 1) for i in range(count - 1)])  3.47 us
  transfers between devices with their start and end apart: 20, of which 9 were waited for; matrix products, arithmetic and copies ran while one was open for 2% of the time, Pallas kernels for 7%

profile of v6, /device:TPU:6, one launch (start us, length us, event | category | flops | bytes accessed | tf_op | source)
XLA Modules:
  0.0 169.8 jit_solution(291203289875271366)
XLA Ops:
  0.8 3.5 %collective-permute-start = (bf16[8,512]{1,0:T(8,128)(2,1)S(1)}, bf16[8,512]{1,0:T(8,128)(2,1)S(1)}, u32[]{:S(2)}, u32[]{:S(2)}) collective-permute-start(bf16[8,512]{1,0:T(8,128)(2,1)S(1)} %slice.18), channel_id=1, source_target_pairs={{0,8},{8,16},{16,24},{24,32},{32,40},{40,48},{48,56},{56,64},{64,7... | collective-permute-start | bytes 24584 | tf_op jit(solution)/shard_map/ppermute | solution.py:229
  8.4 10.9 %collective-permute-start.1 = (bf16[2,3,64,128]{3,2,1,0:T(8,128)(2,1)S(1)}, bf16[2,3,64,128]{3,2,1,0:T(8,128)(2,1)S(1)}, u32[]{:S(2)}, u32[]{:S(2)}) collective-permute-start(bf16[2,3,64,128]{3,2,1,0:T(8,128)(2,1)S(1)} %get-tuple-element.21), channel_id=1, source_target_pairs={{0,256},{256,0},{1,257},{257,1},{2,258},{258,2},{3,259},{259,3},{4... | collective-permute-start | bytes 294920 | tf_op jit(solution)/shard_map/ppermute | solution.py:234
  19.3 3.2 %collective-permute-done.1 = bf16[2,3,64,128]{3,2,1,0:T(8,128)(2,1)S(1)} collective-permute-done((bf16[2,3,64,128]{3,2,1,0:T(8,128)(2,1)S(1)}, bf16[2,3,64,128]{3,2,1,0:T(8,128)(2,1)S(1)}, u32[]{:S(2)}, u32[]{:S(2)}) %collective-permute-start.1) | collective-permute-done | bytes 98336 | tf_op jit(solution)/shard_map/ppermute | solution.py:234
  23.7 6.8 %all-to-all-start = ((bf16[8,3,2,64,128]{4,3,2,1,0:T(8,128)(2,1)}), bf16[8,3,2,64,128]{4,3,2,1,0:T(8,128)(2,1)S(1)}, u32[]{:S(2)}, u32[]{:S(2)}) async-start(bf16[8,3,2,64,128]{4,3,2,1,0:T(8,128)(2,1)} %bitcast.7), calls=%async_computation | async-start | bytes 1572864 | tf_op jit(solution)/shard_map/all_to_all | solution.py:25
  30.4 7.7 %collective-permute-start.2 = (bf16[1,136,512]{2,1,0:T(8,128)(2,1)S(1)}, bf16[1,136,512]{2,1,0:T(8,128)(2,1)S(1)}, u32[]{:S(2)}, u32[]{:S(2)}) collective-permute-start(bf16[1,136,512]{2,1,0:T(8,128)(2,1)S(1)} %maximum_bitcast_fusion), channel_id=1, source_target_pairs={{0,256},{2,258},{4,260},{6,262},{256,0},{258,2},{260,4},{262,6},{1... | collective-permute-start | bytes 417800 | tf_op jit(solution)/shard_map/ppermute | solution.py:234
  38.2 4.6 %collective-permute-done.2 = bf16[1,136,512]{2,1,0:T(8,128)(2,1)S(1)} collective-permute-done((bf16[1,136,512]{2,1,0:T(8,128)(2,1)S(1)}, bf16[1,136,512]{2,1,0:T(8,128)(2,1)S(1)}, u32[]{:S(2)}, u32[]{:S(2)}) %collective-permute-start.2) | collective-permute-done | bytes 139296 | tf_op jit(solution)/shard_map/ppermute | solution.py:234
  42.8 5.1 %collective-permute-start.3 = (bf16[2,136,512]{2,1,0:T(8,128)(2,1)S(1)}, bf16[2,136,512]{2,1,0:T(8,128)(2,1)S(1)}, u32[]{:S(2)}, u32[]{:S(2)}) collective-permute-start(bf16[2,136,512]{2,1,0:T(8,128)(2,1)S(1)} %pad_maximum_fusion.1), channel_id=1, source_target_pairs={{0,4},{2,6},{4,0},{6,2},{256,260},{258,262},{260,256},{262,258},{1... | collective-permute-start | bytes 835592 | tf_op jit(solution)/shard_map/ppermute | solution.py:234
  47.9 8.7 %collective-permute-done.3 = bf16[2,136,512]{2,1,0:T(8,128)(2,1)S(1)} collective-permute-done((bf16[2,136,512]{2,1,0:T(8,128)(2,1)S(1)}, bf16[2,136,512]{2,1,0:T(8,128)(2,1)S(1)}, u32[]{:S(2)}, u32[]{:S(2)}) %collective-permute-start.3) | collective-permute-done | bytes 278560 | tf_op jit(solution)/shard_map/ppermute | solution.py:234
  62.2 6.1 %all-to-all-start.1 = ((bf16[4,8,2,2,64,128]{5,4,3,2,1,0:T(8,128)(2,1)}), bf16[4,8,2,2,64,128]{5,4,3,2,1,0:T(8,128)(2,1)S(1)}, u32[]{:S(2)}, u32[]{:S(2)}) async-start(bf16[4,8,2,2,64,128]{5,4,3,2,1,0:T(8,128)(2,1)} %broadcast_in_dim.11), calls=%async_computation.1 | async-start | bytes 4194304 | tf_op jit(solution)/shard_map/all_to_all | solution.py:25
  68.3 3.5 %collective-permute-start.8 = (bf16[4,136,512]{2,1,0:T(8,128)(2,1)S(1)}, bf16[4,136,512]{2,1,0:T(8,128)(2,1)S(1)}, u32[]{:S(2)}, u32[]{:S(2)}) collective-permute-start(bf16[4,136,512]{2,1,0:T(8,128)(2,1)S(1)} %pad_maximum_fusion.refs_1_.refs_4_), channel_id=1, source_target_pairs={{0,8},{8,0},{1,9},{9,1},{2,10},{10,2},{3,11},{11,3},{4,12},{12,4},... | collective-permute-start | bytes 1671176 | tf_op jit(solution)/shard_map/ppermute | solution.py:234
  71.8 3.0 %collective-permute-start.9 = (bf16[4,136,512]{2,1,0:T(8,128)(2,1)}, bf16[4,136,512]{2,1,0:T(8,128)(2,1)S(1)}, u32[]{:S(2)}, u32[]{:S(2)}) collective-permute-start(bf16[4,136,512]{2,1,0:T(8,128)(2,1)} %collective-permute-done.7.refs_2_.refs_5_), channel_id=1, source_target_pairs={{0,8},{8,0},{1,9},{9,1},{2,10},{10,2},{3,11},{11,3},{4,12},{12,4},... | collective-permute-start | bytes 1671176 | tf_op jit(solution)/shard_map/ppermute | solution.py:234
  79.2 6.4 %collective-permute-done.8.refs_3_.refs_6_ = bf16[4,136,512]{2,1,0:T(8,128)(2,1)S(1)} collective-permute-done((bf16[4,136,512]{2,1,0:T(8,128)(2,1)S(1)}, bf16[4,136,512]{2,1,0:T(8,128)(2,1)S(1)}, u32[]{:S(2)}, u32[]{:S(2)}) %collective-permute-start.8) | collective-permute-done | bytes 557088 | tf_op jit(solution)/shard_map/ppermute | solution.py:234
  87.6 7.3 %collective-permute-done.9.refs_4_.refs_7_ = bf16[4,136,512]{2,1,0:T(8,128)(2,1)S(1)} collective-permute-done((bf16[4,136,512]{2,1,0:T(8,128)(2,1)}, bf16[4,136,512]{2,1,0:T(8,128)(2,1)S(1)}, u32[]{:S(2)}, u32[]{:S(2)}) %collective-permute-start.9) | collective-permute-done | bytes 557088 | tf_op jit(solution)/shard_map/ppermute | solution.py:234
  97.7 2.8 %collective-permute-start.4 = (bf16[8,2,64,128]{3,2,1,0:T(8,128)(2,1)S(1)}, bf16[8,2,64,128]{3,2,1,0:T(8,128)(2,1)S(1)}, u32[]{:S(2)}, u32[]{:S(2)}) collective-permute-start(bf16[8,2,64,128]{3,2,1,0:T(8,128)(2,1)S(1)} %slice_bitcast_fusion.refs_0_), channel_id=1, source_target_pairs={{0,64},{64,0},{128,192},{192,128},{1,65},{65,1},{129,193},{193,129... | collective-permute-start | bytes 786440 | tf_op jit(solution)/shard_map/ppermute | solution.py:234
  100.5 2.8 %collective-permute-start.5 = (bf16[8,2,64,128]{3,2,1,0:T(8,128)(2,1)S(1)}, bf16[8,2,64,128]{3,2,1,0:T(8,128)(2,1)S(1)}, u32[]{:S(2)}, u32[]{:S(2)}) collective-permute-start(bf16[8,2,64,128]{3,2,1,0:T(8,128)(2,1)S(1)} %slice_bitcast_fusion.refs_0_), channel_id=1, source_target_pairs={{0,128},{64,192},{128,0},{192,64},{1,129},{65,193},{129,1},{193,65... | collective-permute-start | bytes 786440 | tf_op jit(solution)/shard_map/ppermute | solution.py:234
  103.4 4.8 %collective-permute-start.6 = (bf16[8,2,64,128]{3,2,1,0:T(8,128)(2,1)S(1)}, bf16[8,2,64,128]{3,2,1,0:T(8,128)(2,1)S(1)}, u32[]{:S(2)}, u32[]{:S(2)}) collective-permute-start(bf16[8,2,64,128]{3,2,1,0:T(8,128)(2,1)S(1)} %slice_bitcast_fusion.refs_0_), channel_id=1, source_target_pairs={{0,192},{64,128},{128,64},{192,0},{1,193},{65,129},{129,65},{193,1... | collective-permute-start | bytes 786440 | tf_op jit(solution)/shard_map/ppermute | solution.py:234
  109.1 5.4 %shard_map.92 = bf16[16,4,8,128]{3,2,1,0:T(8,128)(2,1)} custom-call(s32[5]{0:T(128)S(1)} %stack.35.where, bf16[4,8,2,2,64,128]{5,4,3,2,1,0:T(8,128)(2,1)S(1)} %all-to-all-done.1.refs_0_, bf16[4,136,512]{2,1,0:T(8,128)(2,1)} %copy-done.4, bf16[4,136,512]{2,1,0:T(8,128)(2,1)} %collective-permute-done.7.refs_2_.refs_5_, bf16[4,136,512]{2,1,0:T(8,128)(2,1)} %copy-done.6, ...), custom_call_target="tpu_custom_call" | custom-call | flops 1140850688 | bytes 6558228 | tf_op jit(solution)/shard_map/pallas_call | solution.py:216
  114.5 9.3 %all-to-all-start.2 = ((bf16[16,4,8,128]{3,2,1,0:T(8,128)(2,1)}), bf16[16,4,8,128]{3,2,1,0:T(8,128)(2,1)S(1)}, u32[]{:S(2)}, u32[]{:S(2)}) async-start(bf16[16,4,8,128]{3,2,1,0:T(8,128)(2,1)} %shard_map.92), calls=%async_computation.2 | async-start | bytes 262144 | tf_op jit(solution)/shard_map/all_to_all | solution.py:25
  123.9 4.3 %shard_map.93.query = bf16[2,2,128,128]{3,2,1,0:T(8,128)(2,1)S(1)} custom-call(s32[5]{0:T(128)S(1)} %stack.35.where, bf16[8,2,64,128]{3,2,1,0:T(8,128)(2,1)S(1)} %slice_bitcast_fusion.refs_0_, bf16[8,2,64,128]{3,2,1,0:T(8,128)(2,1)S(1)} %collective-permute-done.4.refs_1_, bf16[8,2,64,128]{3,2,1,0:T(8,128)(2,1)S(1)} %collective-permute-done.5.refs_2_, ...), custom_call_target="tpu_custom_call" | custom-call | flops 570425344 | bytes 5509652 | tf_op jit(solution)/shard_map/pallas_call | solution.py:216
  131.5 2.9 %collective-permute-done.14.near = bf16[2,128,128]{2,1,0:T(8,128)(2,1)S(1)} collective-permute-done((bf16[2,128,128]{2,1,0:T(8,128)(2,1)S(1)}, bf16[2,128,128]{2,1,0:T(8,128)(2,1)S(1)}, u32[]{:S(2)}, u32[]{:S(2)}) %collective-permute-start.14) | collective-permute-done | bytes 65568 | tf_op jit(solution)/shard_map/ppermute | solution.py:234
  136.5 17.6 %all-to-all-start.3 = ((bf16[64,8,128]{2,1,0:T(8,128)(2,1)}), bf16[64,8,128]{2,1,0:T(8,128)(2,1)S(1)}, u32[]{:S(2)}, u32[]{:S(2)}) async-start(bf16[64,8,128]{2,1,0:T(8,128)(2,1)} %shard_map.95), calls=%async_computation.3 | async-start | bytes 262144 | tf_op jit(solution)/shard_map/all_to_all | solution.py:25
  154.2 7.5 %collective-permute-start.15 = (bf16[2,128,128]{2,1,0:T(8,128)(2,1)S(1)}, bf16[2,128,128]{2,1,0:T(8,128)(2,1)S(1)}, u32[]{:S(2)}, u32[]{:S(2)}) collective-permute-start(bf16[2,128,128]{2,1,0:T(8,128)(2,1)S(1)} %pad_maximum_fusion.3), channel_id=1, source_target_pairs={{0,256},{256,0},{1,257},{257,1},{2,258},{258,2},{3,259},{259,3},{4... | collective-permute-start | bytes 196616 | tf_op jit(solution)/shard_map/ppermute | solution.py:234
  161.7 3.2 %collective-permute-done.15.far = bf16[2,128,128]{2,1,0:T(8,128)(2,1)S(1)} collective-permute-done((bf16[2,128,128]{2,1,0:T(8,128)(2,1)S(1)}, bf16[2,128,128]{2,1,0:T(8,128)(2,1)S(1)}, u32[]{:S(2)}, u32[]{:S(2)}) %collective-permute-start.15) | collective-permute-done | bytes 65568 | tf_op jit(solution)/shard_map/ppermute | solution.py:234
  164.9 3.2 %all-to-all-done.3.returned = bf16[64,8,128]{2,1,0:T(8,128)(2,1)S(1)} async-done(((bf16[64,8,128]{2,1,0:T(8,128)(2,1)}), bf16[64,8,128]{2,1,0:T(8,128)(2,1)S(1)}, u32[]{:S(2)}, u32[]{:S(2)}) %all-to-all-start.3) | async-done | bytes 131104 | tf_op jit(solution)/shard_map/all_to_all | solution.py:25
  (66 shorter events, 28.4 us)
Async XLA Ops:
  0.0 30.4 %copy-start.11 = (bf16[128,512]{1,0:T(8,128)(2,1)S(1)}, bf16[128,512]{1,0:T(8,128)(2,1)}, u32[]{:S(2)}) copy-start(bf16[128,512]{1,0:T(8,128)(2,1)} %param.9) | copy-start | bytes 393220
  0.8 7.6 %collective-permute-start = (bf16[8,512]{1,0:T(8,128)(2,1)S(1)}, bf16[8,512]{1,0:T(8,128)(2,1)S(1)}, u32[]{:S(2)}, u32[]{:S(2)}) collective-permute-start(bf16[8,512]{1,0:T(8,128)(2,1)S(1)} %slice.18), channel_id=1, source_target_pairs={{0,8},{8,16},{16,24},{24,32},{32,40},{40,48},{48,56},{56,64},{64,7... | collective-permute-start | bytes 24584 | tf_op jit(solution)/shard_map/ppermute | solution.py:229
  8.4 14.1 %collective-permute-start.1 = (bf16[2,3,64,128]{3,2,1,0:T(8,128)(2,1)S(1)}, bf16[2,3,64,128]{3,2,1,0:T(8,128)(2,1)S(1)}, u32[]{:S(2)}, u32[]{:S(2)}) collective-permute-start(bf16[2,3,64,128]{3,2,1,0:T(8,128)(2,1)S(1)} %get-tuple-element.21), channel_id=1, source_target_pairs={{0,256},{256,0},{1,257},{257,1},{2,258},{258,2},{3,259},{259,3},{4... | collective-permute-start | bytes 294920 | tf_op jit(solution)/shard_map/ppermute | solution.py:234
  22.6 36.8 %copy-start.12 = (f32[3,3,512]{2,1,0:T(4,128)S(1)}, f32[3,3,512]{2,1,0:T(4,128)}, u32[]{:S(2)}) copy-start(f32[3,3,512]{2,1,0:T(4,128)} %param.13) | copy-start | bytes 55300
  23.7 36.5 %all-to-all-start = ((bf16[8,3,2,64,128]{4,3,2,1,0:T(8,128)(2,1)}), bf16[8,3,2,64,128]{4,3,2,1,0:T(8,128)(2,1)S(1)}, u32[]{:S(2)}, u32[]{:S(2)}) async-start(bf16[8,3,2,64,128]{4,3,2,1,0:T(8,128)(2,1)} %bitcast.7), calls=%async_computation | async-start | bytes 1572864 | tf_op jit(solution)/shard_map/all_to_all | solution.py:25
  30.4 12.3 %collective-permute-start.2 = (bf16[1,136,512]{2,1,0:T(8,128)(2,1)S(1)}, bf16[1,136,512]{2,1,0:T(8,128)(2,1)S(1)}, u32[]{:S(2)}, u32[]{:S(2)}) collective-permute-start(bf16[1,136,512]{2,1,0:T(8,128)(2,1)S(1)} %maximum_bitcast_fusion), channel_id=1, source_target_pairs={{0,256},{2,258},{4,260},{6,262},{256,0},{258,2},{260,4},{262,6},{1... | collective-permute-start | bytes 417800 | tf_op jit(solution)/shard_map/ppermute | solution.py:234
  42.8 13.9 %collective-permute-start.3 = (bf16[2,136,512]{2,1,0:T(8,128)(2,1)S(1)}, bf16[2,136,512]{2,1,0:T(8,128)(2,1)S(1)}, u32[]{:S(2)}, u32[]{:S(2)}) collective-permute-start(bf16[2,136,512]{2,1,0:T(8,128)(2,1)S(1)} %pad_maximum_fusion.1), channel_id=1, source_target_pairs={{0,4},{2,6},{4,0},{6,2},{256,260},{258,262},{260,256},{262,258},{1... | collective-permute-start | bytes 835592 | tf_op jit(solution)/shard_map/ppermute | solution.py:234
  56.7 18.2 %copy-start.4 = (bf16[4,136,512]{2,1,0:T(8,128)(2,1)}, bf16[4,136,512]{2,1,0:T(8,128)(2,1)S(1)}, u32[]{:S(2)}) copy-start(bf16[4,136,512]{2,1,0:T(8,128)(2,1)S(1)} %pad_maximum_fusion.refs_1_.refs_4_) | copy-start | bytes 1671172
  56.7 15.1 %collective-permute-start.7 = (bf16[4,136,512]{2,1,0:T(8,128)(2,1)S(1)}, bf16[4,136,512]{2,1,0:T(8,128)(2,1)}, u32[]{:S(2)}, u32[]{:S(2)}) collective-permute-start(bf16[4,136,512]{2,1,0:T(8,128)(2,1)S(1)} %pad_maximum_fusion.refs_1_.refs_4_), channel_id=1, source_target_pairs={{0,2},{2,0},{4,6},{6,4},{256,258},{258,256},{260,262},{262,260},{1... | collective-permute-start | bytes 1671176 | tf_op jit(solution)/shard_map/ppermute | solution.py:234
  62.2 46.9 %all-to-all-start.1 = ((bf16[4,8,2,2,64,128]{5,4,3,2,1,0:T(8,128)(2,1)}), bf16[4,8,2,2,64,128]{5,4,3,2,1,0:T(8,128)(2,1)S(1)}, u32[]{:S(2)}, u32[]{:S(2)}) async-start(bf16[4,8,2,2,64,128]{5,4,3,2,1,0:T(8,128)(2,1)} %broadcast_in_dim.11), calls=%async_computation.1 | async-start | bytes 4194304 | tf_op jit(solution)/shard_map/all_to_all | solution.py:25
  68.3 17.4 %collective-permute-start.8 = (bf16[4,136,512]{2,1,0:T(8,128)(2,1)S(1)}, bf16[4,136,512]{2,1,0:T(8,128)(2,1)S(1)}, u32[]{:S(2)}, u32[]{:S(2)}) collective-permute-start(bf16[4,136,512]{2,1,0:T(8,128)(2,1)S(1)} %pad_maximum_fusion.refs_1_.refs_4_), channel_id=1, source_target_pairs={{0,8},{8,0},{1,9},{9,1},{2,10},{10,2},{3,11},{11,3},{4,12},{12,4},... | collective-permute-start | bytes 1671176 | tf_op jit(solution)/shard_map/ppermute | solution.py:234
  71.8 23.0 %collective-permute-start.9 = (bf16[4,136,512]{2,1,0:T(8,128)(2,1)}, bf16[4,136,512]{2,1,0:T(8,128)(2,1)S(1)}, u32[]{:S(2)}, u32[]{:S(2)}) collective-permute-start(bf16[4,136,512]{2,1,0:T(8,128)(2,1)} %collective-permute-done.7.refs_2_.refs_5_), channel_id=1, source_target_pairs={{0,8},{8,0},{1,9},{9,1},{2,10},{10,2},{3,11},{11,3},{4,12},{12,4},... | collective-permute-start | bytes 1671176 | tf_op jit(solution)/shard_map/ppermute | solution.py:234
  74.9 25.6 %collective-permute-start.10 = (bf16[4,136,512]{2,1,0:T(8,128)(2,1)S(1)}, bf16[4,136,512]{2,1,0:T(8,128)(2,1)S(1)}, u32[]{:S(2)}, u32[]{:S(2)}) collective-permute-start(bf16[4,136,512]{2,1,0:T(8,128)(2,1)S(1)} %pad_maximum_fusion.refs_1_.refs_4_), channel_id=1, source_target_pairs={{0,1},{1,0},{2,3},{3,2},{4,5},{5,4},{6,7},{7,6},{8,9},{9,8},{10,11... | collective-permute-start | bytes 1671176 | tf_op jit(solution)/shard_map/ppermute | solution.py:234
  76.8 26.6 %collective-permute-start.11 = (bf16[4,136,512]{2,1,0:T(8,128)(2,1)}, bf16[4,136,512]{2,1,0:T(8,128)(2,1)S(1)}, u32[]{:S(2)}, u32[]{:S(2)}) collective-permute-start(bf16[4,136,512]{2,1,0:T(8,128)(2,1)} %collective-permute-done.7.refs_2_.refs_5_), channel_id=1, source_target_pairs={{0,1},{1,0},{2,3},{3,2},{4,5},{5,4},{6,7},{7,6},{8,9},{9,8},{10,11... | collective-permute-start | bytes 1671176 | tf_op jit(solution)/shard_map/ppermute | solution.py:234
  85.7 22.6 %copy-start.6 = (bf16[4,136,512]{2,1,0:T(8,128)(2,1)}, bf16[4,136,512]{2,1,0:T(8,128)(2,1)S(1)}, u32[]{:S(2)}) copy-start(bf16[4,136,512]{2,1,0:T(8,128)(2,1)S(1)} %collective-permute-done.8.refs_3_.refs_6_) | copy-start | bytes 1671172
  85.7 22.6 %collective-permute-start.12 = (bf16[4,136,512]{2,1,0:T(8,128)(2,1)S(1)}, bf16[4,136,512]{2,1,0:T(8,128)(2,1)S(1)}, u32[]{:S(2)}, u32[]{:S(2)}) collective-permute-start(bf16[4,136,512]{2,1,0:T(8,128)(2,1)S(1)} %collective-permute-done.8.refs_3_.refs_6_), channel_id=1, source_target_pairs={{0,1},{1,0},{2,3},{3,2},{4,5},{5,4},{6,7},{7,6},{8,9},{9,8},{10,11... | collective-permute-start | bytes 1671176 | tf_op jit(solution)/shard_map/ppermute | solution.py:234
  94.8 14.2 %collective-permute-start.13 = (bf16[4,136,512]{2,1,0:T(8,128)(2,1)S(1)}, bf16[4,136,512]{2,1,0:T(8,128)(2,1)}, u32[]{:S(2)}, u32[]{:S(2)}) collective-permute-start(bf16[4,136,512]{2,1,0:T(8,128)(2,1)S(1)} %collective-permute-done.9.refs_4_.refs_7_), channel_id=1, source_target_pairs={{0,1},{1,0},{2,3},{3,2},{4,5},{5,4},{6,7},{7,6},{8,9},{9,8},{10,11... | collective-permute-start | bytes 1671176 | tf_op jit(solution)/shard_map/ppermute | solution.py:234
  97.7 26.1 %collective-permute-start.4 = (bf16[8,2,64,128]{3,2,1,0:T(8,128)(2,1)S(1)}, bf16[8,2,64,128]{3,2,1,0:T(8,128)(2,1)S(1)}, u32[]{:S(2)}, u32[]{:S(2)}) collective-permute-start(bf16[8,2,64,128]{3,2,1,0:T(8,128)(2,1)S(1)} %slice_bitcast_fusion.refs_0_), channel_id=1, source_target_pairs={{0,64},{64,0},{128,192},{192,128},{1,65},{65,1},{129,193},{193,129... | collective-permute-start | bytes 786440 | tf_op jit(solution)/shard_map/ppermute | solution.py:234
  100.5 23.3 %collective-permute-start.5 = (bf16[8,2,64,128]{3,2,1,0:T(8,128)(2,1)S(1)}, bf16[8,2,64,128]{3,2,1,0:T(8,128)(2,1)S(1)}, u32[]{:S(2)}, u32[]{:S(2)}) collective-permute-start(bf16[8,2,64,128]{3,2,1,0:T(8,128)(2,1)S(1)} %slice_bitcast_fusion.refs_0_), channel_id=1, source_target_pairs={{0,128},{64,192},{128,0},{192,64},{1,129},{65,193},{129,1},{193,65... | collective-permute-start | bytes 786440 | tf_op jit(solution)/shard_map/ppermute | solution.py:234
  103.4 20.5 %collective-permute-start.6 = (bf16[8,2,64,128]{3,2,1,0:T(8,128)(2,1)S(1)}, bf16[8,2,64,128]{3,2,1,0:T(8,128)(2,1)S(1)}, u32[]{:S(2)}, u32[]{:S(2)}) collective-permute-start(bf16[8,2,64,128]{3,2,1,0:T(8,128)(2,1)S(1)} %slice_bitcast_fusion.refs_0_), channel_id=1, source_target_pairs={{0,192},{64,128},{128,64},{192,0},{1,193},{65,129},{129,65},{193,1... | collective-permute-start | bytes 786440 | tf_op jit(solution)/shard_map/ppermute | solution.py:234
  114.5 19.9 %all-to-all-start.2 = ((bf16[16,4,8,128]{3,2,1,0:T(8,128)(2,1)}), bf16[16,4,8,128]{3,2,1,0:T(8,128)(2,1)S(1)}, u32[]{:S(2)}, u32[]{:S(2)}) async-start(bf16[16,4,8,128]{3,2,1,0:T(8,128)(2,1)} %shard_map.92), calls=%async_computation.2 | async-start | bytes 262144 | tf_op jit(solution)/shard_map/all_to_all | solution.py:25
  128.2 6.2 %collective-permute-start.14 = (bf16[2,128,128]{2,1,0:T(8,128)(2,1)S(1)}, bf16[2,128,128]{2,1,0:T(8,128)(2,1)S(1)}, u32[]{:S(2)}, u32[]{:S(2)}) collective-permute-start(bf16[2,128,128]{2,1,0:T(8,128)(2,1)S(1)} %slice_bitcast_fusion.1), channel_id=1, source_target_pairs={{0,8},{8,0},{1,9},{9,1},{2,10},{10,2},{3,11},{11,3},{4,12},{12,4},... | collective-permute-start | bytes 196616 | tf_op jit(solution)/shard_map/ppermute | solution.py:234
  136.5 31.6 %all-to-all-start.3 = ((bf16[64,8,128]{2,1,0:T(8,128)(2,1)}), bf16[64,8,128]{2,1,0:T(8,128)(2,1)S(1)}, u32[]{:S(2)}, u32[]{:S(2)}) async-start(bf16[64,8,128]{2,1,0:T(8,128)(2,1)} %shard_map.95), calls=%async_computation.3 | async-start | bytes 262144 | tf_op jit(solution)/shard_map/all_to_all | solution.py:25
  154.2 10.7 %collective-permute-start.15 = (bf16[2,128,128]{2,1,0:T(8,128)(2,1)S(1)}, bf16[2,128,128]{2,1,0:T(8,128)(2,1)S(1)}, u32[]{:S(2)}, u32[]{:S(2)}) collective-permute-start(bf16[2,128,128]{2,1,0:T(8,128)(2,1)S(1)} %pad_maximum_fusion.3), channel_id=1, source_target_pairs={{0,256},{256,0},{1,257},{257,1},{2,258},{258,2},{3,259},{259,3},{4... | collective-permute-start | bytes 196616 | tf_op jit(solution)/shard_map/ppermute | solution.py:234
  (9 other events, 60.2 us)
